TPU v7x, 256 devices: a whole 4x4x8 slice. The times are simulated.
256 devices in a mesh: pert: 8 (over z), gene: 32 (over x, y, core).
Axes of the slice: x: 4, y: 4, z: 8, core: 2. Of those that a mesh axis runs over, the one named last changes fastest.
Arguments:
- tensor: bfloat16 [8192, 8, 16384], P('pert', None, 'gene'), may hold values from -2400 to 2400
- pert_factor: bfloat16 [8192, 128], P('pert'), may hold values from -10 to 10
- context_factor: bfloat16 [8, 128], replicated, may hold values from -3 to 3
Outputs:
- gene_factor: bfloat16 [16384, 128], P('gene')
- pert_updated: bfloat16 [8192, 128], P('pert')
All inputs are finite; a program needn't handle non-finite values.
Results may differ from a plain program's by a relative error of at most 0.0042.
Values may be sent and summed in bfloat16 or wider, within the bound.
No kernel may reach another device: no remote copies, remote signals or barrier semaphores. Data moves between devices by JAX's collectives and lax.ppermute only.
A program may use at most 64 MiB of HBM per device.

v0:
```python
import jax
import jax.numpy as jnp
from jax import lax
from jax.sharding import PartitionSpec as P

epsilon = 1e-06


def solve_gram(rhs, gram):
    lower = jnp.linalg.cholesky(gram)
    half = lax.linalg.triangular_solve(lower, rhs, left_side=False, lower=True, transpose_a=True)
    return lax.linalg.triangular_solve(lower, half, left_side=False, lower=True, transpose_a=False)


def raw_gram(solved):
    return jnp.dot(
        solved.T, solved, precision=lax.Precision.HIGHEST, preferred_element_type=jnp.float32
    )


def shards(tensor, pert_factor, context_factor):
    rows_i = tensor.shape[0]
    rows_j = tensor.shape[2]
    n_pert = lax.axis_size("pert")
    n_gene = lax.axis_size("gene")
    context32 = context_factor.astype(jnp.float32)
    gram_b = jnp.dot(context_factor.T, context_factor, preferred_element_type=jnp.float32)
    local_gram = jnp.dot(pert_factor.T, pert_factor, preferred_element_type=jnp.float32)
    gene_count = rows_j * n_gene
    tensor_block = tensor
    partial_sum = jnp.einsum(
        "ikj,ir->kjr", tensor_block, pert_factor, preferred_element_type=jnp.float32
    )
    gram_a, mttkrp_c = lax.psum(
        (local_gram, jnp.sum(partial_sum * context32[:, None, :], axis=0)), "pert"
    )
    solved_c = solve_gram(mttkrp_c, gram_a * gram_b)
    gram_s = lax.psum(raw_gram(solved_c), "gene")
    scale_c = jnp.sqrt(jnp.diagonal(gram_s) / gene_count + epsilon)
    gene_factor = (solved_c / scale_c[None, :]).astype(jnp.bfloat16)
    gram_c = gram_s / (scale_c[:, None] * scale_c[None, :])
    gram_pert_mode = gram_c * gram_b
    pert_count = rows_i * n_pert
    tensor_block = tensor
    partial_sum = jnp.einsum(
        "ikj,jr->ikr", tensor_block, gene_factor, preferred_element_type=jnp.float32
    )
    mttkrp_a = lax.psum(jnp.sum(partial_sum * context32[None, :, :], axis=1), "gene")
    solved_a = solve_gram(mttkrp_a, gram_pert_mode)
    squares_a = lax.psum(jnp.sum(solved_a * solved_a, axis=0), "pert")
    scale_a = jnp.sqrt(squares_a / pert_count + epsilon)
    pert_updated = (solved_a / scale_a[None, :]).astype(jnp.bfloat16)
    return (gene_factor, pert_updated)


def solution(mesh):
    return jax.shard_map(
        shards,
        mesh=mesh,
        in_specs=(P("pert", None, "gene"), P("pert", None), P()),
        out_specs=(P("gene", None), P("pert", None)),
        check_vma=False,
    )
```

profile of v0, /device:TPU:1, one launch (start us, length us, event | category | flops | bytes accessed | tf_op | source)
XLA Modules:
  0.0 394.1 jit_solution(13535459443830926320)
XLA Ops:
  7.2 0.7 convert_element_type.9
  8.1 0.9 fusion.24
  9.0 13.0 %multiply_reduce_fusion = f32[512,128]{1,0:T(8,128)} fusion(bf16[1024,8,512]{2,1,0:T(8,128)(2,1)} %param.4, f32[8,128]{1,0:T(8,128)S(1)} %convert_element_type.9, bf16[1024,128]{1,0:T(8,128)(2,1)S(1)} %copy-done), kind=kOutput, calls=%fused_computation.7 | convolution fusion | flops 1074724864 | bytes 8916992 | tf_op jit(solution)/shard_map/ikj,ir->kjr/dot_general | solution.py:31
  22.3 71.8 %all-reduce.9.cloned.1.call-done = (f32[512,128]{1,0:T(8,128)}, f32[128,128]{0,1:T(8,128)}) async-done(((f32[512,128]{1,0:T(8,128)}, f32[128,128]{0,1:T(8,128)}), (f32[512,128]{1,0:T(8,128)}, f32[128,128]{0,1:T(8,128)})) %all-reduce.9.cloned.1.call-update) | async-done | bytes 327696 | tf_op jit(solution)/shard_map/psum | solution.py:34
  94.0 1.1 fusion.23
  95.2 11.7 %cholesky.44 = f32[128,128]{1,0:T(8,128)S(1)} custom-call(f32[128,128]{1,0:T(8,128)S(1)} %fusion.22), custom_call_target="Cholesky" | custom-call | tf_op jit(solution)/shard_map/jit(cholesky)/cholesky | solution.py:10
  106.9 0.6 compare_reduce_fusion.1
  107.6 0.7 fusion.11
  108.2 9.8 %custom-call.12 = f32[1,128,128]{1,2,0:T(8,128)S(1)} custom-call(f32[1,128,128]{2,1,0:T(8,128)S(1)} %fusion.11), custom_call_target="InvertDiagBlocksLowerTriangular" | custom-call | tf_op jit(solution)/shard_map/triangular_solve | solution.py:11
  118.1 1.3 fusion.20
  119.8 1.2 fusion.25
  121.3 111.1 %all-reduce.5.cloned.1.call-done = f32[128,128]{0,1:T(8,128)} async-done(((f32[128,128]{0,1:T(8,128)}), f32[128,128]{0,1:T(8,128)}) %all-reduce.5.cloned.1.call-update) | async-done | bytes 65552 | tf_op jit(solution)/shard_map/psum | solution.py:38
  232.4 1.9 gather_fusion
  234.4 1.0 divide_multiply_fusion
  235.5 11.7 %cholesky.55 = f32[128,128]{1,0:T(8,128)S(1)} custom-call(f32[128,128]{1,0:T(8,128)S(1)} %fusion.17), custom_call_target="Cholesky" | custom-call | tf_op jit(solution)/shard_map/jit(cholesky)/cholesky | solution.py:10
  247.2 9.4 %fusion.4 = f32[1024,128]{0,1:T(8,128)S(1)} fusion(bf16[1024,8,512]{2,1,0:T(8,128)(2,1)} %param.4, f32[8,128]{1,0:T(8,128)S(1)} %convert_element_type.9, bf16[512,128]{1,0:T(8,128)(2,1)S(1)} %divide_convert_fusion.1), kind=kOutput, calls=%fused_computation.6 | convolution fusion | flops 1075707904 | bytes 9048064 | tf_op jit(solution)/shard_map/ikj,jr->ikr/dot_general | solution.py:45
  256.7 1.0 copy.34
  257.7 0.6 compare_reduce_fusion
  258.3 0.7 fusion.12
  259.0 9.8 %custom-call.13 = f32[1,128,128]{1,2,0:T(8,128)S(1)} custom-call(f32[1,128,128]{2,1,0:T(8,128)S(1)} %fusion.12), custom_call_target="InvertDiagBlocksLowerTriangular" | custom-call | tf_op jit(solution)/shard_map/triangular_solve | solution.py:11
  268.8 102.0 %all-reduce.7.cloned.1.call-done = f32[1024,128]{1,0:T(8,128)} async-done(((f32[1024,128]{1,0:T(8,128)}), f32[1024,128]{1,0:T(8,128)}) %all-reduce.7.cloned.1.call-update) | async-done | bytes 524304 | tf_op jit(solution)/shard_map/psum | solution.py:48
  370.8 1.6 fusion.15
  373.1 13.7 %psum.39 = f32[128]{0:T(128)S(1)} all-reduce(f32[128]{0:T(128)S(1)} %get-tuple-element.7), channel_id=1, replica_groups=mesh['pert'=8,'gene'=32] {'pert'}, use_global_device_ids=true, to_apply=%region_9.11 | all-reduce | flops 128 | bytes 1024 | tf_op jit(solution)/shard_map/psum | solution.py:50
  386.8 0.8 divide_convert_fusion
  (24 shorter events, 2.1 us)
Async XLA Ops:
  7.2 1.0 copy-start
  7.2 86.8 %copy-start.2 = (bf16[8,128]{1,0:T(8,128)(2,1)S(1)}, bf16[8,128]{1,0:T(8,128)(2,1)}, u32[]{:S(2)}) copy-start(bf16[8,128]{1,0:T(8,128)(2,1)} %param.6) | copy-start | bytes 6148
  7.2 86.8 %all-reduce.9.cloned.1.call-start = ((), (), s32[]{:S(2)}) async-start(), calls=%async_computation.2 | async-start | bytes 655360 | tf_op jit(solution)/shard_map/psum | solution.py:34
  22.0 210.3 %all-reduce.5.cloned.1.call-start = ((), (), s32[]{:S(2)}) async-start(), calls=%async_computation | async-start | bytes 131072 | tf_op jit(solution)/shard_map/psum | solution.py:38
  121.0 249.8 %all-reduce.7.cloned.1.call-start = ((), (), s32[]{:S(2)}) async-start(), calls=%async_computation.1 | async-start | bytes 1048576 | tf_op jit(solution)/shard_map/psum | solution.py:48
  234.3 138.7 %copy-start.1 = (bf16[512,128]{1,0:T(8,128)(2,1)}, bf16[512,128]{1,0:T(8,128)(2,1)S(1)}, u32[]{:S(2)}) copy-start(bf16[512,128]{1,0:T(8,128)(2,1)S(1)} %divide_convert_fusion.1) | copy-start | bytes 393220
Sparse Core Ops, SparseCore 0:
  22.1 71.8 all-reduce.8
  121.1 111.1 all-reduce.4
  257.8 112.9 all-reduce.6
where the time goes:
time: 398 us; the launch traced here: 394 us
  waiting for transfers between devices  285 us (72%)
  other arithmetic  48.2 us (12%)
  matrix products  29.5 us (7%)
  between operations  13.9 us (3%)
  blocking collectives  13.7 us (3%)
    psum x1, waiting for transfers between devices, shards(): gram_s = lax.psum(raw_gram(solved_c), 'gene')  111 us
    psum x1, waiting for transfers between devices, shards(): lax.psum(jnp.sum(partial_sum * context32[None, :, :], axis=1), 'gene')  102 us
    psum x1, waiting for transfers between devices, shards(): lax.psum((local_gram, jnp.sum(partial_sum * context32[:, None, :], axis=0...  71.8 us
    another operation x6, other arithmetic, solve_gram(): lower = jnp.linalg.cholesky(gram)  24.8 us
    another operation x4, other arithmetic, solve_gram(): lax.linalg.triangular_solve(lower, rhs, left_side=False, lower=True, tran...  20.9 us
    psum x1, blocking collectives, shards(): squares_a = lax.psum(jnp.sum(solved_a * solved_a, axis=0), 'pert')  13.7 us
    dot_general x1, matrix products, shards(): jnp.einsum('ikj,ir->kjr', tensor_block, pert_factor, preferred_element_ty...  13 us
    dot_general x1, matrix products, shards(): jnp.einsum('ikj,jr->ikr', tensor_block, gene_factor, preferred_element_ty...  9.45 us
  transfers between devices with their start and end apart: 3, of which 3 were waited for; matrix products, arithmetic and copies ran while one was open for 3% of the time, Pallas kernels for 0%

commit v1 on v0

v1 whole, which is shorter than its diff:
```python
import functools

import jax
import jax.numpy as jnp
from jax import lax
from jax.experimental import pallas as pl
from jax.experimental.pallas import tpu as pltpu
from jax.sharding import PartitionSpec as P

epsilon = 1e-06
f32 = jnp.float32
bf16 = jnp.bfloat16
HIGHEST = lax.Precision.HIGHEST


def dot(a, b, dims=((1,), (0,)), precision=None):
    return lax.dot_general(a, b, (dims, ((), ())), precision=precision, preferred_element_type=f32)


def split(x):
    hi = x.astype(bf16)
    return hi, (x - hi.astype(f32)).astype(bf16)


def dot_split(a, b):
    n = b.shape[1]
    right = jnp.concatenate(split(b), axis=1)
    product = dot(jnp.concatenate(split(a), axis=1), jnp.concatenate([right, right], axis=0))
    return product[:, :n] + product[:, n:]


def eye(n):
    return (
        lax.broadcasted_iota(jnp.int32, (n, n), 0) == lax.broadcasted_iota(jnp.int32, (n, n), 1)
    ).astype(f32)


def diagonal(a, unit):
    picked = a * unit
    return jnp.sum(picked, axis=0, keepdims=True), jnp.sum(picked, axis=1, keepdims=True)


def row_norm(a):
    return jnp.max(jnp.sum(jnp.abs(a), axis=1, keepdims=True))


def inverse(a):
    unit = eye(a.shape[0])
    diag_row, diag_col = diagonal(a, unit)
    scale_row, scale_col = lax.rsqrt(diag_row), lax.rsqrt(diag_col)
    scaled = a * scale_col * scale_row
    off = row_norm(unit - scaled)
    far = off >= 0.95
    alpha = jnp.where(far, 1.0 / (1.0 + off), 1.0)
    r = unit - alpha * scaled
    x = alpha * (unit + r)
    r = dot_split(r, r)
    n = a.shape[0]

    def advance(x, r):
        product = dot_split(jnp.concatenate([x, r], axis=0), r)
        return x + product[:n, :], product[n:, :]

    def measured(state):
        x, r, _, count = state
        x, r = advance(x, r)
        return x, r, row_norm(r), count + 1

    def bounded(state):
        x, r, bound = state
        return *advance(x, r), bound * bound

    x, r, bound, _ = lax.while_loop(
        lambda s: jnp.logical_and(s[2] > 0.5, s[3] < 40), measured, (x, r, row_norm(r), 0)
    )
    x, r, bound = lax.while_loop(lambda s: s[2] > 1e-7, bounded, (x, r, jnp.minimum(bound, 0.5)))

    def newton(_, x):
        return x + dot_split(x, unit - dot(scaled, x, precision=HIGHEST))

    x = lax.fori_loop(0, jnp.where(far, 4, 1), newton, x)
    return x * scale_col * scale_row


def gram_of(context):
    return dot(context, context, ((0,), (0,)))


def gene_products(tensor_ref, factor_ref, context_ref, out_ref, spread, pattern, total, gram):
    step = pl.program_id(0)
    contexts, rank = context_ref.shape
    rows = factor_ref.shape[0]
    wide = rows * contexts

    @pl.when(step == 0)
    def _():
        lane = lax.broadcasted_iota(jnp.int32, (rows, wide), 1)
        row = lax.broadcasted_iota(jnp.int32, (rows, wide), 0)
        spread[...] = (lane // contexts == row).astype(f32).astype(bf16)
        lane = lax.broadcasted_iota(jnp.int32, (contexts, wide), 1)
        row = lax.broadcasted_iota(jnp.int32, (contexts, wide), 0)
        each = (lane % contexts == row).astype(f32).astype(bf16)
        pattern[...] = dot(context_ref[...], each, ((0,), (0,)))
        total[...] = jnp.zeros_like(total)
        gram[...] = jnp.zeros_like(gram)

    factor = factor_ref[...]
    hi, lo = split(dot(factor, spread[...], ((0,), (0,))) * pattern[...])
    total[...] += dot(jnp.concatenate([hi, lo], axis=0), tensor_ref[...])
    gram[...] += gram_of(factor)

    @pl.when(step == pl.num_programs(0) - 1)
    def _():
        chunks, height, _ = out_ref.shape
        part = rank // chunks
        genes = height - part
        summed = (total[:rank, :] + total[rank:, :]).T
        for q in range(chunks):
            out_ref[q, :genes, :] = summed[q * genes : (q + 1) * genes, :]
            out_ref[q, genes:, :] = gram[q * part : (q + 1) * part, :]


def sum_and_copy(in_ref, out_ref):
    total = jnp.sum(in_ref[...], axis=0)
    for q in range(out_ref.shape[0]):
        out_ref[q] = total


def pert_products(blocks, held_ref, context_ref, tensor_ref, out_ref, solved_ref, stage, wide, sems):
    copies = []
    height = stage.shape[0] // blocks
    for b in range(blocks):
        rows = pl.ds(b * height, height)
        copy = pltpu.make_async_copy(tensor_ref.at[rows, :], stage.at[rows, :], sems.at[b])
        copy.start()
        copies.append(copy)
    chunks, tall, rank = held_ref.shape
    contexts = context_ref.shape[0]
    part = rank // chunks
    genes = tall - part
    context = context_ref[...]
    gram_a = jnp.concatenate([held_ref[q, genes:, :] for q in range(chunks)], axis=0)
    mttkrp = jnp.concatenate([held_ref[q, :genes, :] for q in range(chunks)], axis=0)
    inv = inverse(gram_a * gram_of(context))
    solved = dot(mttkrp, inv, precision=HIGHEST)
    solved_ref[...] = solved
    gram_s = dot(solved, solved, ((0,), (0,)), precision=HIGHEST)
    targets, out_tall, _ = out_ref.shape
    gram_part = rank // targets
    perts = stage.shape[0] // contexts // targets
    for q in range(targets):
        rest = out_tall - perts - gram_part
        out_ref[q, perts:, :] = jnp.concatenate(
            [gram_s[q * gram_part : (q + 1) * gram_part, :], jnp.zeros((rest, rank), f32)], axis=0
        )
    weights = jnp.concatenate(split(solved), axis=1)
    context32 = context.astype(f32)
    per_block = height // contexts
    for b in range(blocks):
        copies[b].wait()
        product = dot(stage[pl.ds(b * height, height), :], weights)
        wide[...] = product[:, :rank] + product[:, rank:]
        total = wide[pl.ds(0, per_block, stride=contexts), :] * context32[0:1, :]
        for k in range(1, contexts):
            total += wide[pl.ds(k, per_block, stride=contexts), :] * context32[k : k + 1, :]
        here = per_block // perts
        out_ref[pl.ds(b * here, here), :perts, :] = total.reshape(here, perts, rank)


def pert_solve(gene_count, held_ref, context_ref, solved_ref, gene_ref, out_ref, squares_ref):
    chunks, tall, rank = held_ref.shape
    gram_part = rank // chunks
    perts = out_ref.shape[0] // chunks
    gram_s = jnp.concatenate(
        [held_ref[q, perts : perts + gram_part, :] for q in range(chunks)], axis=0
    )
    diag_row, _ = diagonal(gram_s, eye(rank))
    scale_c = jnp.sqrt(diag_row / gene_count + epsilon)
    gene_ref[...] = (solved_ref[...] / scale_c).astype(bf16)
    inv = inverse(gram_s * gram_of(context_ref[...])) * scale_c
    mttkrp = held_ref[:, :perts, :].reshape(out_ref.shape)
    solved = dot(mttkrp, inv, precision=HIGHEST)
    out_ref[...] = solved
    squares = jnp.sum(solved * solved, axis=0, keepdims=True)
    squares_ref[...] = jnp.broadcast_to(squares[None], squares_ref.shape)


def pert_scale(pert_count, held_ref, solved_ref, out_ref):
    squares = jnp.sum(held_ref[...], axis=0)[:1, :]
    scale_a = jnp.sqrt(squares / pert_count + epsilon)
    out_ref[...] = (solved_ref[...] / scale_a).astype(bf16)


def vmem(n):
    return [pl.BlockSpec(memory_space=pltpu.VMEM)] * n


def shards(tensor, pert_factor, context_factor):
    rows_i, contexts, rows_j = tensor.shape
    rank = pert_factor.shape[1]
    n_pert = lax.axis_size("pert")
    n_gene = lax.axis_size("gene")
    flat = tensor.reshape(rows_i * contexts, rows_j)
    blocks = 8
    part_i = rows_i // blocks
    genes = rows_j // n_pert
    tall = genes + rank // n_pert

    partial = pl.pallas_call(
        gene_products,
        grid=(blocks,),
        in_specs=[
            pl.BlockSpec((part_i * contexts, rows_j), lambda b: (b, 0)),
            pl.BlockSpec((part_i, rank), lambda b: (b, 0)),
            pl.BlockSpec((contexts, rank), lambda b: (0, 0)),
        ],
        out_specs=pl.BlockSpec((n_pert, tall, rank), lambda b: (0, 0, 0)),
        out_shape=jax.ShapeDtypeStruct((n_pert, tall, rank), f32),
        scratch_shapes=[
            pltpu.VMEM((part_i, part_i * contexts), bf16),
            pltpu.VMEM((rank, part_i * contexts), f32),
            pltpu.VMEM((2 * rank, rows_j), f32),
            pltpu.VMEM((rank, rank), f32),
        ],
        name="gene_products",
    )(flat, pert_factor, context_factor)
    partial = lax.all_to_all(partial, "pert", 0, 0)
    summed = pl.pallas_call(
        sum_and_copy,
        in_specs=vmem(1),
        out_specs=pl.BlockSpec(memory_space=pltpu.VMEM),
        out_shape=jax.ShapeDtypeStruct(partial.shape, f32),
        name="pert_sum",
    )(partial)
    gathered = lax.all_to_all(summed, "pert", 0, 0)

    perts = rows_i // n_gene
    out_tall = -(-(perts + rank // n_gene) // 8) * 8
    partial, solved_c = pl.pallas_call(
        functools.partial(pert_products, blocks),
        in_specs=vmem(2) + [pl.BlockSpec(memory_space=pl.ANY)],
        out_specs=tuple(vmem(2)),
        out_shape=(
            jax.ShapeDtypeStruct((n_gene, out_tall, rank), f32),
            jax.ShapeDtypeStruct((rows_j, rank), f32),
        ),
        scratch_shapes=[
            pltpu.VMEM((rows_i * contexts, rows_j), bf16),
            pltpu.VMEM((part_i * contexts, rank), f32),
            pltpu.SemaphoreType.DMA((blocks,)),
        ],
        name="pert_products",
    )(gathered, context_factor, flat)
    partial = lax.all_to_all(partial, "gene", 0, 0)
    summed = pl.pallas_call(
        sum_and_copy,
        in_specs=vmem(1),
        out_specs=pl.BlockSpec(memory_space=pltpu.VMEM),
        out_shape=jax.ShapeDtypeStruct(partial.shape, f32),
        name="gene_sum",
    )(partial)
    gathered = lax.all_to_all(summed, "gene", 0, 0)

    gene_factor, solved_a, squares = pl.pallas_call(
        functools.partial(pert_solve, rows_j * n_gene),
        in_specs=vmem(3),
        out_specs=tuple(vmem(3)),
        out_shape=(
            jax.ShapeDtypeStruct((rows_j, rank), bf16),
            jax.ShapeDtypeStruct((rows_i, rank), f32),
            jax.ShapeDtypeStruct((n_pert, 8, rank), f32),
        ),
        name="pert_solve",
    )(gathered, context_factor, solved_c)
    squares = lax.all_to_all(squares, "pert", 0, 0)
    pert_updated = pl.pallas_call(
        functools.partial(pert_scale, rows_i * n_pert),
        in_specs=vmem(2),
        out_specs=pl.BlockSpec(memory_space=pltpu.VMEM),
        out_shape=jax.ShapeDtypeStruct((rows_i, rank), bf16),
        name="pert_scale",
    )(squares, solved_a)
    return (gene_factor, pert_updated)


def solution(mesh):
    return jax.shard_map(
        shards,
        mesh=mesh,
        in_specs=(P("pert", None, "gene"), P("pert", None), P()),
        out_specs=(P("gene", None), P("pert", None)),
        check_vma=False,
    )
```

time: 398 us -> 124 us (0.31)
  waiting for transfers between devices: 285 us -> 0 us
  blocking collectives: 13.7 us -> 87.1 us
  other arithmetic: 48.2 us -> 0 us
  Pallas kernels: 0 us -> 35.5 us
  matrix products: 29.5 us -> 0 us
  between operations: 13.9 us -> 0.64 us
    psum x3 -> x0, waiting for transfers between devices: 285 us -> none  [the longest x1 111 us: shards(): gram_s = lax.psum(raw_gram(solved_c), 'gene')]
    all_to_all x0 -> x5, blocking collectives: none -> 87.1 us  [the longest x1 24.3 us: shards(): partial = lax.all_to_all(partial, 'gene', 0, 0)]
    another operation x10 -> x0, other arithmetic: 45.7 us -> none  [the longest x6 24.8 us: solve_gram(): lower = jnp.linalg.cholesky(gram)]
    pallas_call x0 -> x6, Pallas kernels: none -> 35.5 us  [the longest x1 13.7 us: shards(): pl.pallas_call(functools.partial(pert_products, blocks), in_specs=vmem(2)...]
    dot_general x5 -> x0, matrix products: 25.6 us -> none  [the longest x1 13 us: shards(): jnp.einsum('ikj,ir->kjr', tensor_block, pert_factor, preferred_element_ty...]
    psum x1 -> x0, blocking collectives: 13.7 us -> none  [shards(): squares_a = lax.psum(jnp.sum(solved_a * solved_a, axis=0), 'pert')]
  transfers between devices with their start and end apart: 3 -> 0, of which waited for: 3 -> 0; matrix products, arithmetic and copies ran while one was open for 3% -> 0% of each run, Pallas kernels for 0% -> 0%
where the time goes in v1:
time: 124 us; the launch traced here: 123 us
  blocking collectives  87.1 us (70%)
  Pallas kernels  35.5 us (29%)
    all_to_all x1, blocking collectives, shards(): partial = lax.all_to_all(partial, 'gene', 0, 0)  24.3 us
    all_to_all x1, blocking collectives, shards(): partial = lax.all_to_all(partial, 'pert', 0, 0)  20.8 us
    all_to_all x1, blocking collectives, shards(): gathered = lax.all_to_all(summed, 'gene', 0, 0)  17.1 us
    all_to_all x1, blocking collectives, shards(): gathered = lax.all_to_all(summed, 'pert', 0, 0)  14.1 us
    pallas_call x1, Pallas kernels, shards(): pl.pallas_call(functools.partial(pert_products, blocks), in_specs=vmem(2)...  13.7 us
    all_to_all x1, blocking collectives, shards(): squares = lax.all_to_all(squares, 'pert', 0, 0)  10.7 us
    pallas_call x1, Pallas kernels, shards(): pl.pallas_call(gene_products, grid=(blocks,), in_specs=[pl.BlockSpec((par...  9.34 us
    pallas_call x1, Pallas kernels, shards(): pl.pallas_call(functools.partial(pert_solve, rows_j * n_gene), in_specs=v...  6.82 us

profile of v1, /device:TPU:1, one launch (start us, length us, event | category | flops | bytes accessed | tf_op | source)
XLA Modules:
  0.0 123.2 jit_solution(4353466126962556544)
XLA Ops:
  0.6 9.3 %gene_products.1 = f32[8,80,128]{2,1,0:T(8,128)} custom-call(bf16[8192,512]{1,0:T(8,128)(2,1)} %bitcast.1, bf16[1024,128]{1,0:T(8,128)(2,1)} %factor_ref.1, bf16[8,128]{1,0:T(8,128)(2,1)} %context_ref.5), custom_call_target="tpu_custom_call" | custom-call | tf_op jit(solution)/shard_map/gene_products/pallas_call | solution.py:209
  10.0 20.8 %all_to_all.25.in_ref = f32[8,80,128]{2,1,0:T(8,128)} all-to-all(f32[8,80,128]{2,1,0:T(8,128)} %gene_products.1), channel_id=1, replica_groups=mesh['pert'=8,'gene'=32] {'pert'}, dimensions={0} | all-to-all | bytes 655360 | tf_op jit(solution)/shard_map/all_to_all | solution.py:227
  30.8 1.7 %pert_sum.1 = f32[8,80,128]{2,1,0:T(8,128)} custom-call(f32[8,80,128]{2,1,0:T(8,128)} %all_to_all.25.in_ref), custom_call_target="tpu_custom_call" | custom-call | tf_op jit(solution)/shard_map/pert_sum/pallas_call | solution.py:228
  32.5 14.1 %all_to_all.26.held_ref = f32[8,80,128]{2,1,0:T(8,128)} all-to-all(f32[8,80,128]{2,1,0:T(8,128)} %pert_sum.1), channel_id=1, replica_groups=mesh['pert'=8,'gene'=32] {'pert'}, dimensions={0} | all-to-all | bytes 655360 | tf_op jit(solution)/shard_map/all_to_all | solution.py:235
  46.6 13.7 %pert_products.1 = (f32[32,40,128]{2,1,0:T(8,128)}, f32[512,128]{1,0:T(8,128)}) custom-call(f32[8,80,128]{2,1,0:T(8,128)} %all_to_all.26.held_ref, bf16[8,128]{1,0:T(8,128)(2,1)} %context_ref.5, bf16[8192,512]{1,0:T(8,128)(2,1)} %bitcast.2), custom_call_target="tpu_custom_call" | custom-call | tf_op jit(solution)/shard_map/pert_products/pallas_call | solution.py:239
  60.4 24.3 %all_to_all.27.in_ref = f32[32,40,128]{2,1,0:T(8,128)} all-to-all(f32[32,40,128]{2,1,0:T(8,128)} %get-tuple-element.7), channel_id=1, replica_groups=mesh['pert'=8,'gene'=32] {'gene'}, dimensions={0} | all-to-all | bytes 1310720 | tf_op jit(solution)/shard_map/all_to_all | solution.py:254
  84.7 2.0 %gene_sum.1 = f32[32,40,128]{2,1,0:T(8,128)} custom-call(f32[32,40,128]{2,1,0:T(8,128)} %all_to_all.27.in_ref), custom_call_target="tpu_custom_call" | custom-call | tf_op jit(solution)/shard_map/gene_sum/pallas_call | solution.py:255
  86.7 17.1 %all_to_all.28.held_ref = f32[32,40,128]{2,1,0:T(8,128)} all-to-all(f32[32,40,128]{2,1,0:T(8,128)} %gene_sum.1), channel_id=1, replica_groups=mesh['pert'=8,'gene'=32] {'gene'}, dimensions={0} | all-to-all | bytes 1310720 | tf_op jit(solution)/shard_map/all_to_all | solution.py:262
  103.9 6.8 %pert_solve.1 = (bf16[512,128]{1,0:T(8,128)(2,1)}, f32[1024,128]{1,0:T(8,128)}, f32[8,8,128]{2,1,0:T(8,128)}) custom-call(f32[32,40,128]{2,1,0:T(8,128)} %all_to_all.28.held_ref, bf16[8,128]{1,0:T(8,128)(2,1)} %context_ref.5, f32[512,128]{1,0:T(8,128)} %get-tuple-element.8.solved_ref), custom_call_target="tpu_custom_call" | custom-call | tf_op jit(solution)/shard_map/pert_solve/pallas_call | solution.py:264
  110.7 10.7 %all_to_all.29.held_ref = f32[8,8,128]{2,1,0:T(8,128)} all-to-all(f32[8,8,128]{2,1,0:T(8,128)} %get-tuple-element.10), channel_id=1, replica_groups=mesh['pert'=8,'gene'=32] {'pert'}, dimensions={0} | all-to-all | bytes 65536 | tf_op jit(solution)/shard_map/all_to_all | solution.py:275
  121.4 1.8 %pert_scale.1 = bf16[1024,128]{1,0:T(8,128)(2,1)} custom-call(f32[8,8,128]{2,1,0:T(8,128)} %all_to_all.29.held_ref, f32[1024,128]{1,0:T(8,128)} %get-tuple-element.11.solved_ref), custom_call_target="tpu_custom_call" | custom-call | tf_op jit(solution)/shard_map/pert_scale/pallas_call | solution.py:276

commit v2 on v0

v2 whole, which is shorter than its diff:
```python
import functools

import jax
import jax.numpy as jnp
from jax import lax
from jax.experimental import pallas as pl
from jax.experimental.pallas import tpu as pltpu
from jax.sharding import PartitionSpec as P

epsilon = 1e-06
f32 = jnp.float32
bf16 = jnp.bfloat16
HIGHEST = lax.Precision.HIGHEST


def dot(a, b, dims=((1,), (0,)), precision=None):
    return lax.dot_general(a, b, (dims, ((), ())), precision=precision, preferred_element_type=f32)


def split(x):
    hi = x.astype(bf16)
    return hi, (x - hi.astype(f32)).astype(bf16)


def dot_split(a, b):
    n = b.shape[1]
    right = jnp.concatenate(split(b), axis=1)
    product = dot(jnp.concatenate(split(a), axis=1), jnp.concatenate([right, right], axis=0))
    return product[:, :n] + product[:, n:]


def eye(n):
    return (
        lax.broadcasted_iota(jnp.int32, (n, n), 0) == lax.broadcasted_iota(jnp.int32, (n, n), 1)
    ).astype(f32)


def diagonal(a, unit):
    picked = a * unit
    return jnp.sum(picked, axis=0, keepdims=True), jnp.sum(picked, axis=1, keepdims=True)


def row_norm(a):
    return jnp.max(jnp.sum(jnp.abs(a), axis=1, keepdims=True))


def inverse(a):
    unit = eye(a.shape[0])
    diag_row, diag_col = diagonal(a, unit)
    scale_row, scale_col = lax.rsqrt(diag_row), lax.rsqrt(diag_col)
    scaled = a * scale_col * scale_row
    off = row_norm(unit - scaled)
    far = off >= 0.95
    alpha = jnp.where(far, 1.0 / (1.0 + off), 1.0)
    r = unit - alpha * scaled
    x = alpha * (unit + r)
    r = dot_split(r, r)
    n = a.shape[0]

    def advance(x, r):
        product = dot_split(jnp.concatenate([x, r], axis=0), r)
        return x + product[:n, :], product[n:, :]

    def measured(state):
        x, r, _, count = state
        x, r = advance(x, r)
        return x, r, row_norm(r), count + 1

    def bounded(state):
        x, r, bound = state
        return *advance(x, r), bound * bound

    x, r, bound, _ = lax.while_loop(
        lambda s: jnp.logical_and(s[2] > 0.5, s[3] < 40), measured, (x, r, row_norm(r), 0)
    )
    x, r, bound = lax.while_loop(lambda s: s[2] > 1e-7, bounded, (x, r, jnp.minimum(bound, 0.5)))

    def newton(_, x):
        return x + dot_split(x, unit - dot(scaled, x, precision=HIGHEST))

    x = lax.fori_loop(0, jnp.where(far, 4, 1), newton, x)
    return x * scale_col * scale_row


def gram_of(context):
    return dot(context, context, ((0,), (0,)))


def gene_products(blocks, depth, tensor_ref, factor_hbm, context_hbm, out_ref, keep, factor_ref, context_ref, sems, small):
    height = keep.shape[0] // blocks
    copies = []
    for b in range(blocks):
        rows = pl.ds(b * height, height)
        copies.append(pltpu.make_async_copy(tensor_ref.at[rows, :], keep.at[rows, :], sems.at[b]))
    first = pltpu.make_async_copy(factor_hbm, factor_ref, small.at[0])
    second = pltpu.make_async_copy(context_hbm, context_ref, small.at[1])
    first.start()
    second.start()
    for copy in copies[:depth]:
        copy.start()
    contexts, rank = context_ref.shape
    chunks, tall, _ = out_ref.shape
    part = rank // chunks
    genes = tall - part
    first.wait()
    second.wait()
    gram = gram_of(factor_ref[...])
    for q in range(chunks):
        out_ref[q, genes:, :] = gram[q * part : (q + 1) * part, :]
    context32 = context_ref[...].astype(f32)
    perts = height // contexts
    total = jnp.zeros((2 * rank, keep.shape[1]), f32)
    for b in range(blocks):
        factor = factor_ref[pl.ds(b * perts, perts), :].astype(f32)
        rows = (factor[:, None, :] * context32[None]).reshape(height, rank)
        rows = jnp.concatenate(split(rows), axis=1)
        copies[b].wait()
        if b + depth < blocks:
            copies[b + depth].start()
        total += dot(rows, keep[pl.ds(b * height, height), :], ((0,), (0,)))
    summed = (total[:rank, :] + total[rank:, :]).T
    for q in range(chunks):
        out_ref[q, :genes, :] = summed[q * genes : (q + 1) * genes, :]


def sum_and_copy(in_ref, out_ref):
    total = jnp.sum(in_ref[...], axis=0)
    for q in range(out_ref.shape[0]):
        out_ref[q] = total


def add(a_ref, b_ref, out_ref):
    out_ref[...] = a_ref[...] + b_ref[...]


def half_index():
    return lax.rem(lax.axis_index("gene"), 2)


def pert_products(blocks, held_ref, context_ref, tensor_ref, mine_ref, other_ref, solved_ref, gram):
    chunks, tall, rank = held_ref.shape
    contexts = context_ref.shape[0]
    part = rank // chunks
    genes = tall - part
    context = context_ref[...]
    gram_a = jnp.concatenate([held_ref[q, genes:, :] for q in range(chunks)], axis=0)
    mttkrp = jnp.concatenate([held_ref[q, :genes, :] for q in range(chunks)], axis=0)
    inv = inverse(gram_a * gram_of(context))
    solved = dot(mttkrp, inv, precision=HIGHEST)
    solved_ref[...] = solved
    gram[...] = dot(solved, solved, ((0,), (0,)), precision=HIGHEST)
    weights = jnp.concatenate(split(solved), axis=1)
    context32 = context.astype(f32)
    half = tensor_ref.shape[0] // 2
    height = half // blocks
    per_block = height // contexts
    for core, out_ref in ((1 - half_index(), other_ref), (half_index(), mine_ref)):
        targets, out_tall, _ = out_ref.shape
        gram_part = rank // 2 // targets
        perts = half // contexts // targets
        rest = out_tall - perts - gram_part
        here = gram[pl.ds(pl.multiple_of(core * (rank // 2), rank // 2), rank // 2), :]
        for q in range(targets):
            out_ref[q, perts:, :] = jnp.concatenate(
                [here[q * gram_part : (q + 1) * gram_part, :], jnp.zeros((rest, rank), f32)], axis=0
            )
        for b in range(blocks):
            start = pl.multiple_of(core * half + b * height, height)
            product = dot(tensor_ref[pl.ds(start, height), :], weights)
            wide = (product[:, :rank] + product[:, rank:]).reshape(per_block, contexts, rank)
            total = jnp.sum(wide * context32[None], axis=1)
            n = per_block // perts
            out_ref[pl.ds(b * n, n), :perts, :] = total.reshape(n, perts, rank)


def pert_solve(
    gene_count, mine_ref, other_ref, context_ref, solved_ref, gene_ref, out_ref, squares_ref, gram
):
    chunks, tall, rank = mine_ref.shape
    gram_part = rank // 2 // chunks
    perts = out_ref.shape[0] // 2 // chunks
    mine = half_index()
    for core, held_ref in ((mine, mine_ref), (1 - mine, other_ref)):
        rows = jnp.concatenate(
            [held_ref[q, perts : perts + gram_part, :] for q in range(chunks)], axis=0
        )
        gram[pl.ds(pl.multiple_of(core * (rank // 2), rank // 2), rank // 2), :] = rows
    gram_s = gram[...]
    diag_row, _ = diagonal(gram_s, eye(rank))
    scale_c = jnp.sqrt(diag_row / gene_count + epsilon)
    gene_ref[...] = (solved_ref[...] / scale_c).astype(bf16)
    inv = inverse(gram_s * gram_of(context_ref[...])) * scale_c
    half = out_ref.shape[0] // 2
    squares = jnp.zeros((1, rank), f32)
    for core, held_ref in ((mine, mine_ref), (1 - mine, other_ref)):
        mttkrp = held_ref[:, :perts, :].reshape(half, rank)
        solved = dot(mttkrp, inv, precision=HIGHEST)
        out_ref[pl.ds(pl.multiple_of(core * half, half), half), :] = solved
        squares += jnp.sum(solved * solved, axis=0, keepdims=True)
    squares_ref[...] = jnp.broadcast_to(squares[None], squares_ref.shape)


def pert_scale(pert_count, held_ref, solved_ref, out_ref):
    squares = jnp.sum(held_ref[...], axis=0)[:1, :]
    scale_a = jnp.sqrt(squares / pert_count + epsilon)
    out_ref[...] = (solved_ref[...] / scale_a).astype(bf16)


VMEM = pl.BlockSpec(memory_space=pltpu.VMEM)
FAR = pl.BlockSpec(memory_space=pltpu.HBM)


def near(x):
    return pltpu.with_memory_space_constraint(x, pltpu.VMEM)


def far(x):
    return pltpu.with_memory_space_constraint(x, pltpu.HBM)


def call(body, name, inputs, outputs, in_specs=None, scratch=(), limit=16):
    single = not isinstance(outputs, tuple)
    return pl.pallas_call(
        body,
        in_specs=in_specs or [VMEM] * len(inputs),
        out_specs=VMEM if single else (VMEM,) * len(outputs),
        out_shape=outputs,
        scratch_shapes=list(scratch),
        compiler_params=pltpu.CompilerParams(vmem_limit_bytes=limit << 20),
        name=name,
    )(*inputs)


def summed_copies(x, name):
    return call(sum_and_copy, name, (near(x),), pltpu.VMEM(x.shape, f32))


def shards(tensor, pert_factor, context_factor):
    rows_i, contexts, rows_j = tensor.shape
    rank = pert_factor.shape[1]
    n_pert = lax.axis_size("pert")
    n_gene = lax.axis_size("gene")
    flat = tensor.reshape(rows_i * contexts, rows_j)
    blocks = 8
    tall = rows_j // n_pert + rank // n_pert

    partial, kept = call(
        functools.partial(gene_products, blocks, 3),
        "gene_products",
        (far(flat), far(pert_factor), far(context_factor)),
        (pltpu.VMEM((n_pert, tall, rank), f32), pltpu.VMEM(flat.shape, bf16)),
        in_specs=[FAR] * 3,
        scratch=(
            pltpu.VMEM(pert_factor.shape, bf16),
            pltpu.VMEM(context_factor.shape, bf16),
            pltpu.SemaphoreType.DMA((blocks,)),
            pltpu.SemaphoreType.DMA((2,)),
        ),
    )
    partial = lax.all_to_all(partial, "pert", 0, 0)
    gathered = lax.all_to_all(summed_copies(partial, "pert_sum"), "pert", 0, 0)

    chips = n_gene // 2
    perts = rows_i // n_gene
    out_tall = -(-(perts + rank // n_gene) // 8) * 8
    message = pltpu.VMEM((chips, out_tall, rank), f32)
    mine, other, solved_c = call(
        functools.partial(pert_products, 4),
        "pert_products",
        (near(gathered), context_factor, near(kept)),
        (message, message, pltpu.VMEM((rows_j, rank), f32)),
        scratch=(pltpu.VMEM((rank, rank), f32),),
    )
    swap = [(i, i ^ 1) for i in range(n_gene)]
    groups = [[2 * i + core for i in range(chips)] for core in range(2)]
    other = lax.ppermute(other, "gene", swap)
    partial = call(add, "core_sum", (near(mine), near(other)), message)
    partial = lax.all_to_all(partial, "gene", 0, 0, axis_index_groups=groups)
    mine = lax.all_to_all(
        summed_copies(partial, "gene_sum"), "gene", 0, 0, axis_index_groups=groups
    )
    other = lax.ppermute(mine, "gene", swap)

    gene_factor, solved_a, squares = call(
        functools.partial(pert_solve, rows_j * n_gene),
        "pert_solve",
        (near(mine), near(other), context_factor, near(solved_c)),
        (
            jax.ShapeDtypeStruct((rows_j, rank), bf16),
            pltpu.VMEM((rows_i, rank), f32),
            pltpu.VMEM((n_pert, 8, rank), f32),
        ),
        scratch=(pltpu.VMEM((rank, rank), f32),),
    )
    squares = lax.all_to_all(squares, "pert", 0, 0)
    pert_updated = call(
        functools.partial(pert_scale, rows_i * n_pert),
        "pert_scale",
        (near(squares), near(solved_a)),
        jax.ShapeDtypeStruct((rows_i, rank), bf16),
    )
    return (gene_factor, pert_updated)


def solution(mesh):
    return jax.shard_map(
        shards,
        mesh=mesh,
        in_specs=(P("pert", None, "gene"), P("pert", None), P()),
        out_specs=(P("gene", None), P("pert", None)),
        check_vma=False,
    )
```

time: 398 us -> 99 us (0.25)
  waiting for transfers between devices: 285 us -> 2.51 us
  blocking collectives: 13.7 us -> 69.4 us
  other arithmetic: 48.2 us -> 0 us
  matrix products: 29.5 us -> 0 us
  Pallas kernels: 0 us -> 19.8 us
  between operations: 13.9 us -> 0.67 us
  starting transfers between devices: 0.52 us -> 6.46 us
    psum x3 -> x0, waiting for transfers between devices: 285 us -> none  [the longest x1 111 us: shards(): gram_s = lax.psum(raw_gram(solved_c), 'gene')]
    all_to_all x0 -> x5, blocking collectives: none -> 69.4 us  [the longest x1 20.6 us: shards(): partial = lax.all_to_all(partial, 'pert', 0, 0)]
    another operation x10 -> x0, other arithmetic: 45.7 us -> none  [the longest x6 24.8 us: solve_gram(): lower = jnp.linalg.cholesky(gram)]
    dot_general x5 -> x0, matrix products: 25.6 us -> none  [the longest x1 13 us: shards(): jnp.einsum('ikj,ir->kjr', tensor_block, pert_factor, preferred_element_ty...]
    pallas_call x0 -> x7, Pallas kernels: none -> 19.8 us  [call(): pl.pallas_call(body, in_specs=in_specs or [VMEM] * len(inputs), out_specs...]
    psum x1 -> x0, blocking collectives: 13.7 us -> none  [shards(): squares_a = lax.psum(jnp.sum(solved_a * solved_a, axis=0), 'pert')]
    ppermute x0 -> x2, starting transfers between devices: none -> 6.46 us  [the longest x1 3.51 us: shards(): other = lax.ppermute(other, 'gene', swap)]
  transfers between devices with their start and end apart: 3 -> 2, of which waited for: 3 -> 2; matrix products, arithmetic and copies ran while one was open for 3% -> 0% of each run, Pallas kernels for 0% -> 0%
where the time goes in v2:
time: 99 us; the launch traced here: 98.8 us
  blocking collectives  69.4 us (70%)
  Pallas kernels  19.8 us (20%)
  starting transfers between devices  6.46 us (7%)
  waiting for transfers between devices  2.51 us (3%)
    all_to_all x1, blocking collectives, shards(): partial = lax.all_to_all(partial, 'pert', 0, 0)  20.6 us
    pallas_call x7, Pallas kernels, call(): pl.pallas_call(body, in_specs=in_specs or [VMEM] * len(inputs), out_specs...  19.8 us
    all_to_all x1, blocking collectives, shards(): partial = lax.all_to_all(partial, 'gene', 0, 0, axis_index_groups=groups)  14.5 us
    all_to_all x1, blocking collectives, shards(): gathered = lax.all_to_all(summed_copies(partial, 'pert_sum'), 'pert', 0, 0)  13.6 us
    all_to_all x1, blocking collectives, shards(): lax.all_to_all(summed_copies(partial, 'gene_sum'), 'gene', 0, 0, axis_ind...  11.5 us
    all_to_all x1, blocking collectives, shards(): squares = lax.all_to_all(squares, 'pert', 0, 0)  9.23 us
    ppermute x1, starting transfers between devices, shards(): other = lax.ppermute(other, 'gene', swap)  3.51 us
    ppermute x1, starting transfers between devices, shards(): other = lax.ppermute(mine, 'gene', swap)  2.94 us
  transfers between devices with their start and end apart: 2, of which 2 were waited for; matrix products, arithmetic and copies ran while one was open for 0% of the time, Pallas kernels for 0%

profile of v2, /device:TPU:1, one launch (start us, length us, event | category | flops | bytes accessed | tf_op | source)
XLA Modules:
  0.0 98.8 jit_solution(13434265808479378126)
XLA Ops:
  0.6 0.0 copy-start
  0.6 5.8 %gene_products.1 = (f32[8,80,128]{2,1,0:T(8,128)S(1)}, bf16[8192,512]{1,0:T(8,128)(2,1)S(1)}) custom-call(bf16[8192,512]{1,0:T(8,128)(2,1)} %bitcast.1, bf16[1024,128]{1,0:T(8,128)(2,1)} %factor_hbm.1, bf16[8,128]{1,0:T(8,128)(2,1)} %context_ref.3), custom_call_target="tpu_custom_call" | custom-call | tf_op jit(solution)/shard_map/gene_products/pallas_call | solution.py:223
  6.4 20.6 %all_to_all.25.in_ref = f32[8,80,128]{2,1,0:T(8,128)S(1)} all-to-all(f32[8,80,128]{2,1,0:T(8,128)S(1)} %get-tuple-element.10), channel_id=1, replica_groups=mesh['pert'=8,'gene'=32] {'pert'}, dimensions={0} | all-to-all | bytes 655360 | tf_op jit(solution)/shard_map/all_to_all | solution.py:260
  27.0 13.6 %all_to_all.26.held_ref = f32[8,80,128]{2,1,0:T(8,128)S(1)} all-to-all(f32[8,80,128]{2,1,0:T(8,128)S(1)} %pert_sum.1), channel_id=1, replica_groups=mesh['pert'=8,'gene'=32] {'pert'}, dimensions={0} | all-to-all | bytes 655360 | tf_op jit(solution)/shard_map/all_to_all | solution.py:261
  40.6 0.0 copy-done
  40.6 8.1 %pert_products.1 = (f32[16,40,128]{2,1,0:T(8,128)S(1)}, f32[16,40,128]{2,1,0:T(8,128)S(1)}, f32[512,128]{1,0:T(8,128)S(1)}) custom-call(f32[8,80,128]{2,1,0:T(8,128)S(1)} %all_to_all.26.held_ref, bf16[8,128]{1,0:T(8,128)(2,1)S(1)} %copy-done, bf16[8192,512]{1,0:T(8,128)(2,1)S(1)} %get-tuple-element.11.tensor_ref), custom_call_target="tpu_custom_call" | custom-call | tf_op jit(solution)/shard_map/pert_products/pallas_call | solution.py:223
  48.7 3.5 %collective-permute-start = (f32[16,40,128]{2,1,0:T(8,128)S(1)}, f32[16,40,128]{2,1,0:T(8,128)S(1)}, u32[]{:S(2)}, u32[]{:S(2)}) collective-permute-start(f32[16,40,128]{2,1,0:T(8,128)S(1)} %get-tuple-element.13), channel_id=1, source_target_pairs={{0,1},{1,0},{2,3},{3,2},{4,5},{5,4},{6,7},{7,6},{8,9},{9,8},{10,11... | collective-permute-start | bytes 983048 | tf_op jit(solution)/shard_map/ppermute | solution.py:276
  52.2 1.3 %collective-permute-done.b_ref = f32[16,40,128]{2,1,0:T(8,128)S(1)} collective-permute-done((f32[16,40,128]{2,1,0:T(8,128)S(1)}, f32[16,40,128]{2,1,0:T(8,128)S(1)}, u32[]{:S(2)}, u32[]{:S(2)}) %collective-permute-start) | collective-permute-done | bytes 327712 | tf_op jit(solution)/shard_map/ppermute | solution.py:276
  53.5 14.5 %all_to_all.27.in_ref = f32[16,40,128]{2,1,0:T(8,128)S(1)} all-to-all(f32[16,40,128]{2,1,0:T(8,128)S(1)} %core_sum.1), channel_id=1, replica_groups={{0,2,4,6,8,10,12,14,16,18,20,22,24,26,28,30},{1,3,5,7,9,11,13,15,17,19,..., dimensions={0} | all-to-all | bytes 655360 | tf_op jit(solution)/shard_map/all_to_all | solution.py:278
  68.1 11.5 %all_to_all.28.mine_ref = f32[16,40,128]{2,1,0:T(8,128)S(1)} all-to-all(f32[16,40,128]{2,1,0:T(8,128)S(1)} %gene_sum.1), channel_id=1, replica_groups={{0,2,4,6,8,10,12,14,16,18,20,22,24,26,28,30},{1,3,5,7,9,11,13,15,17,19,..., dimensions={0} | all-to-all | bytes 655360 | tf_op jit(solution)/shard_map/all_to_all | solution.py:279
  79.6 2.9 %collective-permute-start.1 = (f32[16,40,128]{2,1,0:T(8,128)S(1)}, f32[16,40,128]{2,1,0:T(8,128)S(1)}, u32[]{:S(2)}, u32[]{:S(2)}) collective-permute-start(f32[16,40,128]{2,1,0:T(8,128)S(1)} %all_to_all.28.mine_ref), channel_id=1, source_target_pairs={{0,1},{1,0},{2,3},{3,2},{4,5},{5,4},{6,7},{7,6},{8,9},{9,8},{10,11... | collective-permute-start | bytes 983048 | tf_op jit(solution)/shard_map/ppermute | solution.py:282
  82.5 1.3 %collective-permute-done.1.other_ref = f32[16,40,128]{2,1,0:T(8,128)S(1)} collective-permute-done((f32[16,40,128]{2,1,0:T(8,128)S(1)}, f32[16,40,128]{2,1,0:T(8,128)S(1)}, u32[]{:S(2)}, u32[]{:S(2)}) %collective-permute-start.1) | collective-permute-done | bytes 327712 | tf_op jit(solution)/shard_map/ppermute | solution.py:282
  83.8 5.1 %pert_solve.1 = (bf16[512,128]{1,0:T(8,128)(2,1)}, f32[1024,128]{1,0:T(8,128)S(1)}, f32[8,8,128]{2,1,0:T(8,128)S(1)}) custom-call(f32[16,40,128]{2,1,0:T(8,128)S(1)} %all_to_all.28.mine_ref, f32[16,40,128]{2,1,0:T(8,128)S(1)} %collective-permute-done.1.other_ref, bf16[8,128]{1,0:T(8,128)(2,1)S(1)} %copy-done, f32[512,128]{1,0:T(8,128)S(1)} %get-tuple-element.14.solved_ref), custom_call_target="tpu_custom_call" | custom-call | tf_op jit(solution)/shard_map/pert_solve/pallas_call | solution.py:223
  88.8 9.2 %all_to_all.29.held_ref = f32[8,8,128]{2,1,0:T(8,128)S(1)} all-to-all(f32[8,8,128]{2,1,0:T(8,128)S(1)} %get-tuple-element.16), channel_id=1, replica_groups=mesh['pert'=8,'gene'=32] {'pert'}, dimensions={0} | all-to-all | bytes 65536 | tf_op jit(solution)/shard_map/all_to_all | solution.py:295
  98.1 0.8 pert_scale.1
  (3 shorter events, 0.1 us)
Async XLA Ops:
  0.6 40.0 %copy-start = (bf16[8,128]{1,0:T(8,128)(2,1)S(1)}, bf16[8,128]{1,0:T(8,128)(2,1)}, u32[]{:S(2)}) copy-start(bf16[8,128]{1,0:T(8,128)(2,1)} %context_ref.3) | copy-start | bytes 6148
  48.7 4.8 %collective-permute-start = (f32[16,40,128]{2,1,0:T(8,128)S(1)}, f32[16,40,128]{2,1,0:T(8,128)S(1)}, u32[]{:S(2)}, u32[]{:S(2)}) collective-permute-start(f32[16,40,128]{2,1,0:T(8,128)S(1)} %get-tuple-element.13), channel_id=1, source_target_pairs={{0,1},{1,0},{2,3},{3,2},{4,5},{5,4},{6,7},{7,6},{8,9},{9,8},{10,11... | collective-permute-start | bytes 983048 | tf_op jit(solution)/shard_map/ppermute | solution.py:276
  79.6 4.2 %collective-permute-start.1 = (f32[16,40,128]{2,1,0:T(8,128)S(1)}, f32[16,40,128]{2,1,0:T(8,128)S(1)}, u32[]{:S(2)}, u32[]{:S(2)}) collective-permute-start(f32[16,40,128]{2,1,0:T(8,128)S(1)} %all_to_all.28.mine_ref), channel_id=1, source_target_pairs={{0,1},{1,0},{2,3},{3,2},{4,5},{5,4},{6,7},{7,6},{8,9},{9,8},{10,11... | collective-permute-start | bytes 983048 | tf_op jit(solution)/shard_map/ppermute | solution.py:282

commit v3 on v2

v3 whole, which is shorter than its diff:
```python
import functools

import jax
import jax.numpy as jnp
from jax import lax
from jax.experimental import pallas as pl
from jax.experimental.pallas import tpu as pltpu
from jax.sharding import PartitionSpec as P

epsilon = 1e-06
f32 = jnp.float32
bf16 = jnp.bfloat16
HIGHEST = lax.Precision.HIGHEST


def dot(a, b, dims=((1,), (0,)), precision=None):
    return lax.dot_general(a, b, (dims, ((), ())), precision=precision, preferred_element_type=f32)


def split(x):
    hi = x.astype(bf16)
    return hi, (x - hi.astype(f32)).astype(bf16)


def dot_split(a, b):
    n = b.shape[1]
    right = jnp.concatenate(split(b), axis=1)
    product = dot(jnp.concatenate(split(a), axis=1), jnp.concatenate([right, right], axis=0))
    return product[:, :n] + product[:, n:]


def eye(n):
    return (
        lax.broadcasted_iota(jnp.int32, (n, n), 0) == lax.broadcasted_iota(jnp.int32, (n, n), 1)
    ).astype(f32)


def diagonal(a, unit):
    picked = a * unit
    return jnp.sum(picked, axis=0, keepdims=True), jnp.sum(picked, axis=1, keepdims=True)


def row_norm(a):
    return jnp.max(jnp.sum(jnp.abs(a), axis=1, keepdims=True))


def inverse(a):
    unit = eye(a.shape[0])
    diag_row, diag_col = diagonal(a, unit)
    scale_row, scale_col = lax.rsqrt(diag_row), lax.rsqrt(diag_col)
    scaled = a * scale_col * scale_row
    off = row_norm(unit - scaled)
    far_off = off >= 0.95
    alpha = jnp.where(far_off, 1.0 / (1.0 + off), 1.0)
    r = unit - alpha * scaled
    x = alpha * (unit + r)
    r = dot_split(r, r)
    n = a.shape[0]

    def advance(x, r):
        product = dot_split(jnp.concatenate([x, r], axis=0), r)
        return x + product[:n, :], product[n:, :]

    def measured(state):
        x, r, _, count = state
        x, r = advance(x, r)
        return x, r, row_norm(r), count + 1

    def bounded(state):
        x, r, bound = state
        return *advance(x, r), bound * bound

    def newton(_, x):
        return x + dot_split(x, unit - dot(scaled, x, precision=HIGHEST))

    x, r, bound, _ = lax.while_loop(
        lambda s: jnp.logical_and(s[2] > 0.95, s[3] < 40),
        measured,
        (x, r, jnp.where(far_off, 1.0, off * off), 0),
    )
    x, r, bound = lax.while_loop(lambda s: s[2] > 1e-7, bounded, (x, r, jnp.minimum(bound, 0.95)))
    x = lax.fori_loop(0, jnp.where(far_off, 4, jnp.where(off > 0.8, 1, 0)), newton, x)
    return x * scale_col * scale_row


def gram_of(context):
    return dot(context, context, ((0,), (0,)))


def gene_products(
    blocks, tensor_ref, factor_hbm, context_hbm, out_ref, keep, factor_ref, context_ref, left, sems, small
):
    height = keep.shape[0] // blocks
    copies = []
    for b in range(blocks):
        rows = pl.ds(b * height, height)
        copies.append(pltpu.make_async_copy(tensor_ref.at[rows, :], keep.at[rows, :], sems.at[b]))
    first = pltpu.make_async_copy(factor_hbm, factor_ref, small.at[0])
    second = pltpu.make_async_copy(context_hbm, context_ref, small.at[1])
    first.start()
    second.start()
    copies[0].start()
    copies[1].start()
    contexts, rank = context_ref.shape
    chunks, tall, _ = out_ref.shape
    part = rank // chunks
    genes = tall - part
    first.wait()
    second.wait()
    gram = gram_of(factor_ref[...])
    for q in range(chunks):
        out_ref[q, genes:, :] = gram[q * part : (q + 1) * part, :]
    context32 = context_ref[...].astype(f32)
    perts = height // contexts

    def build(b):
        factor = factor_ref[pl.ds(b * perts, perts), :].astype(f32)
        rows = (factor[:, None, :] * context32[None]).reshape(height, rank)
        left[b % 2, :rank, :], left[b % 2, rank:, :] = split(rows.T)

    build(0)
    total = None
    for b in range(blocks):
        copies[b].wait()
        if b + 2 < blocks:
            copies[b + 2].start()
        if b + 1 < blocks:
            build(b + 1)
        product = dot(left[b % 2], keep[pl.ds(b * height, height), :])
        total = product if total is None else total + product
    summed = (total[:rank, :] + total[rank:, :]).T
    for q in range(chunks):
        out_ref[q, :genes, :] = summed[q * genes : (q + 1) * genes, :]


def sum_and_copy(in_ref, out_ref):
    total = jnp.sum(in_ref[...], axis=0)
    for q in range(out_ref.shape[0]):
        out_ref[q] = total


def add(a_ref, b_ref, out_ref):
    out_ref[...] = a_ref[...] + b_ref[...]


def half_index():
    return lax.rem(lax.axis_index("gene"), 2)


def contract(blocks, core, tensor_ref, weights, context, gram_ref, out_ref):
    rank = gram_ref.shape[0]
    contexts = context.shape[0]
    context32 = context.astype(f32)
    half = tensor_ref.shape[0] // 2
    height = half // blocks
    per_block = height // contexts
    targets = out_ref.shape[0]
    perts = half // contexts // targets
    out_ref[:, perts:, :] = gram_ref[...].reshape(targets, rank // targets, rank)
    for b in range(blocks):
        start = pl.multiple_of(core * half + b * height, height)
        product = dot(tensor_ref[pl.ds(start, height), :], weights)
        wide = (product[:, :rank] + product[:, rank:]).reshape(per_block, contexts, rank)
        total = jnp.sum(wide * context32[None], axis=1)
        n = per_block // perts
        out_ref[pl.ds(b * n, n), :perts, :] = total.reshape(n, perts, rank)


def gene_solve(blocks, held_ref, context_ref, tensor_ref, other_ref, solved_ref, weights_ref, gram_ref):
    chunks, tall, rank = held_ref.shape
    genes = tall - rank // chunks
    context = context_ref[...]
    gram_a = jnp.concatenate([held_ref[q, genes:, :] for q in range(chunks)], axis=0)
    mttkrp = jnp.concatenate([held_ref[q, :genes, :] for q in range(chunks)], axis=0)
    inv = inverse(gram_a * gram_of(context))
    solved = dot(mttkrp, inv, precision=HIGHEST)
    solved_ref[...] = solved
    weights = jnp.concatenate(split(solved), axis=1)
    weights_ref[...] = weights
    product = dot(weights, weights, ((0,), (0,)))
    product = product[:, :rank] + product[:, rank:]
    gram_ref[...] = product[:rank, :] + product[rank:, :]
    contract(blocks, 1 - half_index(), tensor_ref, weights, context, gram_ref, other_ref)


def pert_products(blocks, weights_ref, context_ref, tensor_ref, gram_ref, mine_ref):
    contract(
        blocks, half_index(), tensor_ref, weights_ref[...], context_ref[...], gram_ref, mine_ref
    )


def pert_inverse(gene_count, mine_ref, context_ref, solved_ref, gene_ref, inv_ref):
    chunks, tall, rank = mine_ref.shape
    perts = tall - rank // chunks
    gram_s = mine_ref[:, perts:, :].reshape(rank, rank)
    diag_row, _ = diagonal(gram_s, eye(rank))
    scale_c = jnp.sqrt(diag_row / gene_count + epsilon)
    gene_ref[...] = (solved_ref[...] / scale_c).astype(bf16)
    inv_ref[...] = inverse(gram_s * gram_of(context_ref[...])) * scale_c


def pert_solve(mine_ref, other_ref, inv_ref, out_ref, squares_ref):
    chunks, tall, rank = mine_ref.shape
    perts = tall - rank // chunks
    inv = inv_ref[...]
    mine = half_index()
    half = out_ref.shape[0] // 2
    squares = []
    for core, held_ref in ((mine, mine_ref), (1 - mine, other_ref)):
        mttkrp = held_ref[:, :perts, :].reshape(half, rank)
        solved = dot(mttkrp, inv, precision=HIGHEST)
        out_ref[pl.ds(pl.multiple_of(core * half, half), half), :] = solved
        squares.append(jnp.sum(solved * solved, axis=0, keepdims=True))
    squares_ref[...] = jnp.broadcast_to((squares[0] + squares[1])[None], squares_ref.shape)


def pert_scale(pert_count, held_ref, solved_ref, out_ref):
    squares = jnp.sum(held_ref[...], axis=0)
    scale_a = jnp.sqrt(squares / pert_count + epsilon)
    out_ref[...] = (solved_ref[...] / scale_a).astype(bf16)


VMEM = pl.BlockSpec(memory_space=pltpu.VMEM)
FAR = pl.BlockSpec(memory_space=pltpu.HBM)


def near(x):
    return pltpu.with_memory_space_constraint(x, pltpu.VMEM)


def far(x):
    return pltpu.with_memory_space_constraint(x, pltpu.HBM)


def call(body, name, inputs, outputs, in_specs=None, scratch=(), limit=16):
    single = not isinstance(outputs, tuple)
    return pl.pallas_call(
        body,
        in_specs=in_specs or [VMEM] * len(inputs),
        out_specs=VMEM if single else (VMEM,) * len(outputs),
        out_shape=outputs,
        scratch_shapes=list(scratch),
        compiler_params=pltpu.CompilerParams(vmem_limit_bytes=limit << 20),
        name=name,
    )(*inputs)


def summed_copies(x, name):
    return call(sum_and_copy, name, (near(x),), pltpu.VMEM(x.shape, f32))


def shards(tensor, pert_factor, context_factor):
    rows_i, contexts, rows_j = tensor.shape
    rank = pert_factor.shape[1]
    n_pert = lax.axis_size("pert")
    n_gene = lax.axis_size("gene")
    flat = tensor.reshape(rows_i * contexts, rows_j)
    blocks = 4
    tall = rows_j // n_pert + rank // n_pert

    partial, kept = call(
        functools.partial(gene_products, blocks),
        "gene_products",
        (far(flat), far(pert_factor), far(context_factor)),
        (pltpu.VMEM((n_pert, tall, rank), f32), pltpu.VMEM(flat.shape, bf16)),
        in_specs=[FAR] * 3,
        scratch=(
            pltpu.VMEM(pert_factor.shape, bf16),
            pltpu.VMEM(context_factor.shape, bf16),
            pltpu.VMEM((2, 2 * rank, flat.shape[0] // blocks), bf16),
            pltpu.SemaphoreType.DMA((blocks,)),
            pltpu.SemaphoreType.DMA((2,)),
        ),
    )
    partial = lax.all_to_all(partial, "pert", 0, 0)
    gathered = lax.all_to_all(summed_copies(partial, "pert_sum"), "pert", 0, 0)

    chips = n_gene // 2
    perts = rows_i // n_gene
    message = pltpu.VMEM((chips, perts + rank // chips, rank), f32)
    square = pltpu.VMEM((rank, rank), f32)
    kept = near(kept)
    other, solved_c, weights, gram_s = call(
        functools.partial(gene_solve, 4),
        "gene_solve",
        (near(gathered), context_factor, kept),
        (
            message,
            pltpu.VMEM((rows_j, rank), f32),
            pltpu.VMEM((rows_j, 2 * rank), bf16),
            square,
        ),
    )
    swap = [(i, i ^ 1) for i in range(n_gene)]
    groups = [[2 * i + core for i in range(chips)] for core in range(2)]
    other = lax.ppermute(other, "gene", swap)
    mine = call(
        functools.partial(pert_products, 4),
        "pert_products",
        (near(weights), context_factor, kept, near(gram_s)),
        message,
    )
    partial = call(add, "core_sum", (near(mine), near(other)), message)
    partial = lax.all_to_all(partial, "gene", 0, 0, axis_index_groups=groups)
    mine = lax.all_to_all(
        summed_copies(partial, "gene_sum"), "gene", 0, 0, axis_index_groups=groups
    )
    other = lax.ppermute(mine, "gene", swap)
    mine = near(mine)
    gene_factor, inv = call(
        functools.partial(pert_inverse, rows_j * n_gene),
        "pert_inverse",
        (mine, context_factor, near(solved_c)),
        (jax.ShapeDtypeStruct((rows_j, rank), bf16), square),
    )
    solved_a, squares = call(
        pert_solve,
        "pert_solve",
        (mine, near(other), near(inv)),
        (pltpu.VMEM((rows_i, rank), f32), pltpu.VMEM((n_pert, 1, rank), f32)),
    )
    squares = lax.all_to_all(squares, "pert", 0, 0)
    pert_updated = call(
        functools.partial(pert_scale, rows_i * n_pert),
        "pert_scale",
        (near(squares), near(solved_a)),
        jax.ShapeDtypeStruct((rows_i, rank), bf16),
    )
    return (gene_factor, pert_updated)


def solution(mesh):
    return jax.shard_map(
        shards,
        mesh=mesh,
        in_specs=(P("pert", None, "gene"), P("pert", None), P()),
        out_specs=(P("gene", None), P("pert", None)),
        check_vma=False,
    )
```

time: 99 us -> 96.2 us (0.972)
  waiting for transfers between devices: 2.51 us -> 0.01 us
    ppermute x1, waiting for transfers between devices: 1.26 us -> 0.01 us  [shards(): other = lax.ppermute(mine, 'gene', swap)]
    ppermute x1, waiting for transfers between devices: 1.26 us -> 0.01 us  [shards(): other = lax.ppermute(other, 'gene', swap)]
    pallas_call x7 -> x9, Pallas kernels: 19.8 us -> 19.7 us  [call(): pl.pallas_call(body, in_specs=in_specs or [VMEM] * len(inputs), out_specs...]
  transfers between devices with their start and end apart: 2 -> 2, of which waited for: 2 -> 0; matrix products, arithmetic and copies ran while one was open for 0% -> 0% of each run, Pallas kernels for 0% -> 6%
where the time goes in v3:
time: 96.2 us; the launch traced here: 96 us
  blocking collectives  69.2 us (72%)
  Pallas kernels  19.7 us (20%)
  starting transfers between devices  6.41 us (7%)
    all_to_all x1, blocking collectives, shards(): partial = lax.all_to_all(partial, 'pert', 0, 0)  20.5 us
    pallas_call x9, Pallas kernels, call(): pl.pallas_call(body, in_specs=in_specs or [VMEM] * len(inputs), out_specs...  19.7 us
    all_to_all x1, blocking collectives, shards(): partial = lax.all_to_all(partial, 'gene', 0, 0, axis_index_groups=groups)  14.6 us
    all_to_all x1, blocking collectives, shards(): gathered = lax.all_to_all(summed_copies(partial, 'pert_sum'), 'pert', 0, 0)  13.6 us
    all_to_all x1, blocking collectives, shards(): lax.all_to_all(summed_copies(partial, 'gene_sum'), 'gene', 0, 0, axis_ind...  11.5 us
    all_to_all x1, blocking collectives, shards(): squares = lax.all_to_all(squares, 'pert', 0, 0)  8.92 us
    ppermute x1, starting transfers between devices, shards(): other = lax.ppermute(other, 'gene', swap)  3.52 us
    ppermute x1, starting transfers between devices, shards(): other = lax.ppermute(mine, 'gene', swap)  2.89 us
  transfers between devices with their start and end apart: 2, of which 0 were waited for; matrix products, arithmetic and copies ran while one was open for 0% of the time, Pallas kernels for 6%

profile of v3, /device:TPU:1, one launch (start us, length us, event | category | flops | bytes accessed | tf_op | source)
XLA Modules:
  0.0 96.0 jit_solution(6648371219847841677)
XLA Ops:
  0.6 0.0 copy-start
  0.6 5.5 %gene_products.1 = (f32[8,80,128]{2,1,0:T(8,128)S(1)}, bf16[8192,512]{1,0:T(8,128)(2,1)S(1)}) custom-call(bf16[8192,512]{1,0:T(8,128)(2,1)} %bitcast.1, bf16[1024,128]{1,0:T(8,128)(2,1)} %factor_hbm.1, bf16[8,128]{1,0:T(8,128)(2,1)} %context_ref.5), custom_call_target="tpu_custom_call" | custom-call | tf_op jit(solution)/shard_map/gene_products/pallas_call | solution.py:237
  6.2 20.5 %all_to_all.25.in_ref = f32[8,80,128]{2,1,0:T(8,128)S(1)} all-to-all(f32[8,80,128]{2,1,0:T(8,128)S(1)} %get-tuple-element.12), channel_id=1, replica_groups=mesh['pert'=8,'gene'=32] {'pert'}, dimensions={0} | all-to-all | bytes 655360 | tf_op jit(solution)/shard_map/all_to_all | solution.py:275
  26.7 13.6 %all_to_all.26.held_ref = f32[8,80,128]{2,1,0:T(8,128)S(1)} all-to-all(f32[8,80,128]{2,1,0:T(8,128)S(1)} %pert_sum.1), channel_id=1, replica_groups=mesh['pert'=8,'gene'=32] {'pert'}, dimensions={0} | all-to-all | bytes 655360 | tf_op jit(solution)/shard_map/all_to_all | solution.py:276
  40.4 0.0 copy-done
  40.4 6.9 %gene_solve.1 = (f32[16,40,128]{2,1,0:T(8,128)S(1)}, f32[512,128]{1,0:T(8,128)S(1)}, bf16[512,256]{1,0:T(8,128)(2,1)S(1)}, f32[128,128]{1,0:T(8,128)S(1)}) custom-call(f32[8,80,128]{2,1,0:T(8,128)S(1)} %all_to_all.26.held_ref, bf16[8,128]{1,0:T(8,128)(2,1)S(1)} %copy-done, bf16[8192,512]{1,0:T(8,128)(2,1)S(1)} %get-tuple-element.13.tensor_ref), custom_call_target="tpu_custom_call" | custom-call | tf_op jit(solution)/shard_map/gene_solve/pallas_call | solution.py:237
  47.3 3.5 %collective-permute-start = (f32[16,40,128]{2,1,0:T(8,128)S(1)}, f32[16,40,128]{2,1,0:T(8,128)S(1)}, u32[]{:S(2)}, u32[]{:S(2)}) collective-permute-start(f32[16,40,128]{2,1,0:T(8,128)S(1)} %get-tuple-element.16), channel_id=1, source_target_pairs={{0,1},{1,0},{2,3},{3,2},{4,5},{5,4},{6,7},{7,6},{8,9},{9,8},{10,11... | collective-permute-start | bytes 983048 | tf_op jit(solution)/shard_map/ppermute | solution.py:296
  50.8 1.3 %pert_products.1.a_ref = f32[16,40,128]{2,1,0:T(8,128)S(1)} custom-call(bf16[512,256]{1,0:T(8,128)(2,1)S(1)} %get-tuple-element.14.weights_ref, bf16[8,128]{1,0:T(8,128)(2,1)S(1)} %copy-done, bf16[8192,512]{1,0:T(8,128)(2,1)S(1)} %get-tuple-element.13.tensor_ref, f32[128,128]{1,0:T(8,128)S(1)} %get-tuple-element.15.gram_ref), custom_call_target="tpu_custom_call" | custom-call | tf_op jit(solution)/shard_map/pert_products/pallas_call | solution.py:237
  52.1 0.0 collective-permute-done.b_ref
  52.2 14.6 %all_to_all.27.in_ref = f32[16,40,128]{2,1,0:T(8,128)S(1)} all-to-all(f32[16,40,128]{2,1,0:T(8,128)S(1)} %core_sum.1), channel_id=1, replica_groups={{0,2,4,6,8,10,12,14,16,18,20,22,24,26,28,30},{1,3,5,7,9,11,13,15,17,19,..., dimensions={0} | all-to-all | bytes 655360 | tf_op jit(solution)/shard_map/all_to_all | solution.py:304
  66.8 11.5 %all_to_all.28.mine_ref = f32[16,40,128]{2,1,0:T(8,128)S(1)} all-to-all(f32[16,40,128]{2,1,0:T(8,128)S(1)} %gene_sum.1), channel_id=1, replica_groups={{0,2,4,6,8,10,12,14,16,18,20,22,24,26,28,30},{1,3,5,7,9,11,13,15,17,19,..., dimensions={0} | all-to-all | bytes 655360 | tf_op jit(solution)/shard_map/all_to_all | solution.py:305
  78.3 2.9 %collective-permute-start.1 = (f32[16,40,128]{2,1,0:T(8,128)S(1)}, f32[16,40,128]{2,1,0:T(8,128)S(1)}, u32[]{:S(2)}, u32[]{:S(2)}) collective-permute-start(f32[16,40,128]{2,1,0:T(8,128)S(1)} %all_to_all.28.mine_ref), channel_id=1, source_target_pairs={{0,1},{1,0},{2,3},{3,2},{4,5},{5,4},{6,7},{7,6},{8,9},{9,8},{10,11... | collective-permute-start | bytes 983048 | tf_op jit(solution)/shard_map/ppermute | solution.py:308
  81.2 4.6 %pert_inverse.1 = (bf16[512,128]{1,0:T(8,128)(2,1)}, f32[128,128]{1,0:T(8,128)S(1)}) custom-call(f32[16,40,128]{2,1,0:T(8,128)S(1)} %all_to_all.28.mine_ref, bf16[8,128]{1,0:T(8,128)(2,1)S(1)} %copy-done, f32[512,128]{1,0:T(8,128)S(1)} %get-tuple-element.17.solved_ref), custom_call_target="tpu_custom_call" | custom-call | tf_op jit(solution)/shard_map/pert_inverse/pallas_call | solution.py:237
  85.7 0.0 collective-permute-done.1.other_ref
  85.8 0.6 pert_solve.1
  86.3 8.9 %all_to_all.29.held_ref = f32[8,1,128]{2,1,0:T(1,128)S(1)} all-to-all(f32[8,1,128]{2,1,0:T(1,128)S(1)} %get-tuple-element.20), channel_id=1, replica_groups=mesh['pert'=8,'gene'=32] {'pert'}, dimensions={0} | all-to-all | bytes 8192 | tf_op jit(solution)/shard_map/all_to_all | solution.py:322
  95.3 0.8 pert_scale.1
  (3 shorter events, 0.1 us)
Async XLA Ops:
  0.6 39.7 %copy-start = (bf16[8,128]{1,0:T(8,128)(2,1)S(1)}, bf16[8,128]{1,0:T(8,128)(2,1)}, u32[]{:S(2)}) copy-start(bf16[8,128]{1,0:T(8,128)(2,1)} %context_ref.5) | copy-start | bytes 6148
  47.3 4.8 %collective-permute-start = (f32[16,40,128]{2,1,0:T(8,128)S(1)}, f32[16,40,128]{2,1,0:T(8,128)S(1)}, u32[]{:S(2)}, u32[]{:S(2)}) collective-permute-start(f32[16,40,128]{2,1,0:T(8,128)S(1)} %get-tuple-element.16), channel_id=1, source_target_pairs={{0,1},{1,0},{2,3},{3,2},{4,5},{5,4},{6,7},{7,6},{8,9},{9,8},{10,11... | collective-permute-start | bytes 983048 | tf_op jit(solution)/shard_map/ppermute | solution.py:296
  78.3 7.5 %collective-permute-start.1 = (f32[16,40,128]{2,1,0:T(8,128)S(1)}, f32[16,40,128]{2,1,0:T(8,128)S(1)}, u32[]{:S(2)}, u32[]{:S(2)}) collective-permute-start(f32[16,40,128]{2,1,0:T(8,128)S(1)} %all_to_all.28.mine_ref), channel_id=1, source_target_pairs={{0,1},{1,0},{2,3},{3,2},{4,5},{5,4},{6,7},{7,6},{8,9},{9,8},{10,11... | collective-permute-start | bytes 983048 | tf_op jit(solution)/shard_map/ppermute | solution.py:308

commit v4 on v3

--- a/solution.py
+++ b/solution.py
@@ -90,43 +90,46 @@
 def gene_products(
     blocks, tensor_ref, factor_hbm, context_hbm, out_ref, keep, factor_ref, context_ref, left, sems, small
 ):
-    height = keep.shape[0] // blocks
+    depth = 3
+    starts = [sum(blocks[:b]) for b in range(len(blocks))]
     copies = []
-    for b in range(blocks):
-        rows = pl.ds(b * height, height)
+    for b, height in enumerate(blocks):
+        rows = pl.ds(starts[b], height)
         copies.append(pltpu.make_async_copy(tensor_ref.at[rows, :], keep.at[rows, :], sems.at[b]))
     first = pltpu.make_async_copy(factor_hbm, factor_ref, small.at[0])
     second = pltpu.make_async_copy(context_hbm, context_ref, small.at[1])
     first.start()
     second.start()
-    copies[0].start()
-    copies[1].start()
+    for copy in copies[:depth]:
+        copy.start()
     contexts, rank = context_ref.shape
     chunks, tall, _ = out_ref.shape
     part = rank // chunks
     genes = tall - part
     first.wait()
     second.wait()
+    context32 = context_ref[...].astype(f32)
+
+    def build(b):
+        perts = blocks[b] // contexts
+        factor = factor_ref[pl.ds(starts[b] // contexts, perts), :].astype(f32)
+        rows = (factor[:, None, :] * context32[None]).reshape(blocks[b], rank)
+        hi, lo = split(rows.T)
+        left[b % 2, :rank, : blocks[b]] = hi
+        left[b % 2, rank:, : blocks[b]] = lo
+
+    build(0)
     gram = gram_of(factor_ref[...])
     for q in range(chunks):
         out_ref[q, genes:, :] = gram[q * part : (q + 1) * part, :]
-    context32 = context_ref[...].astype(f32)
-    perts = height // contexts
-
-    def build(b):
-        factor = factor_ref[pl.ds(b * perts, perts), :].astype(f32)
-        rows = (factor[:, None, :] * context32[None]).reshape(height, rank)
-        left[b % 2, :rank, :], left[b % 2, rank:, :] = split(rows.T)
-
-    build(0)
     total = None
-    for b in range(blocks):
+    for b in range(len(blocks)):
         copies[b].wait()
-        if b + 2 < blocks:
-            copies[b + 2].start()
-        if b + 1 < blocks:
+        if b + depth < len(blocks):
+            copies[b + depth].start()
+        if b + 1 < len(blocks):
             build(b + 1)
-        product = dot(left[b % 2], keep[pl.ds(b * height, height), :])
+        product = dot(left[b % 2, :, : blocks[b]], keep[pl.ds(starts[b], blocks[b]), :])
         total = product if total is None else total + product
     summed = (total[:rank, :] + total[rank:, :]).T
     for q in range(chunks):
@@ -189,14 +192,18 @@
     )
 
 
-def pert_inverse(gene_count, mine_ref, context_ref, solved_ref, gene_ref, inv_ref):
+def pert_inverse(gene_count, mine_ref, context_ref, inv_ref, rate_ref):
     chunks, tall, rank = mine_ref.shape
     perts = tall - rank // chunks
     gram_s = mine_ref[:, perts:, :].reshape(rank, rank)
     diag_row, _ = diagonal(gram_s, eye(rank))
     scale_c = jnp.sqrt(diag_row / gene_count + epsilon)
-    gene_ref[...] = (solved_ref[...] / scale_c).astype(bf16)
+    rate_ref[...] = 1.0 / scale_c
     inv_ref[...] = inverse(gram_s * gram_of(context_ref[...])) * scale_c
+
+
+def gene_scale(solved_ref, rate_ref, out_ref):
+    out_ref[...] = (solved_ref[...] * rate_ref[...]).astype(bf16)
 
 
 def pert_solve(mine_ref, other_ref, inv_ref, out_ref, squares_ref):
@@ -217,7 +224,7 @@
 def pert_scale(pert_count, held_ref, solved_ref, out_ref):
     squares = jnp.sum(held_ref[...], axis=0)
     scale_a = jnp.sqrt(squares / pert_count + epsilon)
-    out_ref[...] = (solved_ref[...] / scale_a).astype(bf16)
+    out_ref[...] = (solved_ref[...] * (1.0 / scale_a)).astype(bf16)
 
 
 VMEM = pl.BlockSpec(memory_space=pltpu.VMEM)
@@ -255,7 +262,8 @@
     n_pert = lax.axis_size("pert")
     n_gene = lax.axis_size("gene")
     flat = tensor.reshape(rows_i * contexts, rows_j)
-    blocks = 4
+    eighth = rows_i * contexts // 8
+    blocks = (eighth, eighth, 2 * eighth, 2 * eighth, 2 * eighth)
     tall = rows_j // n_pert + rank // n_pert
 
     partial, kept = call(
@@ -267,14 +275,15 @@
         scratch=(
             pltpu.VMEM(pert_factor.shape, bf16),
             pltpu.VMEM(context_factor.shape, bf16),
-            pltpu.VMEM((2, 2 * rank, flat.shape[0] // blocks), bf16),
-            pltpu.SemaphoreType.DMA((blocks,)),
+            pltpu.VMEM((2, 2 * rank, max(blocks)), bf16),
+            pltpu.SemaphoreType.DMA((len(blocks),)),
             pltpu.SemaphoreType.DMA((2,)),
         ),
     )
     partial = lax.all_to_all(partial, "pert", 0, 0)
     gathered = lax.all_to_all(summed_copies(partial, "pert_sum"), "pert", 0, 0)
 
+    context_factor = near(context_factor)
     chips = n_gene // 2
     perts = rows_i // n_gene
     message = pltpu.VMEM((chips, perts + rank // chips, rank), f32)
@@ -307,11 +316,11 @@
     )
     other = lax.ppermute(mine, "gene", swap)
     mine = near(mine)
-    gene_factor, inv = call(
+    inv, rate = call(
         functools.partial(pert_inverse, rows_j * n_gene),
         "pert_inverse",
-        (mine, context_factor, near(solved_c)),
-        (jax.ShapeDtypeStruct((rows_j, rank), bf16), square),
+        (mine, context_factor),
+        (square, pltpu.VMEM((1, rank), f32)),
     )
     solved_a, squares = call(
         pert_solve,
@@ -320,6 +329,12 @@
         (pltpu.VMEM((rows_i, rank), f32), pltpu.VMEM((n_pert, 1, rank), f32)),
     )
     squares = lax.all_to_all(squares, "pert", 0, 0)
+    gene_factor = call(
+        gene_scale,
+        "gene_scale",
+        (near(solved_c), near(rate)),
+        jax.ShapeDtypeStruct((rows_j, rank), bf16),
+    )
     pert_updated = call(
         functools.partial(pert_scale, rows_i * n_pert),
         "pert_scale",

time: 96.2 us -> 96.9 us (level)
  blocking collectives: 69.2 us -> 60.4 us
  waiting for transfers between devices: 0.01 us -> 5.73 us
  starting transfers between devices: 6.41 us -> 9.72 us
    all_to_all x1 -> x0, blocking collectives: 8.92 us -> none  [shards(): squares = lax.all_to_all(squares, 'pert', 0, 0)]
    all_to_all x0 -> x1, waiting for transfers between devices: none -> 5.73 us  [shards(): squares = lax.all_to_all(squares, 'pert', 0, 0)]
    all_to_all x0 -> x1, starting transfers between devices: none -> 3.31 us  [shards(): squares = lax.all_to_all(squares, 'pert', 0, 0)]
    pallas_call x9 -> x10, Pallas kernels: 19.7 us -> 19.9 us  [call(): pl.pallas_call(body, in_specs=in_specs or [VMEM] * len(inputs), out_specs...]
  transfers between devices with their start and end apart: 2 -> 3, of which waited for: 0 -> 1; matrix products, arithmetic and copies ran while one was open for 0% -> 0% of each run, Pallas kernels for 6% -> 6%
where the time goes in v4:
time: 96.9 us; the launch traced here: 96.5 us
  blocking collectives  60.4 us (62%)
  Pallas kernels  19.9 us (21%)
  starting transfers between devices  9.72 us (10%)
  waiting for transfers between devices  5.73 us (6%)
    all_to_all x1, blocking collectives, shards(): partial = lax.all_to_all(partial, 'pert', 0, 0)  20.6 us
    pallas_call x10, Pallas kernels, call(): pl.pallas_call(body, in_specs=in_specs or [VMEM] * len(inputs), out_specs...  19.9 us
    all_to_all x1, blocking collectives, shards(): partial = lax.all_to_all(partial, 'gene', 0, 0, axis_index_groups=groups)  14.8 us
    all_to_all x1, blocking collectives, shards(): gathered = lax.all_to_all(summed_copies(partial, 'pert_sum'), 'pert', 0, 0)  13.6 us
    all_to_all x1, blocking collectives, shards(): lax.all_to_all(summed_copies(partial, 'gene_sum'), 'gene', 0, 0, axis_ind...  11.5 us
    all_to_all x1, waiting for transfers between devices, shards(): squares = lax.all_to_all(squares, 'pert', 0, 0)  5.73 us
    ppermute x1, starting transfers between devices, shards(): other = lax.ppermute(other, 'gene', swap)  3.52 us
    all_to_all x1, starting transfers between devices, shards(): squares = lax.all_to_all(squares, 'pert', 0, 0)  3.31 us
  transfers between devices with their start and end apart: 3, of which 1 were waited for; matrix products, arithmetic and copies ran while one was open for 0% of the time, Pallas kernels for 6%

profile of v4, /device:TPU:1, one launch (start us, length us, event | category | flops | bytes accessed | tf_op | source)
XLA Modules:
  0.0 96.5 jit_solution(9153939817570670009)
XLA Ops:
  0.6 0.0 copy-start
  0.6 5.4 %gene_products.1 = (f32[8,80,128]{2,1,0:T(8,128)S(1)}, bf16[8192,512]{1,0:T(8,128)(2,1)S(1)}) custom-call(bf16[8192,512]{1,0:T(8,128)(2,1)} %bitcast.1, bf16[1024,128]{1,0:T(8,128)(2,1)} %factor_hbm.1, bf16[8,128]{1,0:T(8,128)(2,1)} %context_ref.5), custom_call_target="tpu_custom_call" | custom-call | tf_op jit(solution)/shard_map/gene_products/pallas_call | solution.py:244
  6.0 20.6 %all_to_all.25.in_ref = f32[8,80,128]{2,1,0:T(8,128)S(1)} all-to-all(f32[8,80,128]{2,1,0:T(8,128)S(1)} %get-tuple-element.12), channel_id=1, replica_groups=mesh['pert'=8,'gene'=32] {'pert'}, dimensions={0} | all-to-all | bytes 655360 | tf_op jit(solution)/shard_map/all_to_all | solution.py:283
  26.6 13.6 %all_to_all.26.held_ref = f32[8,80,128]{2,1,0:T(8,128)S(1)} all-to-all(f32[8,80,128]{2,1,0:T(8,128)S(1)} %pert_sum.1), channel_id=1, replica_groups=mesh['pert'=8,'gene'=32] {'pert'}, dimensions={0} | all-to-all | bytes 655360 | tf_op jit(solution)/shard_map/all_to_all | solution.py:284
  40.2 0.0 copy-done
  40.2 6.6 %gene_solve.1 = (f32[16,40,128]{2,1,0:T(8,128)S(1)}, f32[512,128]{1,0:T(8,128)S(1)}, bf16[512,256]{1,0:T(8,128)(2,1)S(1)}, f32[128,128]{1,0:T(8,128)S(1)}) custom-call(f32[8,80,128]{2,1,0:T(8,128)S(1)} %all_to_all.26.held_ref, bf16[8,128]{1,0:T(8,128)(2,1)S(1)} %copy-done, bf16[8192,512]{1,0:T(8,128)(2,1)S(1)} %get-tuple-element.13.tensor_ref), custom_call_target="tpu_custom_call" | custom-call | tf_op jit(solution)/shard_map/gene_solve/pallas_call | solution.py:244
  46.9 3.5 %collective-permute-start = (f32[16,40,128]{2,1,0:T(8,128)S(1)}, f32[16,40,128]{2,1,0:T(8,128)S(1)}, u32[]{:S(2)}, u32[]{:S(2)}) collective-permute-start(f32[16,40,128]{2,1,0:T(8,128)S(1)} %get-tuple-element.17), channel_id=1, source_target_pairs={{0,1},{1,0},{2,3},{3,2},{4,5},{5,4},{6,7},{7,6},{8,9},{9,8},{10,11... | collective-permute-start | bytes 983048 | tf_op jit(solution)/shard_map/ppermute | solution.py:305
  50.4 1.3 %pert_products.1.a_ref = f32[16,40,128]{2,1,0:T(8,128)S(1)} custom-call(bf16[512,256]{1,0:T(8,128)(2,1)S(1)} %get-tuple-element.15.weights_ref, bf16[8,128]{1,0:T(8,128)(2,1)S(1)} %copy-done, bf16[8192,512]{1,0:T(8,128)(2,1)S(1)} %get-tuple-element.13.tensor_ref, f32[128,128]{1,0:T(8,128)S(1)} %get-tuple-element.16.gram_ref), custom_call_target="tpu_custom_call" | custom-call | tf_op jit(solution)/shard_map/pert_products/pallas_call | solution.py:244
  51.7 0.0 collective-permute-done.b_ref
  51.7 14.8 %all_to_all.27.in_ref = f32[16,40,128]{2,1,0:T(8,128)S(1)} all-to-all(f32[16,40,128]{2,1,0:T(8,128)S(1)} %core_sum.1), channel_id=1, replica_groups={{0,2,4,6,8,10,12,14,16,18,20,22,24,26,28,30},{1,3,5,7,9,11,13,15,17,19,..., dimensions={0} | all-to-all | bytes 655360 | tf_op jit(solution)/shard_map/all_to_all | solution.py:313
  66.5 11.5 %all_to_all.28.mine_ref = f32[16,40,128]{2,1,0:T(8,128)S(1)} all-to-all(f32[16,40,128]{2,1,0:T(8,128)S(1)} %gene_sum.1), channel_id=1, replica_groups={{0,2,4,6,8,10,12,14,16,18,20,22,24,26,28,30},{1,3,5,7,9,11,13,15,17,19,..., dimensions={0} | all-to-all | bytes 655360 | tf_op jit(solution)/shard_map/all_to_all | solution.py:314
  78.1 2.9 %collective-permute-start.1 = (f32[16,40,128]{2,1,0:T(8,128)S(1)}, f32[16,40,128]{2,1,0:T(8,128)S(1)}, u32[]{:S(2)}, u32[]{:S(2)}) collective-permute-start(f32[16,40,128]{2,1,0:T(8,128)S(1)} %all_to_all.28.mine_ref), channel_id=1, source_target_pairs={{0,1},{1,0},{2,3},{3,2},{4,5},{5,4},{6,7},{7,6},{8,9},{9,8},{10,11... | collective-permute-start | bytes 983048 | tf_op jit(solution)/shard_map/ppermute | solution.py:317
  80.9 3.9 %pert_inverse.1 = (f32[128,128]{1,0:T(8,128)S(1)}, f32[1,128]{1,0:T(1,128)S(1)}) custom-call(f32[16,40,128]{2,1,0:T(8,128)S(1)} %all_to_all.28.mine_ref, bf16[8,128]{1,0:T(8,128)(2,1)S(1)} %copy-done), custom_call_target="tpu_custom_call" | custom-call | tf_op jit(solution)/shard_map/pert_inverse/pallas_call | solution.py:244
  84.9 0.0 collective-permute-done.1.other_ref
  84.9 1.2 %pert_solve.1 = (f32[1024,128]{1,0:T(8,128)S(1)}, f32[8,1,128]{2,1,0:T(1,128)}) custom-call(f32[16,40,128]{2,1,0:T(8,128)S(1)} %all_to_all.28.mine_ref, f32[16,40,128]{2,1,0:T(8,128)S(1)} %collective-permute-done.1.other_ref, f32[128,128]{1,0:T(8,128)S(1)} %get-tuple-element.19.inv_ref), custom_call_target="tpu_custom_call" | custom-call | tf_op jit(solution)/shard_map/pert_solve/pallas_call | solution.py:244
  86.1 3.3 %all-to-all-start.4 = ((f32[8,1,128]{2,1,0:T(1,128)}), f32[8,1,128]{2,1,0:T(1,128)S(1)}, u32[]{:S(2)}, u32[]{:S(2)}) async-start(f32[8,1,128]{2,1,0:T(1,128)} %get-tuple-element.20), calls=%async_computation.4 | async-start | bytes 8192 | tf_op jit(solution)/shard_map/all_to_all | solution.py:331
  89.4 0.7 gene_scale.1
  90.1 5.7 %all-to-all-done.4.held_ref = f32[8,1,128]{2,1,0:T(1,128)S(1)} async-done(((f32[8,1,128]{2,1,0:T(1,128)}), f32[8,1,128]{2,1,0:T(1,128)S(1)}, u32[]{:S(2)}, u32[]{:S(2)}) %all-to-all-start.4) | async-done | bytes 4128 | tf_op jit(solution)/shard_map/all_to_all | solution.py:331
  95.8 0.8 pert_scale.1
  (3 shorter events, 0.1 us)
Async XLA Ops:
  0.6 39.6 %copy-start = (bf16[8,128]{1,0:T(8,128)(2,1)S(1)}, bf16[8,128]{1,0:T(8,128)(2,1)}, u32[]{:S(2)}) copy-start(bf16[8,128]{1,0:T(8,128)(2,1)} %context_ref.5) | copy-start | bytes 6148
  46.9 4.8 %collective-permute-start = (f32[16,40,128]{2,1,0:T(8,128)S(1)}, f32[16,40,128]{2,1,0:T(8,128)S(1)}, u32[]{:S(2)}, u32[]{:S(2)}) collective-permute-start(f32[16,40,128]{2,1,0:T(8,128)S(1)} %get-tuple-element.17), channel_id=1, source_target_pairs={{0,1},{1,0},{2,3},{3,2},{4,5},{5,4},{6,7},{7,6},{8,9},{9,8},{10,11... | collective-permute-start | bytes 983048 | tf_op jit(solution)/shard_map/ppermute | solution.py:305
  78.1 6.8 %collective-permute-start.1 = (f32[16,40,128]{2,1,0:T(8,128)S(1)}, f32[16,40,128]{2,1,0:T(8,128)S(1)}, u32[]{:S(2)}, u32[]{:S(2)}) collective-permute-start(f32[16,40,128]{2,1,0:T(8,128)S(1)} %all_to_all.28.mine_ref), channel_id=1, source_target_pairs={{0,1},{1,0},{2,3},{3,2},{4,5},{5,4},{6,7},{7,6},{8,9},{9,8},{10,11... | collective-permute-start | bytes 983048 | tf_op jit(solution)/shard_map/ppermute | solution.py:317
  86.1 9.7 %all-to-all-start.4 = ((f32[8,1,128]{2,1,0:T(1,128)}), f32[8,1,128]{2,1,0:T(1,128)S(1)}, u32[]{:S(2)}, u32[]{:S(2)}) async-start(f32[8,1,128]{2,1,0:T(1,128)} %get-tuple-element.20), calls=%async_computation.4 | async-start | bytes 8192 | tf_op jit(solution)/shard_map/all_to_all | solution.py:331

commit v5 on v4

--- a/solution.py
+++ b/solution.py
@@ -61,24 +61,19 @@
         product = dot_split(jnp.concatenate([x, r], axis=0), r)
         return x + product[:n, :], product[n:, :]
 
-    def measured(state):
-        x, r, _, count = state
-        x, r = advance(x, r)
-        return x, r, row_norm(r), count + 1
-
-    def bounded(state):
-        x, r, bound = state
-        return *advance(x, r), bound * bound
+    def more(state):
+        x, r, bound, count = state
+        norm = row_norm(r)
+        return *advance(x, r), norm * norm, count + 1
 
     def newton(_, x):
         return x + dot_split(x, unit - dot(scaled, x, precision=HIGHEST))
 
     x, r, bound, _ = lax.while_loop(
-        lambda s: jnp.logical_and(s[2] > 0.95, s[3] < 40),
-        measured,
+        lambda s: jnp.logical_and(s[2] > 1e-7, s[3] < 40),
+        more,
         (x, r, jnp.where(far_off, 1.0, off * off), 0),
     )
-    x, r, bound = lax.while_loop(lambda s: s[2] > 1e-7, bounded, (x, r, jnp.minimum(bound, 0.95)))
     x = lax.fori_loop(0, jnp.where(far_off, 4, jnp.where(off > 0.8, 1, 0)), newton, x)
     return x * scale_col * scale_row
 
@@ -202,10 +197,6 @@
     inv_ref[...] = inverse(gram_s * gram_of(context_ref[...])) * scale_c
 
 
-def gene_scale(solved_ref, rate_ref, out_ref):
-    out_ref[...] = (solved_ref[...] * rate_ref[...]).astype(bf16)
-
-
 def pert_solve(mine_ref, other_ref, inv_ref, out_ref, squares_ref):
     chunks, tall, rank = mine_ref.shape
     perts = tall - rank // chunks
@@ -221,10 +212,23 @@
     squares_ref[...] = jnp.broadcast_to((squares[0] + squares[1])[None], squares_ref.shape)
 
 
-def pert_scale(pert_count, held_ref, solved_ref, out_ref):
+def scale(pert_count, held_ref, solved_a_ref, solved_c_ref, rate_ref, gene_ref, pert_ref, gene, pert, sems):
+    gene[...] = (solved_c_ref[...] * rate_ref[...]).astype(bf16)
+    first = pltpu.make_async_copy(gene, gene_ref, sems.at[0])
+    first.start()
     squares = jnp.sum(held_ref[...], axis=0)
-    scale_a = jnp.sqrt(squares / pert_count + epsilon)
-    out_ref[...] = (solved_ref[...] * (1.0 / scale_a)).astype(bf16)
+    rate = 1.0 / jnp.sqrt(squares / pert_count + epsilon)
+    half = pert.shape[0] // 2
+    copies = []
+    for h in range(2):
+        rows = pl.ds(h * half, half)
+        pert[rows, :] = (solved_a_ref[rows, :] * rate).astype(bf16)
+        copy = pltpu.make_async_copy(pert.at[rows, :], pert_ref.at[rows, :], sems.at[1 + h])
+        copy.start()
+        copies.append(copy)
+    first.wait()
+    for copy in copies:
+        copy.wait()
 
 
 VMEM = pl.BlockSpec(memory_space=pltpu.VMEM)
@@ -239,12 +243,12 @@
     return pltpu.with_memory_space_constraint(x, pltpu.HBM)
 
 
-def call(body, name, inputs, outputs, in_specs=None, scratch=(), limit=16):
+def call(body, name, inputs, outputs, in_specs=None, out_spec=VMEM, scratch=(), limit=16):
     single = not isinstance(outputs, tuple)
     return pl.pallas_call(
         body,
         in_specs=in_specs or [VMEM] * len(inputs),
-        out_specs=VMEM if single else (VMEM,) * len(outputs),
+        out_specs=out_spec if single else (out_spec,) * len(outputs),
         out_shape=outputs,
         scratch_shapes=list(scratch),
         compiler_params=pltpu.CompilerParams(vmem_limit_bytes=limit << 20),
@@ -329,19 +333,18 @@
         (pltpu.VMEM((rows_i, rank), f32), pltpu.VMEM((n_pert, 1, rank), f32)),
     )
     squares = lax.all_to_all(squares, "pert", 0, 0)
-    gene_factor = call(
-        gene_scale,
-        "gene_scale",
-        (near(solved_c), near(rate)),
+    outputs = (
         jax.ShapeDtypeStruct((rows_j, rank), bf16),
-    )
-    pert_updated = call(
-        functools.partial(pert_scale, rows_i * n_pert),
-        "pert_scale",
-        (near(squares), near(solved_a)),
         jax.ShapeDtypeStruct((rows_i, rank), bf16),
     )
-    return (gene_factor, pert_updated)
+    return call(
+        functools.partial(scale, rows_i * n_pert),
+        "scale",
+        (near(squares), near(solved_a), near(solved_c), near(rate)),
+        outputs,
+        out_spec=FAR,
+        scratch=[pltpu.VMEM(o.shape, bf16) for o in outputs] + [pltpu.SemaphoreType.DMA((3,))],
+    )
 
 
 def solution(mesh):

time: 96.9 us -> 94.4 us (0.974)
  blocking collectives: 60.4 us -> 69.4 us
  waiting for transfers between devices: 5.73 us -> 0.01 us
  starting transfers between devices: 9.72 us -> 6.42 us
  Pallas kernels: 19.9 us -> 17.6 us
    all_to_all x0 -> x1, blocking collectives: none -> 8.92 us  [shards(): squares = lax.all_to_all(squares, 'pert', 0, 0)]
    all_to_all x1 -> x0, waiting for transfers between devices: 5.73 us -> none  [shards(): squares = lax.all_to_all(squares, 'pert', 0, 0)]
    all_to_all x1 -> x0, starting transfers between devices: 3.31 us -> none  [shards(): squares = lax.all_to_all(squares, 'pert', 0, 0)]
    pallas_call x10 -> x9, Pallas kernels: 19.9 us -> 17.6 us  [call(): pl.pallas_call(body, in_specs=in_specs or [VMEM] * len(inputs), out_specs...]
  transfers between devices with their start and end apart: 3 -> 2, of which waited for: 1 -> 0; matrix products, arithmetic and copies ran while one was open for 0% -> 0% of each run, Pallas kernels for 6% -> 5%
where the time goes in v5:
time: 94.4 us; the launch traced here: 94.1 us
  blocking collectives  69.4 us (74%)
  Pallas kernels  17.6 us (19%)
  starting transfers between devices  6.42 us (7%)
    all_to_all x1, blocking collectives, shards(): partial = lax.all_to_all(partial, 'pert', 0, 0)  20.6 us
    pallas_call x9, Pallas kernels, call(): pl.pallas_call(body, in_specs=in_specs or [VMEM] * len(inputs), out_specs...  17.6 us
    all_to_all x1, blocking collectives, shards(): partial = lax.all_to_all(partial, 'gene', 0, 0, axis_index_groups=groups)  14.7 us
    all_to_all x1, blocking collectives, shards(): gathered = lax.all_to_all(summed_copies(partial, 'pert_sum'), 'pert', 0, 0)  13.6 us
    all_to_all x1, blocking collectives, shards(): lax.all_to_all(summed_copies(partial, 'gene_sum'), 'gene', 0, 0, axis_ind...  11.5 us
    all_to_all x1, blocking collectives, shards(): squares = lax.all_to_all(squares, 'pert', 0, 0)  8.92 us
    ppermute x1, starting transfers between devices, shards(): other = lax.ppermute(other, 'gene', swap)  3.53 us
    ppermute x1, starting transfers between devices, shards(): other = lax.ppermute(mine, 'gene', swap)  2.89 us
  transfers between devices with their start and end apart: 2, of which 0 were waited for; matrix products, arithmetic and copies ran while one was open for 0% of the time, Pallas kernels for 5%

profile of v5, /device:TPU:1, one launch (start us, length us, event | category | flops | bytes accessed | tf_op | source)
XLA Modules:
  0.0 94.1 jit_solution(2977801630156999352)
XLA Ops:
  0.6 0.0 copy-start
  0.6 5.4 %gene_products.1 = (f32[8,80,128]{2,1,0:T(8,128)S(1)}, bf16[8192,512]{1,0:T(8,128)(2,1)S(1)}) custom-call(bf16[8192,512]{1,0:T(8,128)(2,1)} %bitcast.1, bf16[1024,128]{1,0:T(8,128)(2,1)} %factor_hbm.1, bf16[8,128]{1,0:T(8,128)(2,1)} %context_ref.5), custom_call_target="tpu_custom_call" | custom-call | tf_op jit(solution)/shard_map/gene_products/pallas_call | solution.py:248
  6.0 20.6 %all_to_all.25.in_ref = f32[8,80,128]{2,1,0:T(8,128)S(1)} all-to-all(f32[8,80,128]{2,1,0:T(8,128)S(1)} %get-tuple-element.12), channel_id=1, replica_groups=mesh['pert'=8,'gene'=32] {'pert'}, dimensions={0} | all-to-all | bytes 655360 | tf_op jit(solution)/shard_map/all_to_all | solution.py:287
  26.6 13.6 %all_to_all.26.held_ref = f32[8,80,128]{2,1,0:T(8,128)S(1)} all-to-all(f32[8,80,128]{2,1,0:T(8,128)S(1)} %pert_sum.1), channel_id=1, replica_groups=mesh['pert'=8,'gene'=32] {'pert'}, dimensions={0} | all-to-all | bytes 655360 | tf_op jit(solution)/shard_map/all_to_all | solution.py:288
  40.2 0.0 copy-done
  40.2 5.8 %gene_solve.1 = (f32[16,40,128]{2,1,0:T(8,128)S(1)}, f32[512,128]{1,0:T(8,128)S(1)}, bf16[512,256]{1,0:T(8,128)(2,1)S(1)}, f32[128,128]{1,0:T(8,128)S(1)}) custom-call(f32[8,80,128]{2,1,0:T(8,128)S(1)} %all_to_all.26.held_ref, bf16[8,128]{1,0:T(8,128)(2,1)S(1)} %copy-done, bf16[8192,512]{1,0:T(8,128)(2,1)S(1)} %get-tuple-element.13.tensor_ref), custom_call_target="tpu_custom_call" | custom-call | tf_op jit(solution)/shard_map/gene_solve/pallas_call | solution.py:248
  46.1 3.5 %collective-permute-start = (f32[16,40,128]{2,1,0:T(8,128)S(1)}, f32[16,40,128]{2,1,0:T(8,128)S(1)}, u32[]{:S(2)}, u32[]{:S(2)}) collective-permute-start(f32[16,40,128]{2,1,0:T(8,128)S(1)} %get-tuple-element.16), channel_id=1, source_target_pairs={{0,1},{1,0},{2,3},{3,2},{4,5},{5,4},{6,7},{7,6},{8,9},{9,8},{10,11... | collective-permute-start | bytes 983048 | tf_op jit(solution)/shard_map/ppermute | solution.py:309
  49.6 1.3 %pert_products.1.a_ref = f32[16,40,128]{2,1,0:T(8,128)S(1)} custom-call(bf16[512,256]{1,0:T(8,128)(2,1)S(1)} %get-tuple-element.14.weights_ref, bf16[8,128]{1,0:T(8,128)(2,1)S(1)} %copy-done, bf16[8192,512]{1,0:T(8,128)(2,1)S(1)} %get-tuple-element.13.tensor_ref, f32[128,128]{1,0:T(8,128)S(1)} %get-tuple-element.15.gram_ref), custom_call_target="tpu_custom_call" | custom-call | tf_op jit(solution)/shard_map/pert_products/pallas_call | solution.py:248
  50.9 0.0 collective-permute-done.b_ref
  50.9 14.7 %all_to_all.27.in_ref = f32[16,40,128]{2,1,0:T(8,128)S(1)} all-to-all(f32[16,40,128]{2,1,0:T(8,128)S(1)} %core_sum.1), channel_id=1, replica_groups={{0,2,4,6,8,10,12,14,16,18,20,22,24,26,28,30},{1,3,5,7,9,11,13,15,17,19,..., dimensions={0} | all-to-all | bytes 655360 | tf_op jit(solution)/shard_map/all_to_all | solution.py:317
  65.7 11.5 %all_to_all.28.mine_ref = f32[16,40,128]{2,1,0:T(8,128)S(1)} all-to-all(f32[16,40,128]{2,1,0:T(8,128)S(1)} %gene_sum.1), channel_id=1, replica_groups={{0,2,4,6,8,10,12,14,16,18,20,22,24,26,28,30},{1,3,5,7,9,11,13,15,17,19,..., dimensions={0} | all-to-all | bytes 655360 | tf_op jit(solution)/shard_map/all_to_all | solution.py:318
  77.3 2.9 %collective-permute-start.1 = (f32[16,40,128]{2,1,0:T(8,128)S(1)}, f32[16,40,128]{2,1,0:T(8,128)S(1)}, u32[]{:S(2)}, u32[]{:S(2)}) collective-permute-start(f32[16,40,128]{2,1,0:T(8,128)S(1)} %all_to_all.28.mine_ref), channel_id=1, source_target_pairs={{0,1},{1,0},{2,3},{3,2},{4,5},{5,4},{6,7},{7,6},{8,9},{9,8},{10,11... | collective-permute-start | bytes 983048 | tf_op jit(solution)/shard_map/ppermute | solution.py:321
  80.1 3.6 %pert_inverse.1 = (f32[128,128]{1,0:T(8,128)S(1)}, f32[1,128]{1,0:T(1,128)S(1)}) custom-call(f32[16,40,128]{2,1,0:T(8,128)S(1)} %all_to_all.28.mine_ref, bf16[8,128]{1,0:T(8,128)(2,1)S(1)} %copy-done), custom_call_target="tpu_custom_call" | custom-call | tf_op jit(solution)/shard_map/pert_inverse/pallas_call | solution.py:248
  83.8 0.0 collective-permute-done.1.other_ref
  83.8 0.6 pert_solve.1
  84.4 8.9 %all_to_all.29.held_ref = f32[8,1,128]{2,1,0:T(1,128)S(1)} all-to-all(f32[8,1,128]{2,1,0:T(1,128)S(1)} %get-tuple-element.18), channel_id=1, replica_groups=mesh['pert'=8,'gene'=32] {'pert'}, dimensions={0} | all-to-all | bytes 8192 | tf_op jit(solution)/shard_map/all_to_all | solution.py:335
  93.3 0.8 scale.1
  (3 shorter events, 0.1 us)
Async XLA Ops:
  0.6 39.6 %copy-start = (bf16[8,128]{1,0:T(8,128)(2,1)S(1)}, bf16[8,128]{1,0:T(8,128)(2,1)}, u32[]{:S(2)}) copy-start(bf16[8,128]{1,0:T(8,128)(2,1)} %context_ref.5) | copy-start | bytes 6148
  46.1 4.8 %collective-permute-start = (f32[16,40,128]{2,1,0:T(8,128)S(1)}, f32[16,40,128]{2,1,0:T(8,128)S(1)}, u32[]{:S(2)}, u32[]{:S(2)}) collective-permute-start(f32[16,40,128]{2,1,0:T(8,128)S(1)} %get-tuple-element.16), channel_id=1, source_target_pairs={{0,1},{1,0},{2,3},{3,2},{4,5},{5,4},{6,7},{7,6},{8,9},{9,8},{10,11... | collective-permute-start | bytes 983048 | tf_op jit(solution)/shard_map/ppermute | solution.py:309
  77.3 6.5 %collective-permute-start.1 = (f32[16,40,128]{2,1,0:T(8,128)S(1)}, f32[16,40,128]{2,1,0:T(8,128)S(1)}, u32[]{:S(2)}, u32[]{:S(2)}) collective-permute-start(f32[16,40,128]{2,1,0:T(8,128)S(1)} %all_to_all.28.mine_ref), channel_id=1, source_target_pairs={{0,1},{1,0},{2,3},{3,2},{4,5},{5,4},{6,7},{7,6},{8,9},{9,8},{10,11... | collective-permute-start | bytes 983048 | tf_op jit(solution)/shard_map/ppermute | solution.py:321

commit v6 on v5

--- a/solution.py
+++ b/solution.py
@@ -100,7 +100,7 @@
     contexts, rank = context_ref.shape
     chunks, tall, _ = out_ref.shape
     part = rank // chunks
-    genes = tall - part
+    genes = tall - 2 * part
     first.wait()
     second.wait()
     context32 = context_ref[...].astype(f32)
@@ -114,9 +114,10 @@
         left[b % 2, rank:, : blocks[b]] = lo
 
     build(0)
-    gram = gram_of(factor_ref[...])
-    for q in range(chunks):
-        out_ref[q, genes:, :] = gram[q * part : (q + 1) * part, :]
+    for shift, gram in enumerate(split(gram_of(factor_ref[...]))):
+        for q in range(chunks):
+            rows = pl.ds(genes + shift * part, part)
+            out_ref[q, rows, :] = gram[q * part : (q + 1) * part, :]
     total = None
     for b in range(len(blocks)):
         copies[b].wait()
@@ -126,13 +127,22 @@
             build(b + 1)
         product = dot(left[b % 2, :, : blocks[b]], keep[pl.ds(starts[b], blocks[b]), :])
         total = product if total is None else total + product
-    summed = (total[:rank, :] + total[rank:, :]).T
+    summed = (total[:rank, :] + total[rank:, :]).T.astype(bf16)
     for q in range(chunks):
         out_ref[q, :genes, :] = summed[q * genes : (q + 1) * genes, :]
 
 
 def sum_and_copy(in_ref, out_ref):
     total = jnp.sum(in_ref[...], axis=0)
+    for q in range(out_ref.shape[0]):
+        out_ref[q] = total
+
+
+def narrow_sum_and_copy(part, in_ref, out_ref):
+    total = jnp.sum(in_ref[...].astype(f32), axis=0)
+    genes = total.shape[0] - 2 * part
+    hi, lo = split(total[genes : genes + part, :] + total[genes + part :, :])
+    total = jnp.concatenate([total[:genes, :].astype(bf16), hi, lo], axis=0)
     for q in range(out_ref.shape[0]):
         out_ref[q] = total
 
@@ -166,10 +176,12 @@
 
 def gene_solve(blocks, held_ref, context_ref, tensor_ref, other_ref, solved_ref, weights_ref, gram_ref):
     chunks, tall, rank = held_ref.shape
-    genes = tall - rank // chunks
+    part = rank // chunks
+    genes = tall - 2 * part
     context = context_ref[...]
-    gram_a = jnp.concatenate([held_ref[q, genes:, :] for q in range(chunks)], axis=0)
-    mttkrp = jnp.concatenate([held_ref[q, :genes, :] for q in range(chunks)], axis=0)
+    held = held_ref[...].astype(f32)
+    gram_a = (held[:, genes : genes + part, :] + held[:, genes + part :, :]).reshape(rank, rank)
+    mttkrp = held[:, :genes, :].reshape(chunks * genes, rank)
     inv = inverse(gram_a * gram_of(context))
     solved = dot(mttkrp, inv, precision=HIGHEST)
     solved_ref[...] = solved
@@ -256,8 +268,8 @@
     )(*inputs)
 
 
-def summed_copies(x, name):
-    return call(sum_and_copy, name, (near(x),), pltpu.VMEM(x.shape, f32))
+def summed_copies(body, x, name):
+    return call(body, name, (near(x),), pltpu.VMEM(x.shape, x.dtype))
 
 
 def shards(tensor, pert_factor, context_factor):
@@ -268,13 +280,14 @@
     flat = tensor.reshape(rows_i * contexts, rows_j)
     eighth = rows_i * contexts // 8
     blocks = (eighth, eighth, 2 * eighth, 2 * eighth, 2 * eighth)
-    tall = rows_j // n_pert + rank // n_pert
+    part = rank // n_pert
+    tall = rows_j // n_pert + 2 * part
 
     partial, kept = call(
         functools.partial(gene_products, blocks),
         "gene_products",
         (far(flat), far(pert_factor), far(context_factor)),
-        (pltpu.VMEM((n_pert, tall, rank), f32), pltpu.VMEM(flat.shape, bf16)),
+        (pltpu.VMEM((n_pert, tall, rank), bf16), pltpu.VMEM(flat.shape, bf16)),
         in_specs=[FAR] * 3,
         scratch=(
             pltpu.VMEM(pert_factor.shape, bf16),
@@ -285,7 +298,9 @@
         ),
     )
     partial = lax.all_to_all(partial, "pert", 0, 0)
-    gathered = lax.all_to_all(summed_copies(partial, "pert_sum"), "pert", 0, 0)
+    gathered = lax.all_to_all(
+        summed_copies(functools.partial(narrow_sum_and_copy, part), partial, "pert_sum"), "pert", 0, 0
+    )
 
     context_factor = near(context_factor)
     chips = n_gene // 2
@@ -316,7 +331,7 @@
     partial = call(add, "core_sum", (near(mine), near(other)), message)
     partial = lax.all_to_all(partial, "gene", 0, 0, axis_index_groups=groups)
     mine = lax.all_to_all(
-        summed_copies(partial, "gene_sum"), "gene", 0, 0, axis_index_groups=groups
+        summed_copies(sum_and_copy, partial, "gene_sum"), "gene", 0, 0, axis_index_groups=groups
     )
     other = lax.ppermute(mine, "gene", swap)
     mine = near(mine)

time: 94.4 us -> 88.9 us (0.942)
  blocking collectives: 69.4 us -> 64.2 us
    all_to_all x1, blocking collectives: 20.6 us -> 17.8 us  [shards(): partial = lax.all_to_all(partial, 'pert', 0, 0)]
    all_to_all x2, blocking collectives: 25.1 us -> 23 us  [the longest x1 11.5 us: shards(): lax.all_to_all(summed_copies(sum_and_copy, partial, 'gene_sum'), 'gene',...]
  transfers between devices with their start and end apart: 2 -> 2, of which waited for: 0 -> 0; matrix products, arithmetic and copies ran while one was open for 0% -> 0% of each run, Pallas kernels for 5% -> 6%
where the time goes in v6:
time: 88.9 us; the launch traced here: 88.6 us
  blocking collectives  64.2 us (72%)
  Pallas kernels  17.5 us (20%)
  starting transfers between devices  6.15 us (7%)
    all_to_all x1, blocking collectives, shards(): partial = lax.all_to_all(partial, 'pert', 0, 0)  17.8 us
    pallas_call x9, Pallas kernels, call(): pl.pallas_call(body, in_specs=in_specs or [VMEM] * len(inputs), out_specs...  17.5 us
    all_to_all x1, blocking collectives, shards(): partial = lax.all_to_all(partial, 'gene', 0, 0, axis_index_groups=groups)  14.6 us
    all_to_all x1, blocking collectives, shards(): lax.all_to_all(summed_copies(sum_and_copy, partial, 'gene_sum'), 'gene',...  11.5 us
    all_to_all x1, blocking collectives, shards(): lax.all_to_all(summed_copies(functools.partial(narrow_sum_and_copy, part)...  11.4 us
    all_to_all x1, blocking collectives, shards(): squares = lax.all_to_all(squares, 'pert', 0, 0)  8.92 us
    ppermute x1, starting transfers between devices, shards(): other = lax.ppermute(other, 'gene', swap)  3.26 us
    ppermute x1, starting transfers between devices, shards(): other = lax.ppermute(mine, 'gene', swap)  2.89 us
  transfers between devices with their start and end apart: 2, of which 0 were waited for; matrix products, arithmetic and copies ran while one was open for 0% of the time, Pallas kernels for 6%

profile of v6, /device:TPU:1, one launch (start us, length us, event | category | flops | bytes accessed | tf_op | source)
XLA Modules:
  0.0 88.6 jit_solution(15625540530950286630)
XLA Ops:
  0.6 0.0 copy-start
  0.6 5.3 %gene_products.1 = (bf16[8,96,128]{2,1,0:T(8,128)(2,1)S(1)}, bf16[8192,512]{1,0:T(8,128)(2,1)S(1)}) custom-call(bf16[8192,512]{1,0:T(8,128)(2,1)} %bitcast.1, bf16[1024,128]{1,0:T(8,128)(2,1)} %factor_hbm.1, bf16[8,128]{1,0:T(8,128)(2,1)} %context_ref.5), custom_call_target="tpu_custom_call" | custom-call | tf_op jit(solution)/shard_map/gene_products/pallas_call | solution.py:260
  6.0 17.8 %all_to_all.25.in_ref = bf16[8,96,128]{2,1,0:T(8,128)(2,1)S(1)} all-to-all(bf16[8,96,128]{2,1,0:T(8,128)(2,1)S(1)} %get-tuple-element.12), channel_id=1, replica_groups=mesh['pert'=8,'gene'=32] {'pert'}, dimensions={0} | all-to-all | bytes 393216 | tf_op jit(solution)/shard_map/all_to_all | solution.py:300
  23.8 11.4 %all_to_all.26.held_ref = bf16[8,96,128]{2,1,0:T(8,128)(2,1)S(1)} all-to-all(bf16[8,96,128]{2,1,0:T(8,128)(2,1)S(1)} %pert_sum.1), channel_id=1, replica_groups=mesh['pert'=8,'gene'=32] {'pert'}, dimensions={0} | all-to-all | bytes 393216 | tf_op jit(solution)/shard_map/all_to_all | solution.py:301
  35.2 0.0 copy-done
  35.2 5.8 %gene_solve.1 = (f32[16,40,128]{2,1,0:T(8,128)S(1)}, f32[512,128]{1,0:T(8,128)S(1)}, bf16[512,256]{1,0:T(8,128)(2,1)S(1)}, f32[128,128]{1,0:T(8,128)S(1)}) custom-call(bf16[8,96,128]{2,1,0:T(8,128)(2,1)S(1)} %all_to_all.26.held_ref, bf16[8,128]{1,0:T(8,128)(2,1)S(1)} %copy-done, bf16[8192,512]{1,0:T(8,128)(2,1)S(1)} %get-tuple-element.13.tensor_ref), custom_call_target="tpu_custom_call" | custom-call | tf_op jit(solution)/shard_map/gene_solve/pallas_call | solution.py:260
  41.1 3.3 %collective-permute-start = (f32[16,40,128]{2,1,0:T(8,128)S(1)}, f32[16,40,128]{2,1,0:T(8,128)S(1)}, u32[]{:S(2)}, u32[]{:S(2)}) collective-permute-start(f32[16,40,128]{2,1,0:T(8,128)S(1)} %get-tuple-element.16), channel_id=1, source_target_pairs={{0,1},{1,0},{2,3},{3,2},{4,5},{5,4},{6,7},{7,6},{8,9},{9,8},{10,11... | collective-permute-start | bytes 983048 | tf_op jit(solution)/shard_map/ppermute | solution.py:324
  44.4 1.3 %pert_products.1.a_ref = f32[16,40,128]{2,1,0:T(8,128)S(1)} custom-call(bf16[512,256]{1,0:T(8,128)(2,1)S(1)} %get-tuple-element.14.weights_ref, bf16[8,128]{1,0:T(8,128)(2,1)S(1)} %copy-done, bf16[8192,512]{1,0:T(8,128)(2,1)S(1)} %get-tuple-element.13.tensor_ref, f32[128,128]{1,0:T(8,128)S(1)} %get-tuple-element.15.gram_ref), custom_call_target="tpu_custom_call" | custom-call | tf_op jit(solution)/shard_map/pert_products/pallas_call | solution.py:260
  45.7 0.0 collective-permute-done.b_ref
  45.7 14.6 %all_to_all.27.in_ref = f32[16,40,128]{2,1,0:T(8,128)S(1)} all-to-all(f32[16,40,128]{2,1,0:T(8,128)S(1)} %core_sum.1), channel_id=1, replica_groups={{0,2,4,6,8,10,12,14,16,18,20,22,24,26,28,30},{1,3,5,7,9,11,13,15,17,19,..., dimensions={0} | all-to-all | bytes 655360 | tf_op jit(solution)/shard_map/all_to_all | solution.py:332
  60.3 11.5 %all_to_all.28.mine_ref = f32[16,40,128]{2,1,0:T(8,128)S(1)} all-to-all(f32[16,40,128]{2,1,0:T(8,128)S(1)} %gene_sum.1), channel_id=1, replica_groups={{0,2,4,6,8,10,12,14,16,18,20,22,24,26,28,30},{1,3,5,7,9,11,13,15,17,19,..., dimensions={0} | all-to-all | bytes 655360 | tf_op jit(solution)/shard_map/all_to_all | solution.py:333
  71.8 2.9 %collective-permute-start.1 = (f32[16,40,128]{2,1,0:T(8,128)S(1)}, f32[16,40,128]{2,1,0:T(8,128)S(1)}, u32[]{:S(2)}, u32[]{:S(2)}) collective-permute-start(f32[16,40,128]{2,1,0:T(8,128)S(1)} %all_to_all.28.mine_ref), channel_id=1, source_target_pairs={{0,1},{1,0},{2,3},{3,2},{4,5},{5,4},{6,7},{7,6},{8,9},{9,8},{10,11... | collective-permute-start | bytes 983048 | tf_op jit(solution)/shard_map/ppermute | solution.py:336
  74.7 3.6 %pert_inverse.1 = (f32[128,128]{1,0:T(8,128)S(1)}, f32[1,128]{1,0:T(1,128)S(1)}) custom-call(f32[16,40,128]{2,1,0:T(8,128)S(1)} %all_to_all.28.mine_ref, bf16[8,128]{1,0:T(8,128)(2,1)S(1)} %copy-done), custom_call_target="tpu_custom_call" | custom-call | tf_op jit(solution)/shard_map/pert_inverse/pallas_call | solution.py:260
  78.3 0.0 collective-permute-done.1.other_ref
  78.3 0.6 pert_solve.1
  78.9 8.9 %all_to_all.29.held_ref = f32[8,1,128]{2,1,0:T(1,128)S(1)} all-to-all(f32[8,1,128]{2,1,0:T(1,128)S(1)} %get-tuple-element.18), channel_id=1, replica_groups=mesh['pert'=8,'gene'=32] {'pert'}, dimensions={0} | all-to-all | bytes 8192 | tf_op jit(solution)/shard_map/all_to_all | solution.py:350
  87.9 0.8 scale.1
  (3 shorter events, 0.1 us)
Async XLA Ops:
  0.6 34.6 %copy-start = (bf16[8,128]{1,0:T(8,128)(2,1)S(1)}, bf16[8,128]{1,0:T(8,128)(2,1)}, u32[]{:S(2)}) copy-start(bf16[8,128]{1,0:T(8,128)(2,1)} %context_ref.5) | copy-start | bytes 6148
  41.1 4.6 %collective-permute-start = (f32[16,40,128]{2,1,0:T(8,128)S(1)}, f32[16,40,128]{2,1,0:T(8,128)S(1)}, u32[]{:S(2)}, u32[]{:S(2)}) collective-permute-start(f32[16,40,128]{2,1,0:T(8,128)S(1)} %get-tuple-element.16), channel_id=1, source_target_pairs={{0,1},{1,0},{2,3},{3,2},{4,5},{5,4},{6,7},{7,6},{8,9},{9,8},{10,11... | collective-permute-start | bytes 983048 | tf_op jit(solution)/shard_map/ppermute | solution.py:324
  71.8 6.5 %collective-permute-start.1 = (f32[16,40,128]{2,1,0:T(8,128)S(1)}, f32[16,40,128]{2,1,0:T(8,128)S(1)}, u32[]{:S(2)}, u32[]{:S(2)}) collective-permute-start(f32[16,40,128]{2,1,0:T(8,128)S(1)} %all_to_all.28.mine_ref), channel_id=1, source_target_pairs={{0,1},{1,0},{2,3},{3,2},{4,5},{5,4},{6,7},{7,6},{8,9},{9,8},{10,11... | collective-permute-start | bytes 983048 | tf_op jit(solution)/shard_map/ppermute | solution.py:336

commit v7 on v6

--- a/solution.py
+++ b/solution.py
@@ -132,12 +132,6 @@
         out_ref[q, :genes, :] = summed[q * genes : (q + 1) * genes, :]
 
 
-def sum_and_copy(in_ref, out_ref):
-    total = jnp.sum(in_ref[...], axis=0)
-    for q in range(out_ref.shape[0]):
-        out_ref[q] = total
-
-
 def narrow_sum_and_copy(part, in_ref, out_ref):
     total = jnp.sum(in_ref[...].astype(f32), axis=0)
     genes = total.shape[0] - 2 * part
@@ -147,34 +141,11 @@
         out_ref[q] = total
 
 
-def add(a_ref, b_ref, out_ref):
-    out_ref[...] = a_ref[...] + b_ref[...]
-
-
 def half_index():
     return lax.rem(lax.axis_index("gene"), 2)
 
 
-def contract(blocks, core, tensor_ref, weights, context, gram_ref, out_ref):
-    rank = gram_ref.shape[0]
-    contexts = context.shape[0]
-    context32 = context.astype(f32)
-    half = tensor_ref.shape[0] // 2
-    height = half // blocks
-    per_block = height // contexts
-    targets = out_ref.shape[0]
-    perts = half // contexts // targets
-    out_ref[:, perts:, :] = gram_ref[...].reshape(targets, rank // targets, rank)
-    for b in range(blocks):
-        start = pl.multiple_of(core * half + b * height, height)
-        product = dot(tensor_ref[pl.ds(start, height), :], weights)
-        wide = (product[:, :rank] + product[:, rank:]).reshape(per_block, contexts, rank)
-        total = jnp.sum(wide * context32[None], axis=1)
-        n = per_block // perts
-        out_ref[pl.ds(b * n, n), :perts, :] = total.reshape(n, perts, rank)
-
-
-def gene_solve(blocks, held_ref, context_ref, tensor_ref, other_ref, solved_ref, weights_ref, gram_ref):
+def gene_solve(blocks, held_ref, context_ref, tensor_ref, out_ref, solved_ref):
     chunks, tall, rank = held_ref.shape
     part = rank // chunks
     genes = tall - 2 * part
@@ -186,33 +157,52 @@
     solved = dot(mttkrp, inv, precision=HIGHEST)
     solved_ref[...] = solved
     weights = jnp.concatenate(split(solved), axis=1)
-    weights_ref[...] = weights
     product = dot(weights, weights, ((0,), (0,)))
     product = product[:, :rank] + product[:, rank:]
-    gram_ref[...] = product[:rank, :] + product[rank:, :]
-    contract(blocks, 1 - half_index(), tensor_ref, weights, context, gram_ref, other_ref)
-
-
-def pert_products(blocks, weights_ref, context_ref, tensor_ref, gram_ref, mine_ref):
-    contract(
-        blocks, half_index(), tensor_ref, weights_ref[...], context_ref[...], gram_ref, mine_ref
-    )
-
-
-def pert_inverse(gene_count, mine_ref, context_ref, inv_ref, rate_ref):
+    high, low = (x.astype(f32) for x in split(product[:rank, :] + product[rank:, :]))
+    targets = out_ref.shape[0]
+    share = rank // targets
+    contexts = context.shape[0]
+    perts = tensor_ref.shape[0] // contexts // targets
+    for q in range(targets):
+        rows = slice(q * share, (q + 1) * share)
+        out_ref[q, perts:, :] = jnp.concatenate([high[rows, :], low[rows, :]], axis=0).astype(bf16)
+    context32 = context.astype(f32)
+    height = tensor_ref.shape[0] // blocks
+    per_block = height // contexts
+    chips = targets // 2
+    for b in range(blocks):
+        product = dot(tensor_ref[pl.ds(b * height, height), :], weights)
+        wide = (product[:, :rank] + product[:, rank:]).reshape(per_block, contexts, rank)
+        total = jnp.sum(wide * context32[None], axis=1).astype(bf16)
+        for n in range(per_block // perts):
+            core, chip = divmod(b * per_block // perts + n, chips)
+            out_ref[2 * chip + core, :perts, :] = total[n * perts : (n + 1) * perts, :]
+
+
+def gene_sum(share, in_ref, out_ref):
+    total = jnp.sum(in_ref[...].astype(f32), axis=0)
+    perts = total.shape[0] - 2 * share
+    gram = total[perts : perts + share, :] + total[perts + share :, :]
+    none = jnp.zeros_like(gram)
+    gram = jnp.where(
+        half_index() == 0,
+        jnp.concatenate([gram, none], axis=0),
+        jnp.concatenate([none, gram], axis=0),
+    )
+    total = jnp.concatenate([total[:perts, :], gram], axis=0)
+    for q in range(out_ref.shape[0]):
+        out_ref[q] = total
+
+
+def pert_solve(gene_count, mine_ref, other_ref, context_ref, out_ref, squares_ref, rate_ref):
     chunks, tall, rank = mine_ref.shape
     perts = tall - rank // chunks
-    gram_s = mine_ref[:, perts:, :].reshape(rank, rank)
+    gram_s = (mine_ref[:, perts:, :] + other_ref[:, perts:, :]).reshape(rank, rank)
     diag_row, _ = diagonal(gram_s, eye(rank))
     scale_c = jnp.sqrt(diag_row / gene_count + epsilon)
     rate_ref[...] = 1.0 / scale_c
-    inv_ref[...] = inverse(gram_s * gram_of(context_ref[...])) * scale_c
-
-
-def pert_solve(mine_ref, other_ref, inv_ref, out_ref, squares_ref):
-    chunks, tall, rank = mine_ref.shape
-    perts = tall - rank // chunks
-    inv = inv_ref[...]
+    inv = inverse(gram_s * gram_of(context_ref[...])) * scale_c
     mine = half_index()
     half = out_ref.shape[0] // 2
     squares = []
@@ -268,10 +258,6 @@
     )(*inputs)
 
 
-def summed_copies(body, x, name):
-    return call(body, name, (near(x),), pltpu.VMEM(x.shape, x.dtype))
-
-
 def shards(tensor, pert_factor, context_factor):
     rows_i, contexts, rows_j = tensor.shape
     rank = pert_factor.shape[1]
@@ -298,54 +284,46 @@
         ),
     )
     partial = lax.all_to_all(partial, "pert", 0, 0)
-    gathered = lax.all_to_all(
-        summed_copies(functools.partial(narrow_sum_and_copy, part), partial, "pert_sum"), "pert", 0, 0
-    )
+    gathered = call(
+        functools.partial(narrow_sum_and_copy, part),
+        "pert_sum",
+        (near(partial),),
+        pltpu.VMEM(partial.shape, bf16),
+    )
+    gathered = lax.all_to_all(gathered, "pert", 0, 0)
 
     context_factor = near(context_factor)
     chips = n_gene // 2
     perts = rows_i // n_gene
-    message = pltpu.VMEM((chips, perts + rank // chips, rank), f32)
-    square = pltpu.VMEM((rank, rank), f32)
-    kept = near(kept)
-    other, solved_c, weights, gram_s = call(
-        functools.partial(gene_solve, 4),
+    share = rank // n_gene
+    partial, solved_c = call(
+        functools.partial(gene_solve, 8),
         "gene_solve",
-        (near(gathered), context_factor, kept),
+        (near(gathered), context_factor, near(kept)),
         (
-            message,
+            pltpu.VMEM((n_gene, perts + 2 * share, rank), bf16),
             pltpu.VMEM((rows_j, rank), f32),
-            pltpu.VMEM((rows_j, 2 * rank), bf16),
-            square,
         ),
     )
-    swap = [(i, i ^ 1) for i in range(n_gene)]
+    partial = lax.all_to_all(partial, "gene", 0, 0)
+    summed = call(
+        functools.partial(gene_sum, share),
+        "gene_sum",
+        (near(partial),),
+        pltpu.VMEM((chips, perts + 2 * share, rank), f32),
+    )
     groups = [[2 * i + core for i in range(chips)] for core in range(2)]
-    other = lax.ppermute(other, "gene", swap)
-    mine = call(
-        functools.partial(pert_products, 4),
-        "pert_products",
-        (near(weights), context_factor, kept, near(gram_s)),
-        message,
-    )
-    partial = call(add, "core_sum", (near(mine), near(other)), message)
-    partial = lax.all_to_all(partial, "gene", 0, 0, axis_index_groups=groups)
-    mine = lax.all_to_all(
-        summed_copies(sum_and_copy, partial, "gene_sum"), "gene", 0, 0, axis_index_groups=groups
-    )
-    other = lax.ppermute(mine, "gene", swap)
-    mine = near(mine)
-    inv, rate = call(
-        functools.partial(pert_inverse, rows_j * n_gene),
-        "pert_inverse",
-        (mine, context_factor),
-        (square, pltpu.VMEM((1, rank), f32)),
-    )
-    solved_a, squares = call(
-        pert_solve,
+    mine = lax.all_to_all(summed, "gene", 0, 0, axis_index_groups=groups)
+    other = lax.ppermute(mine, "gene", [(i, i ^ 1) for i in range(n_gene)])
+    solved_a, squares, rate = call(
+        functools.partial(pert_solve, rows_j * n_gene),
         "pert_solve",
-        (mine, near(other), near(inv)),
-        (pltpu.VMEM((rows_i, rank), f32), pltpu.VMEM((n_pert, 1, rank), f32)),
+        (near(mine), near(other), context_factor),
+        (
+            pltpu.VMEM((rows_i, rank), f32),
+            pltpu.VMEM((n_pert, 1, rank), f32),
+            pltpu.VMEM((1, rank), f32),
+        ),
     )
     squares = lax.all_to_all(squares, "pert", 0, 0)
     outputs = (

time: 88.9 us -> 90.3 us (1.016)
  blocking collectives: 64.2 us -> 68.6 us
  starting transfers between devices: 6.15 us -> 2.11 us
  waiting for transfers between devices: 0.01 us -> 1.26 us
    all_to_all x3, blocking collectives: 37.5 us -> 41.9 us  [the longest x1 19.7 us: shards(): partial = lax.all_to_all(partial, 'gene', 0, 0)]
    ppermute x2 -> x1, starting transfers between devices: 6.15 us -> 2.11 us  [shards(): other = lax.ppermute(mine, 'gene', [(i, i ^ 1) for i in range(n_gene)])]
    ppermute x2 -> x1, waiting for transfers between devices: 0.01 us -> 1.26 us  [shards(): other = lax.ppermute(mine, 'gene', [(i, i ^ 1) for i in range(n_gene)])]
    pallas_call x9 -> x6, Pallas kernels: 17.5 us -> 17.4 us  [call(): pl.pallas_call(body, in_specs=in_specs or [VMEM] * len(inputs), out_specs...]
  transfers between devices with their start and end apart: 2 -> 1, of which waited for: 0 -> 1; matrix products, arithmetic and copies ran while one was open for 0% -> 0% of each run, Pallas kernels for 6% -> 0%
where the time goes in v7:
time: 90.3 us; the launch traced here: 90 us
  blocking collectives  68.6 us (76%)
  Pallas kernels  17.4 us (19%)
  starting transfers between devices  2.11 us (2%)
  waiting for transfers between devices  1.26 us (1%)
    all_to_all x1, blocking collectives, shards(): partial = lax.all_to_all(partial, 'gene', 0, 0)  19.7 us
    all_to_all x1, blocking collectives, shards(): partial = lax.all_to_all(partial, 'pert', 0, 0)  17.8 us
    pallas_call x6, Pallas kernels, call(): pl.pallas_call(body, in_specs=in_specs or [VMEM] * len(inputs), out_specs...  17.4 us
    all_to_all x1, blocking collectives, shards(): gathered = lax.all_to_all(gathered, 'pert', 0, 0)  11.4 us
    all_to_all x1, blocking collectives, shards(): mine = lax.all_to_all(summed, 'gene', 0, 0, axis_index_groups=groups)  10.8 us
    all_to_all x1, blocking collectives, shards(): squares = lax.all_to_all(squares, 'pert', 0, 0)  8.92 us
    ppermute x1, starting transfers between devices, shards(): other = lax.ppermute(mine, 'gene', [(i, i ^ 1) for i in range(n_gene)])  2.11 us
  transfers between devices with their start and end apart: 1, of which 1 were waited for; matrix products, arithmetic and copies ran while one was open for 0% of the time, Pallas kernels for 0%

profile of v7, /device:TPU:1, one launch (start us, length us, event | category | flops | bytes accessed | tf_op | source)
XLA Modules:
  0.0 90.0 jit_solution(16721796450899733358)
XLA Ops:
  0.6 0.0 copy-start
  0.6 5.3 %gene_products.1 = (bf16[8,96,128]{2,1,0:T(8,128)(2,1)S(1)}, bf16[8192,512]{1,0:T(8,128)(2,1)S(1)}) custom-call(bf16[8192,512]{1,0:T(8,128)(2,1)} %bitcast.1, bf16[1024,128]{1,0:T(8,128)(2,1)} %factor_hbm.1, bf16[8,128]{1,0:T(8,128)(2,1)} %context_ref.3), custom_call_target="tpu_custom_call" | custom-call | tf_op jit(solution)/shard_map/gene_products/pallas_call | solution.py:250
  6.0 17.8 %all_to_all.25.in_ref = bf16[8,96,128]{2,1,0:T(8,128)(2,1)S(1)} all-to-all(bf16[8,96,128]{2,1,0:T(8,128)(2,1)S(1)} %get-tuple-element.9), channel_id=1, replica_groups=mesh['pert'=8,'gene'=32] {'pert'}, dimensions={0} | all-to-all | bytes 393216 | tf_op jit(solution)/shard_map/all_to_all | solution.py:286
  23.8 11.4 %all_to_all.26.held_ref = bf16[8,96,128]{2,1,0:T(8,128)(2,1)S(1)} all-to-all(bf16[8,96,128]{2,1,0:T(8,128)(2,1)S(1)} %pert_sum.1), channel_id=1, replica_groups=mesh['pert'=8,'gene'=32] {'pert'}, dimensions={0} | all-to-all | bytes 393216 | tf_op jit(solution)/shard_map/all_to_all | solution.py:293
  35.2 0.0 copy-done
  35.2 7.0 %gene_solve.1 = (bf16[32,40,128]{2,1,0:T(8,128)(2,1)S(1)}, f32[512,128]{1,0:T(8,128)S(1)}) custom-call(bf16[8,96,128]{2,1,0:T(8,128)(2,1)S(1)} %all_to_all.26.held_ref, bf16[8,128]{1,0:T(8,128)(2,1)S(1)} %copy-done, bf16[8192,512]{1,0:T(8,128)(2,1)S(1)} %get-tuple-element.10.tensor_ref), custom_call_target="tpu_custom_call" | custom-call | tf_op jit(solution)/shard_map/gene_solve/pallas_call | solution.py:250
  42.2 19.7 %all_to_all.27.in_ref = bf16[32,40,128]{2,1,0:T(8,128)(2,1)S(1)} all-to-all(bf16[32,40,128]{2,1,0:T(8,128)(2,1)S(1)} %get-tuple-element.11), channel_id=1, replica_groups=mesh['pert'=8,'gene'=32] {'gene'}, dimensions={0} | all-to-all | bytes 655360 | tf_op jit(solution)/shard_map/all_to_all | solution.py:308
  61.9 0.1 gene_sum.1
  62.0 10.8 %all_to_all.28.mine_ref = f32[16,40,128]{2,1,0:T(8,128)S(1)} all-to-all(f32[16,40,128]{2,1,0:T(8,128)S(1)} %gene_sum.1), channel_id=1, replica_groups={{0,2,4,6,8,10,12,14,16,18,20,22,24,26,28,30},{1,3,5,7,9,11,13,15,17,19,..., dimensions={0} | all-to-all | bytes 655360 | tf_op jit(solution)/shard_map/all_to_all | solution.py:316
  72.7 2.1 %collective-permute-start = (f32[16,40,128]{2,1,0:T(8,128)S(1)}, f32[16,40,128]{2,1,0:T(8,128)S(1)}, u32[]{:S(2)}, u32[]{:S(2)}) collective-permute-start(f32[16,40,128]{2,1,0:T(8,128)S(1)} %all_to_all.28.mine_ref), channel_id=1, source_target_pairs={{0,1},{1,0},{2,3},{3,2},{4,5},{5,4},{6,7},{7,6},{8,9},{9,8},{10,11... | collective-permute-start | bytes 983048 | tf_op jit(solution)/shard_map/ppermute | solution.py:317
  74.8 1.3 %collective-permute-done.other_ref = f32[16,40,128]{2,1,0:T(8,128)S(1)} collective-permute-done((f32[16,40,128]{2,1,0:T(8,128)S(1)}, f32[16,40,128]{2,1,0:T(8,128)S(1)}, u32[]{:S(2)}, u32[]{:S(2)}) %collective-permute-start) | collective-permute-done | bytes 327712 | tf_op jit(solution)/shard_map/ppermute | solution.py:317
  76.1 4.2 %pert_solve.1 = (f32[1024,128]{1,0:T(8,128)S(1)}, f32[8,1,128]{2,1,0:T(1,128)S(1)}, f32[1,128]{1,0:T(1,128)S(1)}) custom-call(f32[16,40,128]{2,1,0:T(8,128)S(1)} %all_to_all.28.mine_ref, f32[16,40,128]{2,1,0:T(8,128)S(1)} %collective-permute-done.other_ref, bf16[8,128]{1,0:T(8,128)(2,1)S(1)} %copy-done), custom_call_target="tpu_custom_call" | custom-call | tf_op jit(solution)/shard_map/pert_solve/pallas_call | solution.py:250
  80.3 8.9 %all_to_all.29.held_ref = f32[8,1,128]{2,1,0:T(1,128)S(1)} all-to-all(f32[8,1,128]{2,1,0:T(1,128)S(1)} %get-tuple-element.12), channel_id=1, replica_groups=mesh['pert'=8,'gene'=32] {'pert'}, dimensions={0} | all-to-all | bytes 8192 | tf_op jit(solution)/shard_map/all_to_all | solution.py:328
  89.2 0.8 scale.1
  (1 shorter events, 0.0 us)
Async XLA Ops:
  0.6 34.6 %copy-start = (bf16[8,128]{1,0:T(8,128)(2,1)S(1)}, bf16[8,128]{1,0:T(8,128)(2,1)}, u32[]{:S(2)}) copy-start(bf16[8,128]{1,0:T(8,128)(2,1)} %context_ref.3) | copy-start | bytes 6148
  72.7 3.4 %collective-permute-start = (f32[16,40,128]{2,1,0:T(8,128)S(1)}, f32[16,40,128]{2,1,0:T(8,128)S(1)}, u32[]{:S(2)}, u32[]{:S(2)}) collective-permute-start(f32[16,40,128]{2,1,0:T(8,128)S(1)} %all_to_all.28.mine_ref), channel_id=1, source_target_pairs={{0,1},{1,0},{2,3},{3,2},{4,5},{5,4},{6,7},{7,6},{8,9},{9,8},{10,11... | collective-permute-start | bytes 983048 | tf_op jit(solution)/shard_map/ppermute | solution.py:317

commit v8 on v6

--- a/solution.py
+++ b/solution.py
@@ -132,12 +132,6 @@
         out_ref[q, :genes, :] = summed[q * genes : (q + 1) * genes, :]
 
 
-def sum_and_copy(in_ref, out_ref):
-    total = jnp.sum(in_ref[...], axis=0)
-    for q in range(out_ref.shape[0]):
-        out_ref[q] = total
-
-
 def narrow_sum_and_copy(part, in_ref, out_ref):
     total = jnp.sum(in_ref[...].astype(f32), axis=0)
     genes = total.shape[0] - 2 * part
@@ -147,8 +141,22 @@
         out_ref[q] = total
 
 
-def add(a_ref, b_ref, out_ref):
-    out_ref[...] = a_ref[...] + b_ref[...]
+def core_sum(share, a_ref, b_ref, out_ref):
+    total = a_ref[...] + b_ref[...]
+    perts = total.shape[1] - share
+    high, low = split(total[:, perts:, :])
+    out_ref[:, :perts, :] = total[:, :perts, :].astype(bf16)
+    out_ref[:, perts : perts + share, :] = high
+    out_ref[:, perts + share :, :] = low
+
+
+def gene_sum(share, in_ref, out_ref):
+    total = jnp.sum(in_ref[...].astype(f32), axis=0)
+    perts = total.shape[0] - 2 * share
+    gram = total[perts : perts + share, :] + total[perts + share :, :]
+    total = jnp.concatenate([total[:perts, :], gram], axis=0)
+    for q in range(out_ref.shape[0]):
+        out_ref[q] = total
 
 
 def half_index():
@@ -268,10 +276,6 @@
     )(*inputs)
 
 
-def summed_copies(body, x, name):
-    return call(body, name, (near(x),), pltpu.VMEM(x.shape, x.dtype))
-
-
 def shards(tensor, pert_factor, context_factor):
     rows_i, contexts, rows_j = tensor.shape
     rank = pert_factor.shape[1]
@@ -298,9 +302,13 @@
         ),
     )
     partial = lax.all_to_all(partial, "pert", 0, 0)
-    gathered = lax.all_to_all(
-        summed_copies(functools.partial(narrow_sum_and_copy, part), partial, "pert_sum"), "pert", 0, 0
-    )
+    gathered = call(
+        functools.partial(narrow_sum_and_copy, part),
+        "pert_sum",
+        (near(partial),),
+        pltpu.VMEM(partial.shape, bf16),
+    )
+    gathered = lax.all_to_all(gathered, "pert", 0, 0)
 
     context_factor = near(context_factor)
     chips = n_gene // 2
@@ -328,11 +336,16 @@
         (near(weights), context_factor, kept, near(gram_s)),
         message,
     )
-    partial = call(add, "core_sum", (near(mine), near(other)), message)
+    share = rank // chips
+    partial = call(
+        functools.partial(core_sum, share),
+        "core_sum",
+        (near(mine), near(other)),
+        pltpu.VMEM((chips, perts + 2 * share, rank), bf16),
+    )
     partial = lax.all_to_all(partial, "gene", 0, 0, axis_index_groups=groups)
-    mine = lax.all_to_all(
-        summed_copies(sum_and_copy, partial, "gene_sum"), "gene", 0, 0, axis_index_groups=groups
-    )
+    summed = call(functools.partial(gene_sum, share), "gene_sum", (near(partial),), message)
+    mine = lax.all_to_all(summed, "gene", 0, 0, axis_index_groups=groups)
     other = lax.ppermute(mine, "gene", swap)
     mine = near(mine)
     inv, rate = call(

time: 88.9 us -> 87.5 us (0.984)
  blocking collectives: 64.2 us -> 62.8 us
    all_to_all x1, blocking collectives: 14.6 us -> 13.6 us  [shards(): partial = lax.all_to_all(partial, 'gene', 0, 0, axis_index_groups=groups)]
where the time goes in v8:
time: 87.5 us; the launch traced here: 87.2 us
  blocking collectives  62.8 us (72%)
  Pallas kernels  17.5 us (20%)
  starting transfers between devices  6.15 us (7%)
    all_to_all x1, blocking collectives, shards(): partial = lax.all_to_all(partial, 'pert', 0, 0)  17.8 us
    pallas_call x9, Pallas kernels, call(): pl.pallas_call(body, in_specs=in_specs or [VMEM] * len(inputs), out_specs...  17.5 us
    all_to_all x1, blocking collectives, shards(): partial = lax.all_to_all(partial, 'gene', 0, 0, axis_index_groups=groups)  13.6 us
    all_to_all x1, blocking collectives, shards(): gathered = lax.all_to_all(gathered, 'pert', 0, 0)  11.4 us
    all_to_all x1, blocking collectives, shards(): mine = lax.all_to_all(summed, 'gene', 0, 0, axis_index_groups=groups)  11.1 us
    all_to_all x1, blocking collectives, shards(): squares = lax.all_to_all(squares, 'pert', 0, 0)  8.92 us
    ppermute x1, starting transfers between devices, shards(): other = lax.ppermute(other, 'gene', swap)  3.26 us
    ppermute x1, starting transfers between devices, shards(): other = lax.ppermute(mine, 'gene', swap)  2.88 us
  transfers between devices with their start and end apart: 2, of which 0 were waited for; matrix products, arithmetic and copies ran while one was open for 0% of the time, Pallas kernels for 6%

profile of v8, /device:TPU:1, one launch (start us, length us, event | category | flops | bytes accessed | tf_op | source)
XLA Modules:
  0.0 87.2 jit_solution(6292312965652202881)
XLA Ops:
  0.6 0.0 copy-start
  0.6 5.3 %gene_products.1 = (bf16[8,96,128]{2,1,0:T(8,128)(2,1)S(1)}, bf16[8192,512]{1,0:T(8,128)(2,1)S(1)}) custom-call(bf16[8192,512]{1,0:T(8,128)(2,1)} %bitcast.1, bf16[1024,128]{1,0:T(8,128)(2,1)} %factor_hbm.1, bf16[8,128]{1,0:T(8,128)(2,1)} %context_ref.5), custom_call_target="tpu_custom_call" | custom-call | tf_op jit(solution)/shard_map/gene_products/pallas_call | solution.py:268
  6.0 17.8 %all_to_all.25.in_ref = bf16[8,96,128]{2,1,0:T(8,128)(2,1)S(1)} all-to-all(bf16[8,96,128]{2,1,0:T(8,128)(2,1)S(1)} %get-tuple-element.12), channel_id=1, replica_groups=mesh['pert'=8,'gene'=32] {'pert'}, dimensions={0} | all-to-all | bytes 393216 | tf_op jit(solution)/shard_map/all_to_all | solution.py:304
  23.8 11.4 %all_to_all.26.held_ref = bf16[8,96,128]{2,1,0:T(8,128)(2,1)S(1)} all-to-all(bf16[8,96,128]{2,1,0:T(8,128)(2,1)S(1)} %pert_sum.1), channel_id=1, replica_groups=mesh['pert'=8,'gene'=32] {'pert'}, dimensions={0} | all-to-all | bytes 393216 | tf_op jit(solution)/shard_map/all_to_all | solution.py:311
  35.2 0.0 copy-done
  35.2 5.8 %gene_solve.1 = (f32[16,40,128]{2,1,0:T(8,128)S(1)}, f32[512,128]{1,0:T(8,128)S(1)}, bf16[512,256]{1,0:T(8,128)(2,1)S(1)}, f32[128,128]{1,0:T(8,128)S(1)}) custom-call(bf16[8,96,128]{2,1,0:T(8,128)(2,1)S(1)} %all_to_all.26.held_ref, bf16[8,128]{1,0:T(8,128)(2,1)S(1)} %copy-done, bf16[8192,512]{1,0:T(8,128)(2,1)S(1)} %get-tuple-element.13.tensor_ref), custom_call_target="tpu_custom_call" | custom-call | tf_op jit(solution)/shard_map/gene_solve/pallas_call | solution.py:268
  41.1 3.3 %collective-permute-start = (f32[16,40,128]{2,1,0:T(8,128)S(1)}, f32[16,40,128]{2,1,0:T(8,128)S(1)}, u32[]{:S(2)}, u32[]{:S(2)}) collective-permute-start(f32[16,40,128]{2,1,0:T(8,128)S(1)} %get-tuple-element.16), channel_id=1, source_target_pairs={{0,1},{1,0},{2,3},{3,2},{4,5},{5,4},{6,7},{7,6},{8,9},{9,8},{10,11... | collective-permute-start | bytes 983048 | tf_op jit(solution)/shard_map/ppermute | solution.py:332
  44.4 1.3 %pert_products.1.a_ref = f32[16,40,128]{2,1,0:T(8,128)S(1)} custom-call(bf16[512,256]{1,0:T(8,128)(2,1)S(1)} %get-tuple-element.14.weights_ref, bf16[8,128]{1,0:T(8,128)(2,1)S(1)} %copy-done, bf16[8192,512]{1,0:T(8,128)(2,1)S(1)} %get-tuple-element.13.tensor_ref, f32[128,128]{1,0:T(8,128)S(1)} %get-tuple-element.15.gram_ref), custom_call_target="tpu_custom_call" | custom-call | tf_op jit(solution)/shard_map/pert_products/pallas_call | solution.py:268
  45.7 0.0 collective-permute-done.b_ref
  45.7 13.6 %all_to_all.27.in_ref = bf16[16,48,128]{2,1,0:T(8,128)(2,1)S(1)} all-to-all(bf16[16,48,128]{2,1,0:T(8,128)(2,1)S(1)} %core_sum.1), channel_id=1, replica_groups={{0,2,4,6,8,10,12,14,16,18,20,22,24,26,28,30},{1,3,5,7,9,11,13,15,17,19,..., dimensions={0} | all-to-all | bytes 393216 | tf_op jit(solution)/shard_map/all_to_all | solution.py:346
  59.3 11.1 %all_to_all.28.mine_ref = f32[16,40,128]{2,1,0:T(8,128)S(1)} all-to-all(f32[16,40,128]{2,1,0:T(8,128)S(1)} %gene_sum.1), channel_id=1, replica_groups={{0,2,4,6,8,10,12,14,16,18,20,22,24,26,28,30},{1,3,5,7,9,11,13,15,17,19,..., dimensions={0} | all-to-all | bytes 655360 | tf_op jit(solution)/shard_map/all_to_all | solution.py:348
  70.4 2.9 %collective-permute-start.1 = (f32[16,40,128]{2,1,0:T(8,128)S(1)}, f32[16,40,128]{2,1,0:T(8,128)S(1)}, u32[]{:S(2)}, u32[]{:S(2)}) collective-permute-start(f32[16,40,128]{2,1,0:T(8,128)S(1)} %all_to_all.28.mine_ref), channel_id=1, source_target_pairs={{0,1},{1,0},{2,3},{3,2},{4,5},{5,4},{6,7},{7,6},{8,9},{9,8},{10,11... | collective-permute-start | bytes 983048 | tf_op jit(solution)/shard_map/ppermute | solution.py:349
  73.3 3.6 %pert_inverse.1 = (f32[128,128]{1,0:T(8,128)S(1)}, f32[1,128]{1,0:T(1,128)S(1)}) custom-call(f32[16,40,128]{2,1,0:T(8,128)S(1)} %all_to_all.28.mine_ref, bf16[8,128]{1,0:T(8,128)(2,1)S(1)} %copy-done), custom_call_target="tpu_custom_call" | custom-call | tf_op jit(solution)/shard_map/pert_inverse/pallas_call | solution.py:268
  76.9 0.0 collective-permute-done.1.other_ref
  76.9 0.6 pert_solve.1
  77.5 8.9 %all_to_all.29.held_ref = f32[8,1,128]{2,1,0:T(1,128)S(1)} all-to-all(f32[8,1,128]{2,1,0:T(1,128)S(1)} %get-tuple-element.18), channel_id=1, replica_groups=mesh['pert'=8,'gene'=32] {'pert'}, dimensions={0} | all-to-all | bytes 8192 | tf_op jit(solution)/shard_map/all_to_all | solution.py:363
  86.5 0.8 scale.1
  (3 shorter events, 0.1 us)
Async XLA Ops:
  0.6 34.6 %copy-start = (bf16[8,128]{1,0:T(8,128)(2,1)S(1)}, bf16[8,128]{1,0:T(8,128)(2,1)}, u32[]{:S(2)}) copy-start(bf16[8,128]{1,0:T(8,128)(2,1)} %context_ref.5) | copy-start | bytes 6148
  41.1 4.6 %collective-permute-start = (f32[16,40,128]{2,1,0:T(8,128)S(1)}, f32[16,40,128]{2,1,0:T(8,128)S(1)}, u32[]{:S(2)}, u32[]{:S(2)}) collective-permute-start(f32[16,40,128]{2,1,0:T(8,128)S(1)} %get-tuple-element.16), channel_id=1, source_target_pairs={{0,1},{1,0},{2,3},{3,2},{4,5},{5,4},{6,7},{7,6},{8,9},{9,8},{10,11... | collective-permute-start | bytes 983048 | tf_op jit(solution)/shard_map/ppermute | solution.py:332
  70.4 6.5 %collective-permute-start.1 = (f32[16,40,128]{2,1,0:T(8,128)S(1)}, f32[16,40,128]{2,1,0:T(8,128)S(1)}, u32[]{:S(2)}, u32[]{:S(2)}) collective-permute-start(f32[16,40,128]{2,1,0:T(8,128)S(1)} %all_to_all.28.mine_ref), channel_id=1, source_target_pairs={{0,1},{1,0},{2,3},{3,2},{4,5},{5,4},{6,7},{7,6},{8,9},{9,8},{10,11... | collective-permute-start | bytes 983048 | tf_op jit(solution)/shard_map/ppermute | solution.py:349

commit v9 on v8

--- a/solution.py
+++ b/solution.py
@@ -85,7 +85,6 @@
 def gene_products(
     blocks, tensor_ref, factor_hbm, context_hbm, out_ref, keep, factor_ref, context_ref, left, sems, small
 ):
-    depth = 3
     starts = [sum(blocks[:b]) for b in range(len(blocks))]
     copies = []
     for b, height in enumerate(blocks):
@@ -95,8 +94,8 @@
     second = pltpu.make_async_copy(context_hbm, context_ref, small.at[1])
     first.start()
     second.start()
-    for copy in copies[:depth]:
-        copy.start()
+    for copy in copies:
+        copy.start(priority=1)
     contexts, rank = context_ref.shape
     chunks, tall, _ = out_ref.shape
     part = rank // chunks
@@ -121,8 +120,6 @@
     total = None
     for b in range(len(blocks)):
         copies[b].wait()
-        if b + depth < len(blocks):
-            copies[b + depth].start()
         if b + 1 < len(blocks):
             build(b + 1)
         product = dot(left[b % 2, :, : blocks[b]], keep[pl.ds(starts[b], blocks[b]), :])
@@ -187,11 +184,14 @@
     part = rank // chunks
     genes = tall - 2 * part
     context = context_ref[...]
-    held = held_ref[...].astype(f32)
-    gram_a = (held[:, genes : genes + part, :] + held[:, genes + part :, :]).reshape(rank, rank)
-    mttkrp = held[:, :genes, :].reshape(chunks * genes, rank)
+    rows = held_ref[:, genes:, :].astype(f32)
+    gram_a = (rows[:, :part, :] + rows[:, part:, :]).reshape(rank, rank)
+    mttkrp = held_ref[:, :genes, :].reshape(chunks * genes, rank)
     inv = inverse(gram_a * gram_of(context))
-    solved = dot(mttkrp, inv, precision=HIGHEST)
+    high = inv.astype(bf16)
+    middle, low = split(inv - high.astype(f32))
+    product = dot(mttkrp, jnp.concatenate([high, middle], axis=1))
+    solved = product[:, :rank] + (product[:, rank:] + dot(mttkrp, low))
     solved_ref[...] = solved
     weights = jnp.concatenate(split(solved), axis=1)
     weights_ref[...] = weights

time: 87.5 us -> 86.3 us (0.986)
  Pallas kernels: 17.5 us -> 16.3 us
    pallas_call x9, Pallas kernels: 17.5 us -> 16.3 us  [call(): pl.pallas_call(body, in_specs=in_specs or [VMEM] * len(inputs), out_specs...]
where the time goes in v9:
time: 86.3 us; the launch traced here: 86 us
  blocking collectives  62.8 us (73%)
  Pallas kernels  16.3 us (19%)
  starting transfers between devices  6.14 us (7%)
    all_to_all x1, blocking collectives, shards(): partial = lax.all_to_all(partial, 'pert', 0, 0)  17.8 us
    pallas_call x9, Pallas kernels, call(): pl.pallas_call(body, in_specs=in_specs or [VMEM] * len(inputs), out_specs...  16.3 us
    all_to_all x1, blocking collectives, shards(): partial = lax.all_to_all(partial, 'gene', 0, 0, axis_index_groups=groups)  13.6 us
    all_to_all x1, blocking collectives, shards(): gathered = lax.all_to_all(gathered, 'pert', 0, 0)  11.4 us
    all_to_all x1, blocking collectives, shards(): mine = lax.all_to_all(summed, 'gene', 0, 0, axis_index_groups=groups)  11.1 us
    all_to_all x1, blocking collectives, shards(): squares = lax.all_to_all(squares, 'pert', 0, 0)  8.92 us
    ppermute x1, starting transfers between devices, shards(): other = lax.ppermute(other, 'gene', swap)  3.26 us
    ppermute x1, starting transfers between devices, shards(): other = lax.ppermute(mine, 'gene', swap)  2.88 us
  transfers between devices with their start and end apart: 2, of which 0 were waited for; matrix products, arithmetic and copies ran while one was open for 0% of the time, Pallas kernels for 6%

profile of v9, /device:TPU:1, one launch (start us, length us, event | category | flops | bytes accessed | tf_op | source)
XLA Modules:
  0.0 86.0 jit_solution(2350871481511717967)
XLA Ops:
  0.6 0.0 copy-start
  0.6 4.4 %gene_products.1 = (bf16[8,96,128]{2,1,0:T(8,128)(2,1)S(1)}, bf16[8192,512]{1,0:T(8,128)(2,1)S(1)}) custom-call(bf16[8192,512]{1,0:T(8,128)(2,1)} %bitcast.1, bf16[1024,128]{1,0:T(8,128)(2,1)} %factor_hbm.1, bf16[8,128]{1,0:T(8,128)(2,1)} %context_ref.5), custom_call_target="tpu_custom_call" | custom-call | tf_op jit(solution)/shard_map/gene_products/pallas_call | solution.py:268
  5.1 17.8 %all_to_all.25.in_ref = bf16[8,96,128]{2,1,0:T(8,128)(2,1)S(1)} all-to-all(bf16[8,96,128]{2,1,0:T(8,128)(2,1)S(1)} %get-tuple-element.12), channel_id=1, replica_groups=mesh['pert'=8,'gene'=32] {'pert'}, dimensions={0} | all-to-all | bytes 393216 | tf_op jit(solution)/shard_map/all_to_all | solution.py:304
  22.9 11.4 %all_to_all.26.held_ref = bf16[8,96,128]{2,1,0:T(8,128)(2,1)S(1)} all-to-all(bf16[8,96,128]{2,1,0:T(8,128)(2,1)S(1)} %pert_sum.1), channel_id=1, replica_groups=mesh['pert'=8,'gene'=32] {'pert'}, dimensions={0} | all-to-all | bytes 393216 | tf_op jit(solution)/shard_map/all_to_all | solution.py:311
  34.3 0.0 copy-done
  34.3 5.5 %gene_solve.1 = (f32[16,40,128]{2,1,0:T(8,128)S(1)}, f32[512,128]{1,0:T(8,128)S(1)}, bf16[512,256]{1,0:T(8,128)(2,1)S(1)}, f32[128,128]{1,0:T(8,128)S(1)}) custom-call(bf16[8,96,128]{2,1,0:T(8,128)(2,1)S(1)} %all_to_all.26.held_ref, bf16[8,128]{1,0:T(8,128)(2,1)S(1)} %copy-done, bf16[8192,512]{1,0:T(8,128)(2,1)S(1)} %get-tuple-element.13.tensor_ref), custom_call_target="tpu_custom_call" | custom-call | tf_op jit(solution)/shard_map/gene_solve/pallas_call | solution.py:268
  39.9 3.3 %collective-permute-start = (f32[16,40,128]{2,1,0:T(8,128)S(1)}, f32[16,40,128]{2,1,0:T(8,128)S(1)}, u32[]{:S(2)}, u32[]{:S(2)}) collective-permute-start(f32[16,40,128]{2,1,0:T(8,128)S(1)} %get-tuple-element.16), channel_id=1, source_target_pairs={{0,1},{1,0},{2,3},{3,2},{4,5},{5,4},{6,7},{7,6},{8,9},{9,8},{10,11... | collective-permute-start | bytes 983048 | tf_op jit(solution)/shard_map/ppermute | solution.py:332
  43.1 1.3 %pert_products.1.a_ref = f32[16,40,128]{2,1,0:T(8,128)S(1)} custom-call(bf16[512,256]{1,0:T(8,128)(2,1)S(1)} %get-tuple-element.14.weights_ref, bf16[8,128]{1,0:T(8,128)(2,1)S(1)} %copy-done, bf16[8192,512]{1,0:T(8,128)(2,1)S(1)} %get-tuple-element.13.tensor_ref, f32[128,128]{1,0:T(8,128)S(1)} %get-tuple-element.15.gram_ref), custom_call_target="tpu_custom_call" | custom-call | tf_op jit(solution)/shard_map/pert_products/pallas_call | solution.py:268
  44.4 0.0 collective-permute-done.b_ref
  44.5 13.6 %all_to_all.27.in_ref = bf16[16,48,128]{2,1,0:T(8,128)(2,1)S(1)} all-to-all(bf16[16,48,128]{2,1,0:T(8,128)(2,1)S(1)} %core_sum.1), channel_id=1, replica_groups={{0,2,4,6,8,10,12,14,16,18,20,22,24,26,28,30},{1,3,5,7,9,11,13,15,17,19,..., dimensions={0} | all-to-all | bytes 393216 | tf_op jit(solution)/shard_map/all_to_all | solution.py:346
  58.1 11.1 %all_to_all.28.mine_ref = f32[16,40,128]{2,1,0:T(8,128)S(1)} all-to-all(f32[16,40,128]{2,1,0:T(8,128)S(1)} %gene_sum.1), channel_id=1, replica_groups={{0,2,4,6,8,10,12,14,16,18,20,22,24,26,28,30},{1,3,5,7,9,11,13,15,17,19,..., dimensions={0} | all-to-all | bytes 655360 | tf_op jit(solution)/shard_map/all_to_all | solution.py:348
  69.2 2.9 %collective-permute-start.1 = (f32[16,40,128]{2,1,0:T(8,128)S(1)}, f32[16,40,128]{2,1,0:T(8,128)S(1)}, u32[]{:S(2)}, u32[]{:S(2)}) collective-permute-start(f32[16,40,128]{2,1,0:T(8,128)S(1)} %all_to_all.28.mine_ref), channel_id=1, source_target_pairs={{0,1},{1,0},{2,3},{3,2},{4,5},{5,4},{6,7},{7,6},{8,9},{9,8},{10,11... | collective-permute-start | bytes 983048 | tf_op jit(solution)/shard_map/ppermute | solution.py:349
  72.1 3.6 %pert_inverse.1 = (f32[128,128]{1,0:T(8,128)S(1)}, f32[1,128]{1,0:T(1,128)S(1)}) custom-call(f32[16,40,128]{2,1,0:T(8,128)S(1)} %all_to_all.28.mine_ref, bf16[8,128]{1,0:T(8,128)(2,1)S(1)} %copy-done), custom_call_target="tpu_custom_call" | custom-call | tf_op jit(solution)/shard_map/pert_inverse/pallas_call | solution.py:268
  75.7 0.0 collective-permute-done.1.other_ref
  75.7 0.6 pert_solve.1
  76.3 8.9 %all_to_all.29.held_ref = f32[8,1,128]{2,1,0:T(1,128)S(1)} all-to-all(f32[8,1,128]{2,1,0:T(1,128)S(1)} %get-tuple-element.18), channel_id=1, replica_groups=mesh['pert'=8,'gene'=32] {'pert'}, dimensions={0} | all-to-all | bytes 8192 | tf_op jit(solution)/shard_map/all_to_all | solution.py:363
  85.2 0.8 scale.1
  (3 shorter events, 0.1 us)
Async XLA Ops:
  0.6 33.7 %copy-start = (bf16[8,128]{1,0:T(8,128)(2,1)S(1)}, bf16[8,128]{1,0:T(8,128)(2,1)}, u32[]{:S(2)}) copy-start(bf16[8,128]{1,0:T(8,128)(2,1)} %context_ref.5) | copy-start | bytes 6148
  39.9 4.6 %collective-permute-start = (f32[16,40,128]{2,1,0:T(8,128)S(1)}, f32[16,40,128]{2,1,0:T(8,128)S(1)}, u32[]{:S(2)}, u32[]{:S(2)}) collective-permute-start(f32[16,40,128]{2,1,0:T(8,128)S(1)} %get-tuple-element.16), channel_id=1, source_target_pairs={{0,1},{1,0},{2,3},{3,2},{4,5},{5,4},{6,7},{7,6},{8,9},{9,8},{10,11... | collective-permute-start | bytes 983048 | tf_op jit(solution)/shard_map/ppermute | solution.py:332
  69.2 6.5 %collective-permute-start.1 = (f32[16,40,128]{2,1,0:T(8,128)S(1)}, f32[16,40,128]{2,1,0:T(8,128)S(1)}, u32[]{:S(2)}, u32[]{:S(2)}) collective-permute-start(f32[16,40,128]{2,1,0:T(8,128)S(1)} %all_to_all.28.mine_ref), channel_id=1, source_target_pairs={{0,1},{1,0},{2,3},{3,2},{4,5},{5,4},{6,7},{7,6},{8,9},{9,8},{10,11... | collective-permute-start | bytes 983048 | tf_op jit(solution)/shard_map/ppermute | solution.py:349

commit v10 on v9

--- a/solution.py
+++ b/solution.py
@@ -27,6 +27,21 @@
     right = jnp.concatenate(split(b), axis=1)
     product = dot(jnp.concatenate(split(a), axis=1), jnp.concatenate([right, right], axis=0))
     return product[:, :n] + product[:, n:]
+
+
+def split3(x):
+    first = x.astype(bf16)
+    return (first, *split(x - first.astype(f32)))
+
+
+def dot_split3(a, b):
+    n = b.shape[1]
+    a0, a1, a2 = split3(a)
+    b0, b1, b2 = split3(b)
+    right = jnp.concatenate([b0, b1], axis=1)
+    product = dot(jnp.concatenate([a0, a1], axis=1), jnp.concatenate([right, right], axis=0))
+    rest = dot(jnp.concatenate([a2, a0], axis=1), jnp.concatenate([b0, b2], axis=0))
+    return product[:, :n] + (product[:, n:] + rest)
 
 
 def eye(n):
@@ -226,7 +241,7 @@
     squares = []
     for core, held_ref in ((mine, mine_ref), (1 - mine, other_ref)):
         mttkrp = held_ref[:, :perts, :].reshape(half, rank)
-        solved = dot(mttkrp, inv, precision=HIGHEST)
+        solved = dot_split3(mttkrp, inv)
         out_ref[pl.ds(pl.multiple_of(core * half, half), half), :] = solved
         squares.append(jnp.sum(solved * solved, axis=0, keepdims=True))
     squares_ref[...] = jnp.broadcast_to((squares[0] + squares[1])[None], squares_ref.shape)
@@ -238,17 +253,11 @@
     first.start()
     squares = jnp.sum(held_ref[...], axis=0)
     rate = 1.0 / jnp.sqrt(squares / pert_count + epsilon)
-    half = pert.shape[0] // 2
-    copies = []
-    for h in range(2):
-        rows = pl.ds(h * half, half)
-        pert[rows, :] = (solved_a_ref[rows, :] * rate).astype(bf16)
-        copy = pltpu.make_async_copy(pert.at[rows, :], pert_ref.at[rows, :], sems.at[1 + h])
-        copy.start()
-        copies.append(copy)
+    pert[...] = (solved_a_ref[...] * rate).astype(bf16)
+    second = pltpu.make_async_copy(pert, pert_ref, sems.at[1])
+    second.start()
     first.wait()
-    for copy in copies:
-        copy.wait()
+    second.wait()
 
 
 VMEM = pl.BlockSpec(memory_space=pltpu.VMEM)
@@ -371,7 +380,7 @@
         (near(squares), near(solved_a), near(solved_c), near(rate)),
         outputs,
         out_spec=FAR,
-        scratch=[pltpu.VMEM(o.shape, bf16) for o in outputs] + [pltpu.SemaphoreType.DMA((3,))],
+        scratch=[pltpu.VMEM(o.shape, bf16) for o in outputs] + [pltpu.SemaphoreType.DMA((2,))],
     )
 
 

time: 86.3 us -> 86.3 us (level)
  no operation moved by 1% of the time
where the time goes in v10:
time: 86.3 us
  blocking collectives  62.8 us (73%)
  Pallas kernels  16.6 us (19%)
  starting transfers between devices  6.15 us (7%)
    all_to_all x1, blocking collectives, shards(): partial = lax.all_to_all(partial, 'pert', 0, 0)  17.8 us
    pallas_call x9, Pallas kernels, call(): pl.pallas_call(body, in_specs=in_specs or [VMEM] * len(inputs), out_specs...  16.6 us
    all_to_all x1, blocking collectives, shards(): partial = lax.all_to_all(partial, 'gene', 0, 0, axis_index_groups=groups)  13.6 us
    all_to_all x1, blocking collectives, shards(): gathered = lax.all_to_all(gathered, 'pert', 0, 0)  11.4 us
    all_to_all x1, blocking collectives, shards(): mine = lax.all_to_all(summed, 'gene', 0, 0, axis_index_groups=groups)  11.1 us
    all_to_all x1, blocking collectives, shards(): squares = lax.all_to_all(squares, 'pert', 0, 0)  8.92 us
    ppermute x1, starting transfers between devices, shards(): other = lax.ppermute(other, 'gene', swap)  3.27 us
    ppermute x1, starting transfers between devices, shards(): other = lax.ppermute(mine, 'gene', swap)  2.88 us
  transfers between devices with their start and end apart: 2, of which 0 were waited for; matrix products, arithmetic and copies ran while one was open for 0% of the time, Pallas kernels for 6%

profile of v10, /device:TPU:1, one launch (start us, length us, event | category | flops | bytes accessed | tf_op | source)
XLA Modules:
  0.0 86.3 jit_solution(10246851474917073172)
XLA Ops:
  0.6 0.0 copy-start
  0.6 4.4 %gene_products.1 = (bf16[8,96,128]{2,1,0:T(8,128)(2,1)S(1)}, bf16[8192,512]{1,0:T(8,128)(2,1)S(1)}) custom-call(bf16[8192,512]{1,0:T(8,128)(2,1)} %bitcast.1, bf16[1024,128]{1,0:T(8,128)(2,1)} %factor_hbm.1, bf16[8,128]{1,0:T(8,128)(2,1)} %context_ref.5), custom_call_target="tpu_custom_call" | custom-call | tf_op jit(solution)/shard_map/gene_products/pallas_call | solution.py:277
  5.1 17.8 %all_to_all.25.in_ref = bf16[8,96,128]{2,1,0:T(8,128)(2,1)S(1)} all-to-all(bf16[8,96,128]{2,1,0:T(8,128)(2,1)S(1)} %get-tuple-element.12), channel_id=1, replica_groups=mesh['pert'=8,'gene'=32] {'pert'}, dimensions={0} | all-to-all | bytes 393216 | tf_op jit(solution)/shard_map/all_to_all | solution.py:313
  22.9 11.4 %all_to_all.26.held_ref = bf16[8,96,128]{2,1,0:T(8,128)(2,1)S(1)} all-to-all(bf16[8,96,128]{2,1,0:T(8,128)(2,1)S(1)} %pert_sum.1), channel_id=1, replica_groups=mesh['pert'=8,'gene'=32] {'pert'}, dimensions={0} | all-to-all | bytes 393216 | tf_op jit(solution)/shard_map/all_to_all | solution.py:320
  34.3 0.0 copy-done
  34.3 5.7 %gene_solve.1 = (f32[16,40,128]{2,1,0:T(8,128)S(1)}, f32[512,128]{1,0:T(8,128)S(1)}, bf16[512,256]{1,0:T(8,128)(2,1)S(1)}, f32[128,128]{1,0:T(8,128)S(1)}) custom-call(bf16[8,96,128]{2,1,0:T(8,128)(2,1)S(1)} %all_to_all.26.held_ref, bf16[8,128]{1,0:T(8,128)(2,1)S(1)} %copy-done, bf16[8192,512]{1,0:T(8,128)(2,1)S(1)} %get-tuple-element.13.tensor_ref), custom_call_target="tpu_custom_call" | custom-call | tf_op jit(solution)/shard_map/gene_solve/pallas_call | solution.py:277
  40.1 3.3 %collective-permute-start = (f32[16,40,128]{2,1,0:T(8,128)S(1)}, f32[16,40,128]{2,1,0:T(8,128)S(1)}, u32[]{:S(2)}, u32[]{:S(2)}) collective-permute-start(f32[16,40,128]{2,1,0:T(8,128)S(1)} %get-tuple-element.16), channel_id=1, source_target_pairs={{0,1},{1,0},{2,3},{3,2},{4,5},{5,4},{6,7},{7,6},{8,9},{9,8},{10,11... | collective-permute-start | bytes 983048 | tf_op jit(solution)/shard_map/ppermute | solution.py:341
  43.3 1.3 %pert_products.1.a_ref = f32[16,40,128]{2,1,0:T(8,128)S(1)} custom-call(bf16[512,256]{1,0:T(8,128)(2,1)S(1)} %get-tuple-element.14.weights_ref, bf16[8,128]{1,0:T(8,128)(2,1)S(1)} %copy-done, bf16[8192,512]{1,0:T(8,128)(2,1)S(1)} %get-tuple-element.13.tensor_ref, f32[128,128]{1,0:T(8,128)S(1)} %get-tuple-element.15.gram_ref), custom_call_target="tpu_custom_call" | custom-call | tf_op jit(solution)/shard_map/pert_products/pallas_call | solution.py:277
  44.6 0.0 collective-permute-done.b_ref
  44.7 13.6 %all_to_all.27.in_ref = bf16[16,48,128]{2,1,0:T(8,128)(2,1)S(1)} all-to-all(bf16[16,48,128]{2,1,0:T(8,128)(2,1)S(1)} %core_sum.1), channel_id=1, replica_groups={{0,2,4,6,8,10,12,14,16,18,20,22,24,26,28,30},{1,3,5,7,9,11,13,15,17,19,..., dimensions={0} | all-to-all | bytes 393216 | tf_op jit(solution)/shard_map/all_to_all | solution.py:355
  58.3 11.1 %all_to_all.28.mine_ref = f32[16,40,128]{2,1,0:T(8,128)S(1)} all-to-all(f32[16,40,128]{2,1,0:T(8,128)S(1)} %gene_sum.1), channel_id=1, replica_groups={{0,2,4,6,8,10,12,14,16,18,20,22,24,26,28,30},{1,3,5,7,9,11,13,15,17,19,..., dimensions={0} | all-to-all | bytes 655360 | tf_op jit(solution)/shard_map/all_to_all | solution.py:357
  69.4 2.9 %collective-permute-start.1 = (f32[16,40,128]{2,1,0:T(8,128)S(1)}, f32[16,40,128]{2,1,0:T(8,128)S(1)}, u32[]{:S(2)}, u32[]{:S(2)}) collective-permute-start(f32[16,40,128]{2,1,0:T(8,128)S(1)} %all_to_all.28.mine_ref), channel_id=1, source_target_pairs={{0,1},{1,0},{2,3},{3,2},{4,5},{5,4},{6,7},{7,6},{8,9},{9,8},{10,11... | collective-permute-start | bytes 983048 | tf_op jit(solution)/shard_map/ppermute | solution.py:358
  72.3 3.8 %pert_inverse.1 = (f32[128,128]{1,0:T(8,128)S(1)}, f32[1,128]{1,0:T(1,128)S(1)}) custom-call(f32[16,40,128]{2,1,0:T(8,128)S(1)} %all_to_all.28.mine_ref, bf16[8,128]{1,0:T(8,128)(2,1)S(1)} %copy-done), custom_call_target="tpu_custom_call" | custom-call | tf_op jit(solution)/shard_map/pert_inverse/pallas_call | solution.py:277
  76.1 0.0 collective-permute-done.1.other_ref
  76.1 0.5 pert_solve.1
  76.6 8.9 %all_to_all.29.held_ref = f32[8,1,128]{2,1,0:T(1,128)S(1)} all-to-all(f32[8,1,128]{2,1,0:T(1,128)S(1)} %get-tuple-element.18), channel_id=1, replica_groups=mesh['pert'=8,'gene'=32] {'pert'}, dimensions={0} | all-to-all | bytes 8192 | tf_op jit(solution)/shard_map/all_to_all | solution.py:372
  85.5 0.8 scale.1
  (3 shorter events, 0.1 us)
Async XLA Ops:
  0.6 33.7 %copy-start = (bf16[8,128]{1,0:T(8,128)(2,1)S(1)}, bf16[8,128]{1,0:T(8,128)(2,1)}, u32[]{:S(2)}) copy-start(bf16[8,128]{1,0:T(8,128)(2,1)} %context_ref.5) | copy-start | bytes 6148
  40.1 4.6 %collective-permute-start = (f32[16,40,128]{2,1,0:T(8,128)S(1)}, f32[16,40,128]{2,1,0:T(8,128)S(1)}, u32[]{:S(2)}, u32[]{:S(2)}) collective-permute-start(f32[16,40,128]{2,1,0:T(8,128)S(1)} %get-tuple-element.16), channel_id=1, source_target_pairs={{0,1},{1,0},{2,3},{3,2},{4,5},{5,4},{6,7},{7,6},{8,9},{9,8},{10,11... | collective-permute-start | bytes 983048 | tf_op jit(solution)/shard_map/ppermute | solution.py:341
  69.4 6.7 %collective-permute-start.1 = (f32[16,40,128]{2,1,0:T(8,128)S(1)}, f32[16,40,128]{2,1,0:T(8,128)S(1)}, u32[]{:S(2)}, u32[]{:S(2)}) collective-permute-start(f32[16,40,128]{2,1,0:T(8,128)S(1)} %all_to_all.28.mine_ref), channel_id=1, source_target_pairs={{0,1},{1,0},{2,3},{3,2},{4,5},{5,4},{6,7},{7,6},{8,9},{9,8},{10,11... | collective-permute-start | bytes 983048 | tf_op jit(solution)/shard_map/ppermute | solution.py:358

commit v11 on v10

--- a/solution.py
+++ b/solution.py
@@ -84,10 +84,11 @@
     def newton(_, x):
         return x + dot_split(x, unit - dot(scaled, x, precision=HIGHEST))
 
+    x, r = advance(x, r)
+    norm = row_norm(r)
+    x, r = advance(x, r)
     x, r, bound, _ = lax.while_loop(
-        lambda s: jnp.logical_and(s[2] > 1e-7, s[3] < 40),
-        more,
-        (x, r, jnp.where(far_off, 1.0, off * off), 0),
+        lambda s: jnp.logical_and(s[2] > 1e-7, s[3] < 40), more, (x, r, norm * norm, 2)
     )
     x = lax.fori_loop(0, jnp.where(far_off, 4, jnp.where(off > 0.8, 1, 0)), newton, x)
     return x * scale_col * scale_row

time: 86.3 us -> 86.4 us (level)
  no operation moved by 1% of the time
where the time goes in v11:
time: 86.4 us; the launch traced here: 86.3 us
  blocking collectives  62.8 us (73%)
  Pallas kernels  16.6 us (19%)
  starting transfers between devices  6.15 us (7%)
    all_to_all x1, blocking collectives, shards(): partial = lax.all_to_all(partial, 'pert', 0, 0)  17.8 us
    pallas_call x9, Pallas kernels, call(): pl.pallas_call(body, in_specs=in_specs or [VMEM] * len(inputs), out_specs...  16.6 us
    all_to_all x1, blocking collectives, shards(): partial = lax.all_to_all(partial, 'gene', 0, 0, axis_index_groups=groups)  13.6 us
    all_to_all x1, blocking collectives, shards(): gathered = lax.all_to_all(gathered, 'pert', 0, 0)  11.4 us
    all_to_all x1, blocking collectives, shards(): mine = lax.all_to_all(summed, 'gene', 0, 0, axis_index_groups=groups)  11.1 us
    all_to_all x1, blocking collectives, shards(): squares = lax.all_to_all(squares, 'pert', 0, 0)  8.92 us
    ppermute x1, starting transfers between devices, shards(): other = lax.ppermute(other, 'gene', swap)  3.27 us
    ppermute x1, starting transfers between devices, shards(): other = lax.ppermute(mine, 'gene', swap)  2.88 us
  transfers between devices with their start and end apart: 2, of which 0 were waited for; matrix products, arithmetic and copies ran while one was open for 0% of the time, Pallas kernels for 6%

profile of v11, /device:TPU:1, one launch (start us, length us, event | category | flops | bytes accessed | tf_op | source)
XLA Modules:
  0.0 86.3 jit_solution(12152073353957384806)
XLA Ops:
  0.6 0.0 copy-start
  0.6 4.4 %gene_products.1 = (bf16[8,96,128]{2,1,0:T(8,128)(2,1)S(1)}, bf16[8192,512]{1,0:T(8,128)(2,1)S(1)}) custom-call(bf16[8192,512]{1,0:T(8,128)(2,1)} %bitcast.1, bf16[1024,128]{1,0:T(8,128)(2,1)} %factor_hbm.1, bf16[8,128]{1,0:T(8,128)(2,1)} %context_ref.5), custom_call_target="tpu_custom_call" | custom-call | tf_op jit(solution)/shard_map/gene_products/pallas_call | solution.py:278
  5.1 17.8 %all_to_all.25.in_ref = bf16[8,96,128]{2,1,0:T(8,128)(2,1)S(1)} all-to-all(bf16[8,96,128]{2,1,0:T(8,128)(2,1)S(1)} %get-tuple-element.12), channel_id=1, replica_groups=mesh['pert'=8,'gene'=32] {'pert'}, dimensions={0} | all-to-all | bytes 393216 | tf_op jit(solution)/shard_map/all_to_all | solution.py:314
  22.9 11.4 %all_to_all.26.held_ref = bf16[8,96,128]{2,1,0:T(8,128)(2,1)S(1)} all-to-all(bf16[8,96,128]{2,1,0:T(8,128)(2,1)S(1)} %pert_sum.1), channel_id=1, replica_groups=mesh['pert'=8,'gene'=32] {'pert'}, dimensions={0} | all-to-all | bytes 393216 | tf_op jit(solution)/shard_map/all_to_all | solution.py:321
  34.3 0.0 copy-done
  34.3 5.7 %gene_solve.1 = (f32[16,40,128]{2,1,0:T(8,128)S(1)}, f32[512,128]{1,0:T(8,128)S(1)}, bf16[512,256]{1,0:T(8,128)(2,1)S(1)}, f32[128,128]{1,0:T(8,128)S(1)}) custom-call(bf16[8,96,128]{2,1,0:T(8,128)(2,1)S(1)} %all_to_all.26.held_ref, bf16[8,128]{1,0:T(8,128)(2,1)S(1)} %copy-done, bf16[8192,512]{1,0:T(8,128)(2,1)S(1)} %get-tuple-element.13.tensor_ref), custom_call_target="tpu_custom_call" | custom-call | tf_op jit(solution)/shard_map/gene_solve/pallas_call | solution.py:278
  40.1 3.3 %collective-permute-start = (f32[16,40,128]{2,1,0:T(8,128)S(1)}, f32[16,40,128]{2,1,0:T(8,128)S(1)}, u32[]{:S(2)}, u32[]{:S(2)}) collective-permute-start(f32[16,40,128]{2,1,0:T(8,128)S(1)} %get-tuple-element.16), channel_id=1, source_target_pairs={{0,1},{1,0},{2,3},{3,2},{4,5},{5,4},{6,7},{7,6},{8,9},{9,8},{10,11... | collective-permute-start | bytes 983048 | tf_op jit(solution)/shard_map/ppermute | solution.py:342
  43.3 1.3 %pert_products.1.a_ref = f32[16,40,128]{2,1,0:T(8,128)S(1)} custom-call(bf16[512,256]{1,0:T(8,128)(2,1)S(1)} %get-tuple-element.14.weights_ref, bf16[8,128]{1,0:T(8,128)(2,1)S(1)} %copy-done, bf16[8192,512]{1,0:T(8,128)(2,1)S(1)} %get-tuple-element.13.tensor_ref, f32[128,128]{1,0:T(8,128)S(1)} %get-tuple-element.15.gram_ref), custom_call_target="tpu_custom_call" | custom-call | tf_op jit(solution)/shard_map/pert_products/pallas_call | solution.py:278
  44.6 0.0 collective-permute-done.b_ref
  44.7 13.6 %all_to_all.27.in_ref = bf16[16,48,128]{2,1,0:T(8,128)(2,1)S(1)} all-to-all(bf16[16,48,128]{2,1,0:T(8,128)(2,1)S(1)} %core_sum.1), channel_id=1, replica_groups={{0,2,4,6,8,10,12,14,16,18,20,22,24,26,28,30},{1,3,5,7,9,11,13,15,17,19,..., dimensions={0} | all-to-all | bytes 393216 | tf_op jit(solution)/shard_map/all_to_all | solution.py:356
  58.3 11.1 %all_to_all.28.mine_ref = f32[16,40,128]{2,1,0:T(8,128)S(1)} all-to-all(f32[16,40,128]{2,1,0:T(8,128)S(1)} %gene_sum.1), channel_id=1, replica_groups={{0,2,4,6,8,10,12,14,16,18,20,22,24,26,28,30},{1,3,5,7,9,11,13,15,17,19,..., dimensions={0} | all-to-all | bytes 655360 | tf_op jit(solution)/shard_map/all_to_all | solution.py:358
  69.4 2.9 %collective-permute-start.1 = (f32[16,40,128]{2,1,0:T(8,128)S(1)}, f32[16,40,128]{2,1,0:T(8,128)S(1)}, u32[]{:S(2)}, u32[]{:S(2)}) collective-permute-start(f32[16,40,128]{2,1,0:T(8,128)S(1)} %all_to_all.28.mine_ref), channel_id=1, source_target_pairs={{0,1},{1,0},{2,3},{3,2},{4,5},{5,4},{6,7},{7,6},{8,9},{9,8},{10,11... | collective-permute-start | bytes 983048 | tf_op jit(solution)/shard_map/ppermute | solution.py:359
  72.3 3.8 %pert_inverse.1 = (f32[128,128]{1,0:T(8,128)S(1)}, f32[1,128]{1,0:T(1,128)S(1)}) custom-call(f32[16,40,128]{2,1,0:T(8,128)S(1)} %all_to_all.28.mine_ref, bf16[8,128]{1,0:T(8,128)(2,1)S(1)} %copy-done), custom_call_target="tpu_custom_call" | custom-call | tf_op jit(solution)/shard_map/pert_inverse/pallas_call | solution.py:278
  76.1 0.0 collective-permute-done.1.other_ref
  76.1 0.5 pert_solve.1
  76.6 8.9 %all_to_all.29.held_ref = f32[8,1,128]{2,1,0:T(1,128)S(1)} all-to-all(f32[8,1,128]{2,1,0:T(1,128)S(1)} %get-tuple-element.18), channel_id=1, replica_groups=mesh['pert'=8,'gene'=32] {'pert'}, dimensions={0} | all-to-all | bytes 8192 | tf_op jit(solution)/shard_map/all_to_all | solution.py:373
  85.5 0.8 scale.1
  (3 shorter events, 0.1 us)
Async XLA Ops:
  0.6 33.7 %copy-start = (bf16[8,128]{1,0:T(8,128)(2,1)S(1)}, bf16[8,128]{1,0:T(8,128)(2,1)}, u32[]{:S(2)}) copy-start(bf16[8,128]{1,0:T(8,128)(2,1)} %context_ref.5) | copy-start | bytes 6148
  40.1 4.6 %collective-permute-start = (f32[16,40,128]{2,1,0:T(8,128)S(1)}, f32[16,40,128]{2,1,0:T(8,128)S(1)}, u32[]{:S(2)}, u32[]{:S(2)}) collective-permute-start(f32[16,40,128]{2,1,0:T(8,128)S(1)} %get-tuple-element.16), channel_id=1, source_target_pairs={{0,1},{1,0},{2,3},{3,2},{4,5},{5,4},{6,7},{7,6},{8,9},{9,8},{10,11... | collective-permute-start | bytes 983048 | tf_op jit(solution)/shard_map/ppermute | solution.py:342
  69.4 6.7 %collective-permute-start.1 = (f32[16,40,128]{2,1,0:T(8,128)S(1)}, f32[16,40,128]{2,1,0:T(8,128)S(1)}, u32[]{:S(2)}, u32[]{:S(2)}) collective-permute-start(f32[16,40,128]{2,1,0:T(8,128)S(1)} %all_to_all.28.mine_ref), channel_id=1, source_target_pairs={{0,1},{1,0},{2,3},{3,2},{4,5},{5,4},{6,7},{7,6},{8,9},{9,8},{10,11... | collective-permute-start | bytes 983048 | tf_op jit(solution)/shard_map/ppermute | solution.py:359

commit v12 on v11

--- a/solution.py
+++ b/solution.py
@@ -327,7 +327,7 @@
     square = pltpu.VMEM((rank, rank), f32)
     kept = near(kept)
     other, solved_c, weights, gram_s = call(
-        functools.partial(gene_solve, 4),
+        functools.partial(gene_solve, 2),
         "gene_solve",
         (near(gathered), context_factor, kept),
         (
@@ -341,7 +341,7 @@
     groups = [[2 * i + core for i in range(chips)] for core in range(2)]
     other = lax.ppermute(other, "gene", swap)
     mine = call(
-        functools.partial(pert_products, 4),
+        functools.partial(pert_products, 2),
         "pert_products",
         (near(weights), context_factor, kept, near(gram_s)),
         message,

time: 86.4 us -> 86.4 us (level)
  no operation moved by 1% of the time
where the time goes in v12:
time: 86.4 us; the launch traced here: 86.1 us
  blocking collectives  63 us (73%)
  Pallas kernels  16.4 us (19%)
  starting transfers between devices  5.97 us (7%)
    all_to_all x1, blocking collectives, shards(): partial = lax.all_to_all(partial, 'pert', 0, 0)  17.8 us
    pallas_call x9, Pallas kernels, call(): pl.pallas_call(body, in_specs=in_specs or [VMEM] * len(inputs), out_specs...  16.4 us
    all_to_all x1, blocking collectives, shards(): partial = lax.all_to_all(partial, 'gene', 0, 0, axis_index_groups=groups)  13.6 us
    all_to_all x1, blocking collectives, shards(): gathered = lax.all_to_all(gathered, 'pert', 0, 0)  11.4 us
    all_to_all x1, blocking collectives, shards(): mine = lax.all_to_all(summed, 'gene', 0, 0, axis_index_groups=groups)  11.3 us
    all_to_all x1, blocking collectives, shards(): squares = lax.all_to_all(squares, 'pert', 0, 0)  8.92 us
    ppermute x1, starting transfers between devices, shards(): other = lax.ppermute(other, 'gene', swap)  3.26 us
    ppermute x1, starting transfers between devices, shards(): other = lax.ppermute(mine, 'gene', swap)  2.71 us
  transfers between devices with their start and end apart: 2, of which 0 were waited for; matrix products, arithmetic and copies ran while one was open for 0% of the time, Pallas kernels for 6%

profile of v12, /device:TPU:1, one launch (start us, length us, event | category | flops | bytes accessed | tf_op | source)
XLA Modules:
  0.0 86.1 jit_solution(2119769813943158121)
XLA Ops:
  0.6 0.0 copy-start
  0.6 4.4 %gene_products.1 = (bf16[8,96,128]{2,1,0:T(8,128)(2,1)S(1)}, bf16[8192,512]{1,0:T(8,128)(2,1)S(1)}) custom-call(bf16[8192,512]{1,0:T(8,128)(2,1)} %bitcast.1, bf16[1024,128]{1,0:T(8,128)(2,1)} %factor_hbm.1, bf16[8,128]{1,0:T(8,128)(2,1)} %context_ref.5), custom_call_target="tpu_custom_call" | custom-call | tf_op jit(solution)/shard_map/gene_products/pallas_call | solution.py:278
  5.1 17.8 %all_to_all.25.in_ref = bf16[8,96,128]{2,1,0:T(8,128)(2,1)S(1)} all-to-all(bf16[8,96,128]{2,1,0:T(8,128)(2,1)S(1)} %get-tuple-element.12), channel_id=1, replica_groups=mesh['pert'=8,'gene'=32] {'pert'}, dimensions={0} | all-to-all | bytes 393216 | tf_op jit(solution)/shard_map/all_to_all | solution.py:314
  22.9 11.4 %all_to_all.26.held_ref = bf16[8,96,128]{2,1,0:T(8,128)(2,1)S(1)} all-to-all(bf16[8,96,128]{2,1,0:T(8,128)(2,1)S(1)} %pert_sum.1), channel_id=1, replica_groups=mesh['pert'=8,'gene'=32] {'pert'}, dimensions={0} | all-to-all | bytes 393216 | tf_op jit(solution)/shard_map/all_to_all | solution.py:321
  34.3 0.0 copy-done
  34.3 5.6 %gene_solve.1 = (f32[16,40,128]{2,1,0:T(8,128)S(1)}, f32[512,128]{1,0:T(8,128)S(1)}, bf16[512,256]{1,0:T(8,128)(2,1)S(1)}, f32[128,128]{1,0:T(8,128)S(1)}) custom-call(bf16[8,96,128]{2,1,0:T(8,128)(2,1)S(1)} %all_to_all.26.held_ref, bf16[8,128]{1,0:T(8,128)(2,1)S(1)} %copy-done, bf16[8192,512]{1,0:T(8,128)(2,1)S(1)} %get-tuple-element.13.tensor_ref), custom_call_target="tpu_custom_call" | custom-call | tf_op jit(solution)/shard_map/gene_solve/pallas_call | solution.py:278
  39.9 3.3 %collective-permute-start = (f32[16,40,128]{2,1,0:T(8,128)S(1)}, f32[16,40,128]{2,1,0:T(8,128)S(1)}, u32[]{:S(2)}, u32[]{:S(2)}) collective-permute-start(f32[16,40,128]{2,1,0:T(8,128)S(1)} %get-tuple-element.16), channel_id=1, source_target_pairs={{0,1},{1,0},{2,3},{3,2},{4,5},{5,4},{6,7},{7,6},{8,9},{9,8},{10,11... | collective-permute-start | bytes 983048 | tf_op jit(solution)/shard_map/ppermute | solution.py:342
  43.2 1.4 %pert_products.1.a_ref = f32[16,40,128]{2,1,0:T(8,128)S(1)} custom-call(bf16[512,256]{1,0:T(8,128)(2,1)S(1)} %get-tuple-element.14.weights_ref, bf16[8,128]{1,0:T(8,128)(2,1)S(1)} %copy-done, bf16[8192,512]{1,0:T(8,128)(2,1)S(1)} %get-tuple-element.13.tensor_ref, f32[128,128]{1,0:T(8,128)S(1)} %get-tuple-element.15.gram_ref), custom_call_target="tpu_custom_call" | custom-call | tf_op jit(solution)/shard_map/pert_products/pallas_call | solution.py:278
  44.6 0.0 collective-permute-done.b_ref
  44.7 13.6 %all_to_all.27.in_ref = bf16[16,48,128]{2,1,0:T(8,128)(2,1)S(1)} all-to-all(bf16[16,48,128]{2,1,0:T(8,128)(2,1)S(1)} %core_sum.1), channel_id=1, replica_groups={{0,2,4,6,8,10,12,14,16,18,20,22,24,26,28,30},{1,3,5,7,9,11,13,15,17,19,..., dimensions={0} | all-to-all | bytes 393216 | tf_op jit(solution)/shard_map/all_to_all | solution.py:356
  58.3 11.3 %all_to_all.28.mine_ref = f32[16,40,128]{2,1,0:T(8,128)S(1)} all-to-all(f32[16,40,128]{2,1,0:T(8,128)S(1)} %gene_sum.1), channel_id=1, replica_groups={{0,2,4,6,8,10,12,14,16,18,20,22,24,26,28,30},{1,3,5,7,9,11,13,15,17,19,..., dimensions={0} | all-to-all | bytes 655360 | tf_op jit(solution)/shard_map/all_to_all | solution.py:358
  69.6 2.7 %collective-permute-start.1 = (f32[16,40,128]{2,1,0:T(8,128)S(1)}, f32[16,40,128]{2,1,0:T(8,128)S(1)}, u32[]{:S(2)}, u32[]{:S(2)}) collective-permute-start(f32[16,40,128]{2,1,0:T(8,128)S(1)} %all_to_all.28.mine_ref), channel_id=1, source_target_pairs={{0,1},{1,0},{2,3},{3,2},{4,5},{5,4},{6,7},{7,6},{8,9},{9,8},{10,11... | collective-permute-start | bytes 983048 | tf_op jit(solution)/shard_map/ppermute | solution.py:359
  72.3 3.6 %pert_inverse.1 = (f32[128,128]{1,0:T(8,128)S(1)}, f32[1,128]{1,0:T(1,128)S(1)}) custom-call(f32[16,40,128]{2,1,0:T(8,128)S(1)} %all_to_all.28.mine_ref, bf16[8,128]{1,0:T(8,128)(2,1)S(1)} %copy-done), custom_call_target="tpu_custom_call" | custom-call | tf_op jit(solution)/shard_map/pert_inverse/pallas_call | solution.py:278
  76.0 0.0 collective-permute-done.1.other_ref
  76.0 0.5 pert_solve.1
  76.4 8.9 %all_to_all.29.held_ref = f32[8,1,128]{2,1,0:T(1,128)S(1)} all-to-all(f32[8,1,128]{2,1,0:T(1,128)S(1)} %get-tuple-element.18), channel_id=1, replica_groups=mesh['pert'=8,'gene'=32] {'pert'}, dimensions={0} | all-to-all | bytes 8192 | tf_op jit(solution)/shard_map/all_to_all | solution.py:373
  85.3 0.8 scale.1
  (3 shorter events, 0.1 us)
Async XLA Ops:
  0.6 33.7 %copy-start = (bf16[8,128]{1,0:T(8,128)(2,1)S(1)}, bf16[8,128]{1,0:T(8,128)(2,1)}, u32[]{:S(2)}) copy-start(bf16[8,128]{1,0:T(8,128)(2,1)} %context_ref.5) | copy-start | bytes 6148
  39.9 4.7 %collective-permute-start = (f32[16,40,128]{2,1,0:T(8,128)S(1)}, f32[16,40,128]{2,1,0:T(8,128)S(1)}, u32[]{:S(2)}, u32[]{:S(2)}) collective-permute-start(f32[16,40,128]{2,1,0:T(8,128)S(1)} %get-tuple-element.16), channel_id=1, source_target_pairs={{0,1},{1,0},{2,3},{3,2},{4,5},{5,4},{6,7},{7,6},{8,9},{9,8},{10,11... | collective-permute-start | bytes 983048 | tf_op jit(solution)/shard_map/ppermute | solution.py:342
  69.6 6.4 %collective-permute-start.1 = (f32[16,40,128]{2,1,0:T(8,128)S(1)}, f32[16,40,128]{2,1,0:T(8,128)S(1)}, u32[]{:S(2)}, u32[]{:S(2)}) collective-permute-start(f32[16,40,128]{2,1,0:T(8,128)S(1)} %all_to_all.28.mine_ref), channel_id=1, source_target_pairs={{0,1},{1,0},{2,3},{3,2},{4,5},{5,4},{6,7},{7,6},{8,9},{9,8},{10,11... | collective-permute-start | bytes 983048 | tf_op jit(solution)/shard_map/ppermute | solution.py:359
